TPU v7x, 32 devices: a whole 2x2x4 slice. The times are simulated.
32 devices in a mesh: rep: 4 (over y, core), fsdp: 4 (over z), tp: 2 (over x).
Axes of the slice: x: 2, y: 2, z: 4, core: 2. Of those that a mesh axis runs over, the one named last changes fastest.
Arguments:
- tokens: bfloat16 [5632, 1024], P(('rep', 'fsdp')), may hold values from -6 to 6
- segment_ids: int32 [5632], P(('rep', 'fsdp')), may hold values from 0 to 11, as said below
- valid_keys: int32 [5632], P(('rep', 'fsdp')), may hold values 0 or 1
- norm_gain: bfloat16 [1, 2, 1024], P(None, None, 'fsdp'), may hold values from 0.25 to 1.75
- norm_bias: bfloat16 [1, 2, 1024], P(None, None, 'fsdp'), may hold values from -3 to 3
- qkv_weight: bfloat16 [1, 1024, 3, 1024], P(None, 'fsdp', None, 'tp')
- qv_bias: bfloat16 [1, 2, 16, 64], P(None, None, 'tp', 'fsdp'), may hold values from -3 to 3
- out_weight: bfloat16 [1, 1024, 1024], P(None, 'tp', 'fsdp'), may hold values from -1 to 1
- up_weight: bfloat16 [1, 1024, 4096], P(None, 'fsdp', 'tp'), may hold values from -0.1875 to 0.1875
- up_bias: bfloat16 [1, 64, 64], P(None, 'tp', 'fsdp'), may hold values from -3 to 3
- down_weight: bfloat16 [1, 4096, 1024], P(None, 'tp', 'fsdp'), may hold values from -0.09375 to 0.09375
- out_bias: bfloat16 [1, 2, 1024], P(None, None, 'fsdp'), may hold values from -2 to 2
- layer_scale: bfloat16 [1, 2, 1024], P(None, None, 'fsdp'), may hold values from 0.29882812 to 1
- cotangent: bfloat16 [5632, 1024], P(('rep', 'fsdp')), may hold values from -6 to 6
Outputs:
- block_out: bfloat16 [5632, 1024], P(('rep', 'fsdp'))
- tokens_grad: float32 [5632, 1024], P(('rep', 'fsdp'))
- norm_gain_grad: float32 [1, 2, 1024], P(None, None, 'fsdp')
- norm_bias_grad: float32 [1, 2, 1024], P(None, None, 'fsdp')
- qkv_weight_grad: float32 [1, 1024, 3, 1024], P(None, 'fsdp', None, 'tp')
- qv_bias_grad: float32 [1, 2, 16, 64], P(None, None, 'tp', 'fsdp')
- out_weight_grad: float32 [1, 1024, 1024], P(None, 'tp', 'fsdp')
- up_weight_grad: float32 [1, 1024, 4096], P(None, 'fsdp', 'tp')
- up_bias_grad: float32 [1, 64, 64], P(None, 'tp', 'fsdp')
- down_weight_grad: float32 [1, 4096, 1024], P(None, 'tp', 'fsdp')
- out_bias_grad: float32 [1, 2, 1024], P(None, None, 'fsdp')
- layer_scale_grad: float32 [1, 2, 1024], P(None, None, 'fsdp')
Inputs may be any that keep to these rules, and one draw needn't show every extreme that they name: `segment_ids`: non-decreasing along the tokens; no segment crosses a block of 1408 tokens (one index of rep); each such block holds (1406) // 1370 images of exactly 1370 consecutive tokens, with a piece of 1 or more tokens before them and one after them, each piece a segment of its own.
All inputs are finite; a program needn't handle non-finite values. No bound on the sum of `valid_keys` on one device may be relied on, other than what follows from the above.
Results may differ from a plain program's by a relative error of at most 0.014.
Values may be sent and summed in bfloat16 or wider, within the bound.
No kernel may reach another device: no remote copies, remote signals or barrier semaphores. Data moves between devices by JAX's collectives and lax.ppermute only.
A program may use at most 128 MiB of HBM per device.

v0:
```python
import jax
import jax.numpy as jnp
from jax import lax
from jax.sharding import PartitionSpec as P

HD = 64
L = 1


EPSILON = 1e-06
ROOT_HALF = 0.7071067811865476
INV_ROOT_TWO_PI = 0.3989422804014327
NEG_LARGE = -1e30


def norm_forward(values, gain, shift):
    centred = values - jnp.mean(values, axis=-1, keepdims=True)
    inverse = lax.rsqrt(jnp.mean(centred * centred, axis=-1, keepdims=True) + EPSILON)
    normal_part = centred * inverse
    return (normal_part * gain + shift, normal_part, inverse)


def norm_backward(upstream, normal_part, inverse, gain):
    scaled = upstream * gain
    inner = (
        scaled
        - jnp.mean(scaled, axis=-1, keepdims=True)
        - normal_part * jnp.mean(scaled * normal_part, axis=-1, keepdims=True)
    )
    return (inverse * inner, jnp.sum(upstream * normal_part, axis=0), jnp.sum(upstream, axis=0))


def gelu_value(pre):
    return 0.5 * pre * (1.0 + lax.erf(pre * ROOT_HALF))


def gelu_slope(pre):
    return 0.5 * (1.0 + lax.erf(pre * ROOT_HALF)) + pre * INV_ROOT_TWO_PI * jnp.exp(
        -0.5 * pre * pre
    )


def sum_heads(partial_value):
    return lax.psum(partial_value, "tp")


def gather_forward(w_qkv, w_out, w_up, w_down, gains, shifts, biases, scales, qv_part, up_part):
    return (
        lax.all_gather(w_qkv, "fsdp", axis=0, tiled=True),
        lax.all_gather(w_out, "fsdp", axis=1, tiled=True),
        lax.all_gather(w_up, "fsdp", axis=0, tiled=True),
        lax.all_gather(w_down, "fsdp", axis=1, tiled=True),
        lax.all_gather(gains, "fsdp", axis=1, tiled=True),
        lax.all_gather(shifts, "fsdp", axis=1, tiled=True),
        lax.all_gather(biases, "fsdp", axis=1, tiled=True),
        lax.all_gather(scales, "fsdp", axis=1, tiled=True),
        lax.all_gather(qv_part, "fsdp", axis=2, tiled=True),
        lax.all_gather(up_part, "fsdp", axis=1, tiled=True),
    )


def gather_backward(w_qkv, w_out, w_up, w_down, gains, shifts, biases, scales, qv_part, up_part):
    return (
        lax.all_gather(w_qkv, "fsdp", axis=0, tiled=True),
        lax.all_gather(w_out, "fsdp", axis=1, tiled=True),
        lax.all_gather(w_up, "fsdp", axis=0, tiled=True),
        lax.all_gather(w_down, "fsdp", axis=1, tiled=True),
        lax.all_gather(gains, "fsdp", axis=1, tiled=True),
        lax.all_gather(shifts, "fsdp", axis=1, tiled=True),
        lax.all_gather(biases, "fsdp", axis=1, tiled=True),
        lax.all_gather(scales, "fsdp", axis=1, tiled=True),
        lax.all_gather(qv_part, "fsdp", axis=2, tiled=True),
        lax.all_gather(up_part, "fsdp", axis=1, tiled=True),
    )


def allowed_keys(query_seg, key_code, row_count, own_start):
    key_int = key_code.astype(jnp.int32)
    key_seg = key_int // 2
    key_live = key_int % 2
    positions = jnp.arange(key_int.shape[0], dtype=jnp.int32)
    diagonal = positions[None, :] == jnp.arange(row_count, dtype=jnp.int32)[:, None] + own_start
    return (query_seg[:, None] == key_seg[None, :]) & ((key_live[None, :] == 1) | diagonal)


def split_heads(flat, head_count):
    return flat.reshape(flat.shape[0], head_count, -1).transpose(1, 0, 2)


def join_heads(stacked):
    return stacked.transpose(1, 0, 2).reshape(stacked.shape[1], -1)


def attend_forward(query_heads, key_heads, value_heads, allowed, score_scale):

    def one_head(operands):
        q_one, k_one, v_one = operands
        scores = (
            jnp.einsum("qd,kd->qk", q_one, k_one, preferred_element_type=jnp.float32) * score_scale
        )
        scores = jnp.where(allowed, scores, NEG_LARGE)
        top = jnp.max(scores, axis=1, keepdims=True)
        expo = jnp.where(allowed, jnp.exp(scores - top), 0.0)
        total = jnp.sum(expo, axis=1, keepdims=True)
        weights = (expo / total).astype(jnp.bfloat16)
        mixed = jnp.einsum("qk,kd->qd", weights, v_one, preferred_element_type=jnp.float32)
        return (mixed.astype(jnp.bfloat16), (top + jnp.log(total))[:, 0])

    return lax.map(one_head, (query_heads, key_heads, value_heads))


def attend_backward(
    query_heads, key_heads, value_heads, mixed_heads, grad_heads, log_total, allowed, score_scale
):

    def one_head(operands):
        q_one, k_one, v_one, o_one, g_one, t_one = operands
        scores = (
            jnp.einsum("qd,kd->qk", q_one, k_one, preferred_element_type=jnp.float32) * score_scale
        )
        probs = jnp.where(allowed, jnp.exp(scores - t_one[:, None]), 0.0)
        d_value = jnp.einsum(
            "qk,qd->kd", probs.astype(jnp.bfloat16), g_one, preferred_element_type=jnp.float32
        )
        d_probs = jnp.einsum("qd,kd->qk", g_one, v_one, preferred_element_type=jnp.float32)
        inner = jnp.sum(
            g_one.astype(jnp.float32) * o_one.astype(jnp.float32), axis=1, keepdims=True
        )
        d_scores = (probs * (d_probs - inner)).astype(jnp.bfloat16)
        d_query = (
            jnp.einsum("qk,kd->qd", d_scores, k_one, preferred_element_type=jnp.float32)
            * score_scale
        )
        d_key = (
            jnp.einsum("qk,qd->kd", d_scores, q_one, preferred_element_type=jnp.float32)
            * score_scale
        )
        return (d_query, d_key, d_value)

    return lax.map(
        one_head, (query_heads, key_heads, value_heads, mixed_heads, grad_heads, log_total)
    )


def layer_params(
    layer_index,
    qkv_weight,
    out_weight,
    up_weight,
    down_weight,
    norm_gain,
    norm_bias,
    out_bias,
    layer_scale,
    qv_bias,
    up_bias,
    again,
):
    if again:
        return gather_backward(
            qkv_weight[layer_index],
            out_weight[layer_index],
            up_weight[layer_index],
            down_weight[layer_index],
            norm_gain[layer_index],
            norm_bias[layer_index],
            out_bias[layer_index],
            layer_scale[layer_index],
            qv_bias[layer_index],
            up_bias[layer_index],
        )
    return gather_forward(
        qkv_weight[layer_index],
        out_weight[layer_index],
        up_weight[layer_index],
        down_weight[layer_index],
        norm_gain[layer_index],
        norm_bias[layer_index],
        out_bias[layer_index],
        layer_scale[layer_index],
        qv_bias[layer_index],
        up_bias[layer_index],
    )


def local(
    tokens,
    segment_ids,
    valid_keys,
    norm_gain,
    norm_bias,
    qkv_weight,
    qv_bias,
    out_weight,
    up_weight,
    up_bias,
    down_weight,
    out_bias,
    layer_scale,
    cotangent,
):
    row_count = tokens.shape[0]
    width = tokens.shape[1]
    local_width = qkv_weight.shape[3]
    local_heads = qv_bias.shape[2]
    score_scale = HD ** (-0.5)
    key_code = (segment_ids * 2 + valid_keys).astype(jnp.float32).astype(jnp.bfloat16)
    weight_args = (
        qkv_weight,
        out_weight,
        up_weight,
        down_weight,
        norm_gain,
        norm_bias,
        out_bias,
        layer_scale,
        qv_bias,
        up_bias,
    )
    resid = tokens.astype(jnp.float32)
    kept = []
    layer_index = 0
    gathered = layer_params(layer_index, *weight_args, False)
    kept.append(gathered)
    w_qkv, w_out, w_up, w_down, gain_half, shift_half, bias_half, scale_half, qv_full, up_full = (
        gathered
    )
    gains = gain_half.astype(jnp.float32)
    shifts = shift_half.astype(jnp.float32)
    biases = bias_half.astype(jnp.float32)
    scales = scale_half.astype(jnp.float32)
    query_bias = qv_full.astype(jnp.float32).reshape(2, local_width)
    normed, part_one, inv_one = norm_forward(resid, gains[0], shifts[0])
    first_in = normed.astype(jnp.bfloat16)
    project = jnp.dot(
        first_in, w_qkv.reshape(width, 3 * local_width), preferred_element_type=jnp.float32
    ).reshape(row_count, 3, local_width)
    query = (project[:, 0] + query_bias[0]).astype(jnp.bfloat16)
    keys = project[:, 1].astype(jnp.bfloat16)
    values = (project[:, 2] + query_bias[1]).astype(jnp.bfloat16)
    pairs = jnp.stack([keys, values], axis=1)
    all_pairs = lax.all_gather(pairs, "fsdp", axis=0, tiled=True)
    all_codes = lax.all_gather(key_code, "fsdp", axis=0, tiled=True)
    own_start = lax.axis_index("fsdp") * row_count
    allowed = allowed_keys(segment_ids, all_codes, row_count, own_start)
    query_heads = split_heads(query, local_heads)
    key_heads = split_heads(all_pairs[:, 0], local_heads)
    value_heads = split_heads(all_pairs[:, 1], local_heads)
    mixed_heads, log_total = attend_forward(
        query_heads, key_heads, value_heads, allowed, score_scale
    )
    mixed_flat = join_heads(mixed_heads)
    branch_one = (
        sum_heads(jnp.dot(mixed_flat, w_out, preferred_element_type=jnp.float32)) + biases[0]
    )
    resid_one = resid + scales[0] * branch_one
    normed_two, part_two, inv_two = norm_forward(resid_one, gains[1], shifts[1])
    second_in = normed_two.astype(jnp.bfloat16)
    hidden_pre = jnp.dot(second_in, w_up, preferred_element_type=jnp.float32) + up_full.astype(
        jnp.float32
    ).reshape(-1)
    hidden = gelu_value(hidden_pre).astype(jnp.bfloat16)
    branch_two = sum_heads(jnp.dot(hidden, w_down, preferred_element_type=jnp.float32)) + biases[1]
    saved = [
        (
            part_one,
            inv_one,
            first_in,
            query_heads,
            key_heads,
            value_heads,
            allowed,
            mixed_heads,
            log_total,
            mixed_flat,
            branch_one,
            part_two,
            inv_two,
            second_in,
            hidden_pre,
            hidden,
            branch_two,
        )
    ]
    resid = resid_one + scales[1] * branch_two
    block_out = resid.astype(jnp.bfloat16)
    shard_grads = [None] * L
    upstream = cotangent.astype(jnp.float32)
    for layer_index in reversed(range(L)):
        gathered = layer_params(layer_index, *weight_args, True)
        (
            w_qkv,
            w_out,
            w_up,
            w_down,
            gain_half,
            shift_half,
            bias_half,
            scale_half,
            qv_full,
            up_full,
        ) = gathered
        gains = gain_half.astype(jnp.float32)
        scales = scale_half.astype(jnp.float32)
        (
            part_one,
            inv_one,
            first_in,
            query_heads,
            key_heads,
            value_heads,
            allowed,
            mixed_heads,
            log_total,
            mixed_flat,
            branch_one,
            part_two,
            inv_two,
            second_in,
            hidden_pre,
            hidden,
            branch_two,
        ) = saved[layer_index]
        scale_two = jnp.sum(upstream * branch_two, axis=0)
        bias_two = jnp.sum(upstream * scales[1], axis=0)
        branch_grad = (upstream * scales[1]).astype(jnp.bfloat16)
        d_down = jnp.einsum("rf,rd->fd", hidden, branch_grad, preferred_element_type=jnp.float32)
        d_hidden = jnp.einsum(
            "rd,fd->rf", branch_grad, w_down, preferred_element_type=jnp.float32
        ) * gelu_slope(hidden_pre)
        d_up_bias = jnp.sum(d_hidden, axis=0)
        d_hidden_half = d_hidden.astype(jnp.bfloat16)
        d_up = jnp.einsum("rd,rf->df", second_in, d_hidden_half, preferred_element_type=jnp.float32)
        d_second = sum_heads(
            jnp.einsum("rf,df->rd", d_hidden_half, w_up, preferred_element_type=jnp.float32)
        )
        d_norm_two, gain_two, shift_two = norm_backward(d_second, part_two, inv_two, gains[1])
        upstream_one = upstream + d_norm_two
        scale_one = jnp.sum(upstream_one * branch_one, axis=0)
        bias_one = jnp.sum(upstream_one * scales[0], axis=0)
        branch_grad_one = (upstream_one * scales[0]).astype(jnp.bfloat16)
        d_out = jnp.einsum(
            "re,rd->ed", mixed_flat, branch_grad_one, preferred_element_type=jnp.float32
        )
        d_mixed = jnp.einsum(
            "rd,ed->re", branch_grad_one, w_out, preferred_element_type=jnp.float32
        ).astype(jnp.bfloat16)
        d_query_heads, d_key_heads, d_value_heads = attend_backward(
            query_heads,
            key_heads,
            value_heads,
            mixed_heads,
            split_heads(d_mixed, local_heads),
            log_total,
            allowed,
            score_scale,
        )
        d_pairs = jnp.stack([join_heads(d_key_heads), join_heads(d_value_heads)], axis=1)
        d_local = lax.psum_scatter(d_pairs, "fsdp", scatter_dimension=0, tiled=True)
        d_query = join_heads(d_query_heads)
        d_qv = jnp.stack([jnp.sum(d_query, axis=0), jnp.sum(d_local[:, 1], axis=0)]).reshape(
            2, local_heads, HD
        )
        d_project = (
            jnp.stack([d_query, d_local[:, 0], d_local[:, 1]], axis=1)
            .astype(jnp.bfloat16)
            .reshape(row_count, 3 * local_width)
        )
        d_qkv = jnp.einsum(
            "rd,rc->dc", first_in, d_project, preferred_element_type=jnp.float32
        ).reshape(width, 3, local_width)
        d_first = sum_heads(
            jnp.einsum(
                "rc,dc->rd",
                d_project,
                w_qkv.reshape(width, 3 * local_width),
                preferred_element_type=jnp.float32,
            )
        )
        d_norm_one, gain_one, shift_one = norm_backward(d_first, part_one, inv_one, gains[0])
        upstream = upstream_one + d_norm_one
        d_gain = jnp.stack([gain_one, gain_two])
        d_shift = jnp.stack([shift_one, shift_two])
        d_bias = jnp.stack([bias_one, bias_two])
        d_scale = jnp.stack([scale_one, scale_two])
        d_up_groups = d_up_bias.reshape(-1, HD)
        pieces = (
            lax.psum_scatter(d_qkv, "fsdp", scatter_dimension=0, tiled=True),
            lax.psum_scatter(d_out, "fsdp", scatter_dimension=1, tiled=True),
            lax.psum_scatter(d_up, "fsdp", scatter_dimension=0, tiled=True),
            lax.psum_scatter(d_down, "fsdp", scatter_dimension=1, tiled=True),
            lax.psum_scatter(d_gain, "fsdp", scatter_dimension=1, tiled=True),
            lax.psum_scatter(d_shift, "fsdp", scatter_dimension=1, tiled=True),
            lax.psum_scatter(d_bias, "fsdp", scatter_dimension=1, tiled=True),
            lax.psum_scatter(d_scale, "fsdp", scatter_dimension=1, tiled=True),
            lax.psum_scatter(d_qv, "fsdp", scatter_dimension=2, tiled=True),
            lax.psum_scatter(d_up_groups, "fsdp", scatter_dimension=1, tiled=True),
        )
        pieces = lax.psum(
            (
                pieces[0],
                pieces[1],
                pieces[2],
                pieces[3],
                pieces[4],
                pieces[5],
                pieces[6],
                pieces[7],
                pieces[8],
                pieces[9],
            ),
            "rep",
        )
        shard_grads[layer_index] = pieces
    stacked = [jnp.stack([shard_grads[0][member]]) for member in range(10)]
    return (
        block_out,
        upstream,
        stacked[4],
        stacked[5],
        stacked[0],
        stacked[8],
        stacked[1],
        stacked[2],
        stacked[9],
        stacked[3],
        stacked[6],
        stacked[7],
    )


def solution(mesh):
    placed = (
        P(("rep", "fsdp"), None),
        P(("rep", "fsdp")),
        P(("rep", "fsdp")),
        P(None, None, "fsdp"),
        P(None, None, "fsdp"),
        P(None, "fsdp", None, "tp"),
        P(None, None, "tp", "fsdp"),
        P(None, "tp", "fsdp"),
        P(None, "fsdp", "tp"),
        P(None, "tp", "fsdp"),
        P(None, "tp", "fsdp"),
        P(None, None, "fsdp"),
        P(None, None, "fsdp"),
        P(("rep", "fsdp"), None),
    )
    return jax.shard_map(
        local,
        mesh=mesh,
        in_specs=placed,
        out_specs=(
            P(("rep", "fsdp"), None),
            P(("rep", "fsdp"), None),
            P(None, None, "fsdp"),
            P(None, None, "fsdp"),
            P(None, "fsdp", None, "tp"),
            P(None, None, "tp", "fsdp"),
            P(None, "tp", "fsdp"),
            P(None, "fsdp", "tp"),
            P(None, "tp", "fsdp"),
            P(None, "tp", "fsdp"),
            P(None, None, "fsdp"),
            P(None, None, "fsdp"),
        ),
        check_vma=False,
    )
```

profile of v0, /device:TPU:0, one launch (start us, length us, event | category | flops | bytes accessed | tf_op | source)
XLA Modules:
  0.0 1491.6 jit_solution(13915368727927495780)
XLA Ops:
  8.7 14.8 all-gather.4
  23.8 11.9 all-gather.1
  35.7 8.4 all-gather.2
  44.7 31.1 %all-gather.18.cloned.1.call-done = bf16[1,1024,3,512]{3,1,2,0:T(8,128)(2,1)} async-done(((bf16[1,256,3,512]{3,1,2,0:T(8,128)(2,1)}), bf16[1,1024,3,512]{3,1,2,0:T(8,128)(2,1)}) %all-gather.18.cloned.1.call-update) | async-done | bytes 3145744 | tf_op jit(solution)/shard_map/all_gather | solution.py:49
  75.8 4.7 copy.122
  80.5 3.3 fusion.59
  87.3 9.2 all-reduce
  97.5 45.5 %all-gather.16.cloned.1.call-done = bf16[1408,2,512]{2,0,1:T(8,128)(2,1)} async-done(((bf16[352,2,512]{2,0,1:T(8,128)(2,1)}), bf16[1408,2,512]{2,0,1:T(8,128)(2,1)}) %all-gather.16.cloned.1.call-update) | async-done | bytes 2883600 | tf_op jit(solution)/shard_map/all_gather | solution.py:242
  143.0 3.6 fusion.119
  148.4 2.7 copy.131
  155.6 51.1 %while.28 = (s32[]{:T(128)}, bf16[8,352,64]{1,2,0:T(8,128)(2,1)S(1)}, f32[8,352]{1,0:T(8,128)}, bf16[8,352,64]{2,1,0:T(8,128)(2,1)S(1)}, bf16[8,1408,64]{2,1,0:T...) while((s32[]{:T(128)}, ...), condition=%wide.region_5.6_spmd.clone, body=%wide.region_2.5_spmd.clone.sunk | while | flops 137803424 | bytes 6866433 | solution.py:109
  206.7 3.3 fusion.95
  211.3 13.2 all-gather.8
  224.6 8.4 all-gather.6
  233.0 9.0 all-gather
  242.6 14.9 %all-reduce.9.cloned.1.call-done = f32[352,1024]{1,0:T(8,128)} async-done(((f32[352,1024]{1,0:T(8,128)}), f32[352,1024]{1,0:T(8,128)}) %all-reduce.9.cloned.1.call-update) | async-done | bytes 1441808 | tf_op jit(solution)/shard_map/psum | solution.py:44
  259.6 80.2 %all-gather.22.cloned.1.call-done = bf16[1,1024,2048]{2,1,0:T(8,128)(2,1)} async-done(((bf16[1,256,2048]{2,1,0:T(8,128)(2,1)}), bf16[1,1024,2048]{2,1,0:T(8,128)(2,1)}) %all-gather.22.cloned.1.call-update) | async-done | bytes 4194320 | tf_op jit(solution)/shard_map/all_gather | solution.py:51
  339.7 6.0 multiply_convert_fusion
  345.8 74.4 %all-gather.24.cloned.1.call-done = bf16[1,2048,1024]{2,1,0:T(8,128)(2,1)} async-done(((bf16[1,2048,256]{2,1,0:T(8,128)(2,1)}), bf16[1,2048,1024]{2,1,0:T(8,128)(2,1)}) %all-gather.24.cloned.1.call-update) | async-done | bytes 4194320 | tf_op jit(solution)/shard_map/all_gather | solution.py:52
  420.2 6.9 fusion.125
  428.3 2.8 fusion.55
  431.2 46.9 %all-reduce.11.cloned.1.call-done = f32[352,1024]{1,0:T(8,128)} async-done(((f32[352,1024]{1,0:T(8,128)}), f32[352,1024]{1,0:T(8,128)}) %all-reduce.11.cloned.1.call-update) | async-done | bytes 1441808 | tf_op jit(solution)/shard_map/psum | solution.py:44
  486.0 83.8 %while.29 = (s32[]{:T(128)}, f32[8,352,64]{1,2,0:T(8,128)}, f32[8,1408,64]{1,2,0:T(8,128)}, f32[8,1408,64]{1,2,0:T(8,128)}, bf16[8,352,64]{2,1,0:T(8,128)(2,1)},...) while((s32[]{:T(128)}, f32[8,352,64]{1,2,0:T(8,128)}, ...), condition=%wide.region_15.16_spmd.clone, body=%wide.region_13.15_spmd.clone.sunk | while | flops 322848416 | bytes 11573533 | solution.py:140
  569.9 3.4 copy.140
  573.3 3.5 copy.139
  576.8 5.8 pad_maximum_fusion
  582.9 5.4 fusion.53
  589.8 95.2 %reduce-scatter.24.cloned.1.call-done = f32[352,2,512]{2,0,1:T(8,128)} async-done(((f32[1408,2,512]{2,0,1:T(8,128)}), f32[352,2,512]{2,0,1:T(8,128)}) %reduce-scatter.24.cloned.1.call-update) | async-done | bytes 1441808 | tf_op jit(solution)/shard_map/reduce_scatter | solution.py:359
  685.1 4.7 fusion.80
  690.8 3.4 fusion.106
  694.3 7.1 fusion.99
  702.0 7.0 fusion.102
  710.0 6.0 fusion.92
  721.0 49.6 %all-reduce.15.cloned.1.call-done = (f32[352,1024]{1,0:T(8,128)}, f32[352,1024]{1,0:T(8,128)}) async-done(((f32[352,1024]{1,0:T(8,128)}, f32[352,1024]{1,0:T(8,128)}), (f32[352,1024]{1,0:T(8,128)}, f32[352,1024]{1,0:T(8,128)})) %all-reduce.15.cloned.1.call-update) | async-done | bytes 2883600 | tf_op jit(solution)/shard_map/psum | solution.py:44
  778.6 38.3 %reduce-scatter.28.cloned.1.call-done = f32[512,256]{1,0:T(8,128)} async-done(((f32[512,1024]{1,0:T(8,128)}), f32[512,256]{1,0:T(8,128)}) %reduce-scatter.28.cloned.1.call-update) | async-done | bytes 524304 | tf_op jit(solution)/shard_map/reduce_scatter | solution.py:389
  817.0 146.2 %reduce-scatter.30.cloned.1.call-done = f32[256,2048]{1,0:T(8,128)} async-done(((f32[1024,2048]{1,0:T(8,128)}), f32[256,2048]{1,0:T(8,128)}) %reduce-scatter.30.cloned.1.call-update) | async-done | bytes 2097168 | tf_op jit(solution)/shard_map/reduce_scatter | solution.py:390
  963.2 147.5 %reduce-scatter.32.cloned.1.call-done = f32[2048,256]{1,0:T(8,128)} async-done(((f32[2048,1024]{1,0:T(8,128)}), f32[2048,256]{1,0:T(8,128)}) %reduce-scatter.32.cloned.1.call-update) | async-done | bytes 2097168 | tf_op jit(solution)/shard_map/reduce_scatter | solution.py:391
  1110.7 113.7 %reduce-scatter.26.cloned.1.call-done = f32[256,3,512]{2,0,1:T(8,128)} async-done(((f32[1024,3,512]{2,0,1:T(8,128)}), f32[256,3,512]{2,0,1:T(8,128)}) %reduce-scatter.26.cloned.1.call-update) | async-done | bytes 1572880 | tf_op jit(solution)/shard_map/reduce_scatter | solution.py:388
  1224.4 21.8 %reduce-scatter.40.cloned.1.call-done = f32[16,32]{1,0:T(8,128)} async-done(((f32[64,32]{1,0:T(8,128)}), f32[16,32]{1,0:T(8,128)}) %reduce-scatter.40.cloned.1.call-update) | async-done | bytes 2064
  1247.0 19.3 %reduce-scatter.38.cloned.1.call-done = f32[16,16]{1,0:T(8,128)} async-done(((f32[64,16]{1,0:T(8,128)}), f32[16,16]{1,0:T(8,128)}) %reduce-scatter.38.cloned.1.call-update) | async-done | bytes 1040
  1267.1 3.0 fusion.88
  1270.1 18.9 %reduce-scatter.36.cloned.1.call-done = f32[256,2]{1,0:T(8,128)} async-done(((f32[1024,2]{1,0:T(8,128)}), f32[256,2]{1,0:T(8,128)}) %reduce-scatter.36.cloned.1.call-update) | async-done | bytes 2064
  1289.9 21.8 %reduce-scatter.34.cloned.1.call-done = f32[256,2]{1,0:T(8,128)} async-done(((f32[1024,2]{1,0:T(8,128)}), f32[256,2]{1,0:T(8,128)}) %reduce-scatter.34.cloned.1.call-update) | async-done | bytes 2064
  1312.7 21.8 %reduce-scatter.42.cloned.1.call-done = f32[256,2]{1,0:T(8,128)} async-done(((f32[1024,2]{1,0:T(8,128)}), f32[256,2]{1,0:T(8,128)}) %reduce-scatter.42.cloned.1.call-update) | async-done | bytes 2064
  1335.6 21.4 %reduce-scatter.44.cloned.1.call-done = f32[256,2]{1,0:T(8,128)} async-done(((f32[1024,2]{1,0:T(8,128)}), f32[256,2]{1,0:T(8,128)}) %reduce-scatter.44.cloned.1.call-update) | async-done | bytes 2064
  1358.0 11.8 all-reduce.1
  1370.4 107.0 %all-reduce.13.cloned.1.call-done = (f32[1,256,3,512]{3,1,2,0:T(8,128)}, f32[1,512,256]{2,1,0:T(8,128)}, f32[1,256,2048]{2,1,0:T(8,128)}, f32[1,2048,256]{2,1,0:T(8,128)}) async-done(((f32[1,256,3,512]{3,1,2,0:T(8,128)}, f32[1,512,256]{2,1,0:T(8,128)}, f32[1,256,2048]{2,1,0:T(8,128)}, f32[1,2048,256]{2,1,0:T(8,128)}), (f32[1,256,3,512]{3,1,2,0:T(8,128)}, f32[1,512,256]{2,1,0:T(8,128)}, ...) | async-done | bytes 6291472 | tf_op jit(solution)/shard_map/psum | solution.py:399
  1477.5 2.8 copy.203
  (322 shorter events, 187.9 us)
Async XLA Ops:
  7.2 36.9 %copy-start = (bf16[352,1024]{1,0:T(8,128)(2,1)S(1)}, bf16[352,1024]{1,0:T(8,128)(2,1)}, u32[]{:S(2)}) copy-start(bf16[352,1024]{1,0:T(8,128)(2,1)} %param.18) | copy-start | bytes 2162692
  7.2 68.6 %all-gather.18.cloned.1.call-start = ((), (), s32[]{:S(2)}) async-start(), calls=%async_computation.19 | async-start | bytes 3932160 | tf_op jit(solution)/shard_map/all_gather | solution.py:49
  7.9 135.1 %all-gather.16.cloned.1.call-start = ((), (), s32[]{:S(2)}) async-start(), calls=%async_computation.11 | async-start | bytes 3604480 | tf_op jit(solution)/shard_map/all_gather | solution.py:242
  44.3 36.2 %copy-start.18 = (f32[352]{0:T(512)}, f32[352]{0:T(512)S(1)}, u32[]{:S(2)}) copy-start(f32[352]{0:T(512)S(1)} %broadcast_multiply_fusion.5) | copy-start | bytes 4228
  44.6 35.9 %copy-start.22 = (f32[352]{0:T(512)}, f32[352]{0:T(512)S(1)}, u32[]{:S(2)}) copy-start(f32[352]{0:T(512)S(1)} %add_rsqrt_fusion.1) | copy-start | bytes 4228
  44.6 35.9 %copy-start.24 = (f32[1,1,1024]{2,1,0:T(1,128)}, f32[1,1,1024]{2,1,0:T(1,128)S(1)}, u32[]{:S(2)}) copy-start(f32[1,1,1024]{2,1,0:T(1,128)S(1)} %get-tuple-element.461) | copy-start | bytes 12292
  84.0 1.8 copy-start.37
  84.0 3.0 copy-start.17
  84.0 3.0 copy-start.33
  85.0 121.7 %all-gather.20.cloned.1.call-start = ((), (), s32[]{:S(2)}) async-start(), calls=%async_computation.20 | async-start | bytes 1310720 | tf_op jit(solution)/shard_map/all_gather | solution.py:50
  85.7 171.8 %all-reduce.9.cloned.1.call-start = ((), (), s32[]{:S(2)}) async-start(), calls=%async_computation.12 | async-start | bytes 2883584 | tf_op jit(solution)/shard_map/psum | solution.py:44
  206.7 3.3 copy-start.7
  206.7 3.3 copy-start.11
  210.0 14.6 copy-start.34
  210.0 23.0 %copy-start.35 = (bf16[1,2,256]{2,1,0:T(2,128)(2,1)S(1)}, bf16[1,2,256]{2,1,0:T(2,128)(2,1)}, u32[]{:S(2)}) copy-start(bf16[1,2,256]{2,1,0:T(2,128)(2,1)} %param.30) | copy-start | bytes 3076
  210.0 129.7 %all-gather.22.cloned.1.call-start = ((), (), s32[]{:S(2)}) async-start(), calls=%async_computation.21 | async-start | bytes 5242880 | tf_op jit(solution)/shard_map/all_gather | solution.py:51
  210.6 209.6 %all-gather.24.cloned.1.call-start = ((), (), s32[]{:S(2)}) async-start(), calls=%async_computation.22 | async-start | bytes 5242880 | tf_op jit(solution)/shard_map/all_gather | solution.py:52
  211.2 266.9 %all-reduce.11.cloned.1.call-start = ((), (), s32[]{:S(2)}) async-start(), calls=%async_computation.13 | async-start | bytes 2883584 | tf_op jit(solution)/shard_map/psum | solution.py:44
  242.0 178.2 %copy-start.20 = (f32[1,1,1024]{2,1,0:T(1,128)}, f32[1,1,1024]{2,1,0:T(1,128)S(1)}, u32[]{:S(2)}) copy-start(f32[1,1,1024]{2,1,0:T(1,128)S(1)} %get-tuple-element.456) | copy-start | bytes 12292
  339.7 80.5 %copy-start.3 = (bf16[352,1024]{1,0:T(8,128)(2,1)S(1)}, bf16[352,1024]{1,0:T(8,128)(2,1)}, u32[]{:S(2)}) copy-start(bf16[352,1024]{1,0:T(8,128)(2,1)} %param.31) | copy-start | bytes 2162692
  420.2 8.1 copy-start.36
  431.1 254.0 %reduce-scatter.24.cloned.1.call-start = ((), (), s32[]{:S(2)}) async-start(), calls=%async_computation.14 | async-start | bytes 7208960 | tf_op jit(solution)/shard_map/reduce_scatter | solution.py:359
  478.1 2.7 copy-start.4
  478.1 2.7 copy-start.5
  480.9 2.7 copy-start.6
  582.6 188.0 %all-reduce.15.cloned.1.call-start = ((), (), s32[]{:S(2)}) async-start(), calls=%async_computation.30 | async-start | bytes 5767168 | tf_op jit(solution)/shard_map/psum | solution.py:44
  589.8 100.0 %copy-start.13 = (bf16[352,1,512]{2,0,1:T(8,128)(2,1)}, bf16[352,1,512]{2,0,1:T(8,128)(2,1)S(1)}, u32[]{:S(2)}) copy-start(bf16[352,1,512]{2,0,1:T(8,128)(2,1)S(1)} %copy.141) | copy-start | bytes 1081348
  689.8 127.1 %reduce-scatter.28.cloned.1.call-start = ((), (), s32[]{:S(2)}) async-start(), calls=%async_computation.16 | async-start | bytes 2621440 | tf_op jit(solution)/shard_map/reduce_scatter | solution.py:389
  694.2 269.0 %reduce-scatter.30.cloned.1.call-start = ((), (), s32[]{:S(2)}) async-start(), calls=%async_computation.17 | async-start | bytes 10485760 | tf_op jit(solution)/shard_map/reduce_scatter | solution.py:390
  701.4 409.3 %reduce-scatter.32.cloned.1.call-start = ((), (), s32[]{:S(2)}) async-start(), calls=%async_computation.18 | async-start | bytes 10485760 | tf_op jit(solution)/shard_map/reduce_scatter | solution.py:391
  709.1 515.3 %reduce-scatter.26.cloned.1.call-start = ((), (), s32[]{:S(2)}) async-start(), calls=%async_computation.15 | async-start | bytes 7864320 | tf_op jit(solution)/shard_map/reduce_scatter | solution.py:388
  716.0 530.2 %reduce-scatter.40.cloned.1.call-start = ((), (), s32[]{:S(2)}) async-start(), calls=%async_computation.26 | async-start | bytes 40960
  717.5 548.8 %reduce-scatter.38.cloned.1.call-start = ((), (), s32[]{:S(2)}) async-start(), calls=%async_computation.25 | async-start | bytes 40960
  718.8 53.9 %copy-start.28 = (f32[1,1,1024]{2,1,0:T(1,128)S(1)}, f32[1,1,1024]{2,1,0:T(1,128)}, u32[]{:S(2)}) copy-start(f32[1,1,1024]{2,1,0:T(1,128)} %get-tuple-element.454) | copy-start | bytes 12292
  721.0 568.0 %reduce-scatter.36.cloned.1.call-start = ((), (), s32[]{:S(2)}) async-start(), calls=%async_computation.24 | async-start | bytes 655360
  770.6 2.2 copy-start.15
  772.8 1.3 copy-start.27
  772.8 2.5 copy-start.26
  774.1 2.3 copy-start.30
  775.1 2.3 copy-start.29
  775.2 536.6 %reduce-scatter.34.cloned.1.call-start = ((), (), s32[]{:S(2)}) async-start(), calls=%async_computation.23 | async-start | bytes 655360
  776.3 558.3 %reduce-scatter.42.cloned.1.call-start = ((), (), s32[]{:S(2)}) async-start(), calls=%async_computation.27 | async-start | bytes 655360
  777.4 579.5 %reduce-scatter.44.cloned.1.call-start = ((), (), s32[]{:S(2)}) async-start(), calls=%async_computation.28 | async-start | bytes 655360
  778.6 698.9 %all-reduce.13.cloned.1.call-start = ((), (), s32[]{:S(2)}) async-start(), calls=%async_computation.29 | async-start | bytes 12582912 | tf_op jit(solution)/shard_map/psum | solution.py:399
  1224.4 42.8 %copy-start.2 = (f32[352,1024]{1,0:T(8,128)S(1)}, f32[352,1024]{1,0:T(8,128)}, u32[]{:S(2)}) copy-start(f32[352,1024]{1,0:T(8,128)} %copy-done.1) | copy-start | bytes 4325380
  1477.5 2.8 copy-start.16
  1477.5 3.6 copy-start.10
  1481.1 2.3 copy-start.9
  (10 other events, 9.9 us)
Sparse Core Ops, SparseCore 0:
  9.6 66.1 all-gather.17
  85.1 57.8 all-gather.15
  144.6 28.6 all-gather.19
  210.2 47.3 all-reduce.8
  259.0 80.7 all-gather.21
  341.2 79.0 all-gather.23
  431.2 46.8 all-reduce.10
  582.7 102.2 reduce-scatter.23
  690.0 80.5 all-reduce.14
  773.3 43.6 reduce-scatter.27
  819.3 143.7 reduce-scatter.29
  965.4 145.2 reduce-scatter.31
  1112.9 111.3 reduce-scatter.25
  1226.5 19.7 reduce-scatter.39
  1248.9 17.3 reduce-scatter.37
  1269.0 19.9 reduce-scatter.35
  1291.6 20.0 reduce-scatter.33
  1314.5 20.0 reduce-scatter.41
  1336.9 20.0 reduce-scatter.43
  1359.4 117.9 all-reduce.12
where the time goes:
time: 1500 us; the launch traced here: 1490 us
  waiting for transfers between devices  1120 us (75%)
  matrix products  158 us (11%)
  blocking collectives  86.7 us (6%)
  local copies, waits for them, and re-layouts  79.9 us (5%)
  other arithmetic  32 us (2%)
  between operations  15.5 us (1%)
    reduce_scatter x1, waiting for transfers between devices, local(): lax.psum_scatter(d_down, 'fsdp', scatter_dimension=1, tiled=True)  147 us
    reduce_scatter x1, waiting for transfers between devices, local(): lax.psum_scatter(d_up, 'fsdp', scatter_dimension=0, tiled=True)  146 us
    unnamed x26, waiting for transfers between devices  128 us
    reduce_scatter x1, waiting for transfers between devices, local(): lax.psum_scatter(d_qkv, 'fsdp', scatter_dimension=0, tiled=True)  114 us
    psum x3, waiting for transfers between devices, sum_heads(): return lax.psum(partial_value, 'tp')  111 us
    psum x1, waiting for transfers between devices, local(): lax.psum((pieces[0], pieces[1], pieces[2], pieces[3], pieces[4], pieces[5...  107 us
    reduce_scatter x1, waiting for transfers between devices, local(): d_local = lax.psum_scatter(d_pairs, 'fsdp', scatter_dimension=0, tiled=True)  95.2 us
    all_gather x1, waiting for transfers between devices, gather_forward(): lax.all_gather(w_up, 'fsdp', axis=0, tiled=True)  80.2 us
  transfers between devices with their start and end apart: 20, of which 19 were waited for; matrix products, arithmetic and copies ran while one was open for 9% of the time, Pallas kernels for 0%

commit v1 on v0

v1 whole, which is shorter than its diff:
```python
import functools

import jax
import jax.numpy as jnp
from jax import lax
from jax.experimental import pallas as pl
from jax.experimental.pallas import tpu as pltpu
from jax.sharding import PartitionSpec as P

HD = 64
QB = 128
EPSILON = 1e-06
ROOT_HALF = 0.7071067811865476
INV_ROOT_TWO_PI = 0.3989422804014327
NEG_LARGE = -1e30
BF = jnp.bfloat16
F32 = jnp.float32


def norm_forward(values, gain, shift):
    centred = values - jnp.mean(values, axis=-1, keepdims=True)
    inverse = lax.rsqrt(jnp.mean(centred * centred, axis=-1, keepdims=True) + EPSILON)
    normal_part = centred * inverse
    return (normal_part * gain + shift, normal_part, inverse)


def norm_backward(upstream, normal_part, inverse, gain):
    scaled = upstream * gain
    inner = (
        scaled
        - jnp.mean(scaled, axis=-1, keepdims=True)
        - normal_part * jnp.mean(scaled * normal_part, axis=-1, keepdims=True)
    )
    return (inverse * inner, jnp.sum(upstream * normal_part, axis=0), jnp.sum(upstream, axis=0))


def gelu_value(pre):
    return 0.5 * pre * (1.0 + lax.erf(pre * ROOT_HALF))


def gelu_slope(pre):
    return 0.5 * (1.0 + lax.erf(pre * ROOT_HALF)) + pre * INV_ROOT_TWO_PI * jnp.exp(
        -0.5 * pre * pre
    )


def dot(a, b):
    return jnp.dot(a, b, preferred_element_type=F32)


def dot_nt(a, b):
    return lax.dot_general(a, b, (((1,), (1,)), ((), ())), preferred_element_type=F32)


def dot_tn(a, b):
    return lax.dot_general(a, b, (((0,), (0,)), ((), ())), preferred_element_type=F32)


def spread_heads(rows, heads):
    wide = rows.astype(F32)
    lane_head = lax.broadcasted_iota(jnp.int32, wide.shape, 1) // HD
    parts = [jnp.where(lane_head == h, wide, 0.0) for h in range(heads)]
    return jnp.concatenate(parts, axis=0).astype(BF)


def own_blocks(across, heads):
    return jnp.concatenate(
        [across[h * HD : (h + 1) * HD, h * QB : (h + 1) * QB] for h in range(heads)], axis=0
    )


def fill_bias(bias_ref, key_ref, query_row, off):
    bias_ref[...] = jnp.where(key_ref[...] == query_row, 0.0, NEG_LARGE)
    eye = lax.broadcasted_iota(jnp.int32, (QB, QB), 0) == lax.broadcasted_iota(
        jnp.int32, (QB, QB), 1
    )
    bias_ref[pl.ds(off, QB), :] = jnp.where(eye, 0.0, bias_ref[pl.ds(off, QB), :])


def forward_kernel(heads, x_ref, key_ref, seg_ref, o_ref, lse_ref, vt_ref, bias_ref):
    width = heads * HD
    total_rows = x_ref.shape[0]
    vt_ref[...] = x_ref[:, 2 * width : 3 * width].astype(F32).T.astype(BF)

    def step(i, carry):
        off = pl.multiple_of(i * QB, QB)
        query = spread_heads(x_ref[pl.ds(off, QB), 0:width] * (HD**-0.5), heads)
        fill_bias(bias_ref, key_ref, seg_ref[i], off)
        scores = dot_nt(x_ref[:, width : 2 * width], query)
        bias = bias_ref[...]
        scores = scores + jnp.concatenate([bias] * heads, axis=1)
        top = jnp.max(scores, axis=0, keepdims=True)
        expo = jnp.exp(scores - top)
        total = jnp.sum(expo, axis=0, keepdims=True)
        weights = (expo * (1.0 / total)).astype(BF)
        mixed = own_blocks(dot(vt_ref[...], weights), heads)
        o_ref[pl.ds(off, QB), :] = mixed.T.astype(BF)
        lse_ref[i] = top + jnp.log(total)
        return carry

    lax.fori_loop(0, total_rows // QB, step, 0)


def backward_kernel(
    heads,
    x_ref,
    o_ref,
    g_ref,
    lse_ref,
    key_ref,
    seg_ref,
    dx_ref,
    sums_ref,
    kt_ref,
    dk_ref,
    dv_ref,
    bias_ref,
):
    width = heads * HD
    total_rows = x_ref.shape[0]
    kt_ref[...] = x_ref[:, width : 2 * width].astype(F32).T.astype(BF)
    dk_ref[...] = jnp.zeros_like(dk_ref)
    dv_ref[...] = jnp.zeros_like(dv_ref)

    def step(i, query_sum):
        off = pl.multiple_of(i * QB, QB)
        query = spread_heads(x_ref[pl.ds(off, QB), 0:width] * (HD**-0.5), heads)
        g_rows = g_ref[pl.ds(off, QB), :]
        grad = spread_heads(g_rows, heads)
        product = (g_rows.astype(F32) * o_ref[pl.ds(off, QB), :].astype(F32)).T
        delta = jnp.concatenate(
            [
                jnp.sum(product[h * HD : (h + 1) * HD], axis=0, keepdims=True)
                for h in range(heads)
            ],
            axis=1,
        )
        fill_bias(bias_ref, key_ref, seg_ref[i], off)
        scores = dot_nt(x_ref[:, width : 2 * width], query)
        bias = bias_ref[...]
        probs = jnp.exp(scores + jnp.concatenate([bias] * heads, axis=1) - lse_ref[i])
        d_probs = dot_nt(x_ref[:, 2 * width : 3 * width], grad)
        dv_ref[...] += dot(probs.astype(BF), grad)
        d_scores = (probs * (d_probs - delta)).astype(BF)
        dk_ref[...] += dot(d_scores, query)
        d_query = own_blocks(dot(kt_ref[...], d_scores), heads).T * (HD**-0.5)
        dx_ref[pl.ds(off, QB), 0:width] = d_query.astype(BF)
        return query_sum + jnp.sum(d_query, axis=0, keepdims=True)

    query_sum = lax.fori_loop(0, total_rows // QB, step, jnp.zeros((1, width), F32))
    dx_ref[:, width : 2 * width] = dk_ref[...].astype(BF)
    dx_ref[:, 2 * width : 3 * width] = dv_ref[...].astype(BF)
    sums_ref[...] = jnp.concatenate(
        [query_sum, jnp.sum(dv_ref[...], axis=0, keepdims=True)], axis=0
    )


def attend_forward(x, key_codes, seg_rows, heads):
    rows = x.shape[0]
    width = heads * HD
    return pl.pallas_call(
        functools.partial(forward_kernel, heads),
        out_shape=(
            jax.ShapeDtypeStruct((rows, width), BF),
            jax.ShapeDtypeStruct((rows // QB, 1, heads * QB), F32),
        ),
        scratch_shapes=[pltpu.VMEM((width, rows), BF), pltpu.VMEM((rows, QB), F32)],
        cost_estimate=pl.CostEstimate(
            flops=4 * rows * rows * width,
            transcendentals=rows * rows * heads,
            bytes_accessed=rows * width * 8,
        ),
        name="attend_forward",
    )(x, key_codes, seg_rows)


def attend_backward(x, mixed, grad, lse, key_codes, seg_rows, heads):
    rows = x.shape[0]
    width = heads * HD
    return pl.pallas_call(
        functools.partial(backward_kernel, heads),
        out_shape=(
            jax.ShapeDtypeStruct((rows, 3 * width), BF),
            jax.ShapeDtypeStruct((2, width), F32),
        ),
        scratch_shapes=[
            pltpu.VMEM((width, rows), BF),
            pltpu.VMEM((rows, width), F32),
            pltpu.VMEM((rows, width), F32),
            pltpu.VMEM((rows, QB), F32),
        ],
        cost_estimate=pl.CostEstimate(
            flops=10 * rows * rows * width,
            transcendentals=rows * rows * heads,
            bytes_accessed=rows * width * 20,
        ),
        name="attend_backward",
    )(x, mixed, grad, lse, key_codes, seg_rows)


def after(value, *others):
    return lax.optimization_barrier((value, *others))[0]


def local(
    n,
    reps,
    tokens,
    segment_ids,
    valid_keys,
    norm_gain,
    norm_bias,
    qkv_weight,
    qv_bias,
    out_weight,
    up_weight,
    up_bias,
    down_weight,
    out_bias,
    layer_scale,
    cotangent,
):
    rows, width = tokens.shape
    ys = reps // 2
    local_heads = qv_bias.shape[2]
    hidden = up_weight.shape[2]
    heads = local_heads // n
    head_cols = heads * HD
    unit_cols = hidden // reps
    part = width // n
    z = lax.axis_index("fsdp")
    rep = lax.axis_index("rep")
    y, core = rep // 2, rep % 2

    def z_pull(x, s):
        return lax.ppermute(x, "fsdp", [((j + s) % n, j) for j in range(n)])

    def z_push(x, s):
        return z_pull(x, n - s)

    def y_pull(x, d):
        return lax.ppermute(
            x, "rep", [(((a + d) % ys) * 2 + c, a * 2 + c) for a in range(ys) for c in range(2)]
        )

    def y_push(x, d):
        return y_pull(x, ys - d)

    def core_swap(x):
        return lax.ppermute(x, "rep", [(r, r ^ 1) for r in range(reps)])

    def gather_z(x):
        return [x] + [z_pull(x, s) for s in range(1, n)]

    def gather_rep(x):
        near = [x] + [y_pull(x, d) for d in range(1, ys)]
        return near + [core_swap(v) for v in near]

    slot_rep = [((y + d) % ys) * 2 + core for d in range(ys)]
    slot_rep = slot_rep + [((y + d) % ys) * 2 + 1 - core for d in range(ys)]

    def in_rep_order(slots, axis):
        stacked = jnp.stack(slots)
        picks = []
        for a in range(reps):
            slot = (a // 2 - y) % ys + ys * ((a % 2) ^ core)
            picks.append(lax.dynamic_index_in_dim(stacked, slot, 0, keepdims=False))
        return jnp.concatenate(picks, axis=axis)

    def from_own(x, axis, block):
        return lax.dynamic_slice_in_dim(
            jnp.concatenate([x, x], axis=axis), z * block, x.shape[axis], axis
        )

    def to_plain(x, axis, block):
        return lax.dynamic_slice_in_dim(
            jnp.concatenate([x, x], axis=axis), ((n - z) % n) * block, x.shape[axis], axis
        )

    def sum_tp(x):
        mine = x
        return mine + lax.ppermute(mine, "tp", [(0, 1), (1, 0)])

    def exchange_heads(slots):
        stacked = jnp.stack(slots)
        blocks = [lax.dynamic_index_in_dim(stacked, z, 0, keepdims=False)]
        for s in range(1, n):
            out = lax.dynamic_index_in_dim(stacked, (z + n - s) % n, 0, keepdims=False)
            blocks.append(z_pull(out, s))
        return jnp.concatenate(blocks, axis=0)

    def return_heads(x):
        blocks = [x[s * rows : (s + 1) * rows] for s in range(n)]
        return [blocks[0]] + [z_pull(blocks[n - s], s) for s in range(1, n)]

    q_cols = local_heads * HD // reps
    piece_qkv = lax.dynamic_slice_in_dim(qkv_weight[0], rep * q_cols, q_cols, 2).reshape(
        part, 3 * q_cols
    )
    piece_out = lax.dynamic_slice_in_dim(out_weight[0], rep * q_cols, q_cols, 0)
    piece_up = lax.dynamic_slice_in_dim(up_weight[0], rep * unit_cols, unit_cols, 1)
    piece_down = lax.dynamic_slice_in_dim(down_weight[0], rep * unit_cols, unit_cols, 0)

    codes = (segment_ids * 2 + valid_keys).astype(F32).astype(BF)
    code_rows = -(-rows // part)
    codes = jnp.pad(codes, (0, code_rows * part - rows)).reshape(code_rows, part)
    features = jnp.concatenate([norm_gain[0], norm_bias[0], out_bias[0], layer_scale[0], codes])
    units = jnp.concatenate([qv_bias.reshape(2 * local_heads, -1), up_bias[0]])

    gathered_qkv = gather_z(piece_qkv)
    gathered_features = gather_z(features)
    gathered_units = gather_z(units)
    slots_qkv = gather_rep(jnp.concatenate(gathered_qkv, axis=0))
    w_qkv = jnp.concatenate(slots_qkv, axis=1)

    piece_out = after(piece_out, *gathered_qkv)
    piece_up = after(piece_up, *gathered_qkv)
    w_out = jnp.concatenate(gather_rep(jnp.concatenate(gather_z(piece_out), axis=1)), axis=0)
    w_up = jnp.concatenate(gather_rep(jnp.concatenate(gather_z(piece_up), axis=0)), axis=1)

    small = jnp.concatenate([f[:8] for f in gathered_features], axis=1).astype(F32)
    gains, shifts, biases, scales = small[0:2], small[2:4], small[4:6], small[6:8]
    all_codes = jnp.concatenate([f[8:].reshape(-1)[:rows] for f in gathered_features])
    all_codes = all_codes.astype(jnp.int32)
    group_seg = all_codes // 2
    key_codes = jnp.where(all_codes % 2 == 1, group_seg, -1)
    group_rows = all_codes.shape[0]
    key_codes = jnp.broadcast_to(key_codes[:, None], (group_rows, QB))
    seg_rows = group_seg.reshape(group_rows // QB, 1, QB)
    unit_lanes = units.shape[1]
    units_full = to_plain(jnp.concatenate(gathered_units, axis=1), 1, unit_lanes).astype(F32)
    qv_full = units_full[: 2 * local_heads].reshape(2, local_heads * HD)
    up_full = units_full[2 * local_heads :].reshape(-1)
    qv_slots = [lax.dynamic_slice_in_dim(qv_full, r * q_cols, q_cols, 1) for r in slot_rep]
    up_slots = jnp.concatenate(
        [lax.dynamic_slice_in_dim(up_full, r * unit_cols, unit_cols, 0) for r in slot_rep]
    )
    bias_qkv = jnp.concatenate(
        [jnp.concatenate([b[0], jnp.zeros((q_cols,), F32), b[1]]) for b in qv_slots]
    )

    resid = from_own(tokens, 1, part).astype(F32)
    upstream = from_own(cotangent, 1, part).astype(F32)

    normed, part_one, inv_one = norm_forward(resid, gains[0], shifts[0])
    first_in = normed.astype(BF)
    project = (dot(first_in, w_qkv) + bias_qkv).astype(BF)
    slot_cols = 3 * head_cols
    x_heads = exchange_heads([project[:, k * slot_cols : (k + 1) * slot_cols] for k in range(n)])
    piece_down = after(piece_down, x_heads)
    w_down = jnp.concatenate(gather_rep(jnp.concatenate(gather_z(piece_down), axis=1)), axis=0)
    mixed, lse = attend_forward(x_heads, key_codes, seg_rows, heads)
    mixed_slots = to_plain(jnp.stack(return_heads(mixed)), 0, 1)
    mixed_flat = jnp.concatenate([mixed_slots[k] for k in range(n)], axis=1)
    branch_one = sum_tp(dot(mixed_flat, w_out)) + biases[0]
    resid_one = resid + scales[0] * branch_one
    normed_two, part_two, inv_two = norm_forward(resid_one, gains[1], shifts[1])
    second_in = normed_two.astype(BF)
    hidden_pre = dot(second_in, w_up) + up_slots
    hidden_act = gelu_value(hidden_pre).astype(BF)
    branch_two = sum_tp(dot(hidden_act, w_down)) + biases[1]
    block_out = to_plain((resid_one + scales[1] * branch_two).astype(BF), 1, part)

    def reduce_grad(lead, tail, slot_axis, z_axis):
        total = lead + core_swap(tail)
        step = total.shape[slot_axis] // ys
        cuts = [lax.slice_in_dim(total, d * step, (d + 1) * step, axis=slot_axis) for d in range(ys)]
        mine = cuts[0]
        for d in range(1, ys):
            mine = mine + y_push(cuts[d].astype(BF), d).astype(F32)
        block = mine.shape[z_axis] // n
        blocks = [lax.slice_in_dim(mine, s * block, (s + 1) * block, axis=z_axis) for s in range(n)]
        result = blocks[0]
        for s in range(1, n):
            result = result + z_push(blocks[s], s)
        return gather_rep(result)

    scale_two = jnp.sum(upstream * branch_two, axis=0)
    bias_two = jnp.sum(upstream * scales[1], axis=0)
    branch_grad = (upstream * scales[1]).astype(BF)
    half = hidden // 2
    grad_down = reduce_grad(
        dot_tn(hidden_act[:, :half], branch_grad), dot_tn(hidden_act[:, half:], branch_grad), 0, 1
    )
    d_hidden = dot_nt(branch_grad, w_down) * gelu_slope(hidden_pre)
    d_up_bias = jnp.sum(d_hidden, axis=0)
    d_hidden_half = d_hidden.astype(BF)
    grad_up = reduce_grad(
        dot_tn(second_in, d_hidden_half[:, :half]), dot_tn(second_in, d_hidden_half[:, half:]), 1, 0
    )
    d_second = sum_tp(dot_nt(d_hidden_half, w_up))
    d_norm_two, gain_two, shift_two = norm_backward(d_second, part_two, inv_two, gains[1])
    upstream_one = upstream + d_norm_two
    scale_one = jnp.sum(upstream_one * branch_one, axis=0)
    bias_one = jnp.sum(upstream_one * scales[0], axis=0)
    branch_grad_one = (upstream_one * scales[0]).astype(BF)
    half = mixed_flat.shape[1] // 2
    grad_out = reduce_grad(
        dot_tn(mixed_flat[:, :half], branch_grad_one),
        dot_tn(mixed_flat[:, half:], branch_grad_one),
        0,
        1,
    )
    d_mixed = dot_nt(branch_grad_one, w_out).astype(BF)
    g_heads = exchange_heads([d_mixed[:, k * head_cols : (k + 1) * head_cols] for k in range(n)])
    dx_heads, head_sums = attend_backward(
        x_heads, mixed, g_heads, lse, key_codes, seg_rows, heads
    )
    dx_slots = to_plain(jnp.stack(return_heads(dx_heads)), 0, 1)
    d_project = jnp.concatenate([dx_slots[k] for k in range(n)], axis=1)
    half = d_project.shape[1] // 2
    grad_qkv = reduce_grad(
        dot_tn(first_in, d_project[:, :half]), dot_tn(first_in, d_project[:, half:]), 1, 0
    )
    d_first = sum_tp(dot_nt(d_project, w_qkv))
    d_norm_one, gain_one, shift_one = norm_backward(d_first, part_one, inv_one, gains[0])
    tokens_grad = to_plain(upstream_one + d_norm_one, 1, part)

    feature_grads = to_plain(
        jnp.stack(
            [gain_one, gain_two, shift_one, shift_two, bias_one, bias_two, scale_one, scale_two]
        ),
        1,
        part,
    )
    own_rep = lax.dynamic_index_in_dim(jnp.stack(slot_rep), z, 0, keepdims=False)
    qv_grads = lax.dynamic_update_slice_in_dim(
        jnp.zeros((2, local_heads * HD), F32), head_sums, own_rep * head_cols, 1
    )
    up_grads = in_rep_order(
        [d_up_bias[k * unit_cols : (k + 1) * unit_cols] for k in range(reps)], 0
    )
    packed = jnp.concatenate(
        [feature_grads.reshape(-1), qv_grads.reshape(-1), up_grads]
    ).reshape(-1, 128)

    def total_over(values, position, count):
        stacked = jnp.stack(values)
        turned = lax.dynamic_slice_in_dim(
            jnp.concatenate([stacked, stacked]), (count - position) % count, count, 0
        )
        return jnp.sum(turned, axis=0)

    packed = total_over([packed] + [z_pull(packed, s) for s in range(1, n)], z, n)
    packed = total_over([packed] + [y_pull(packed, d) for d in range(1, ys)], y, ys)
    packed = packed + core_swap(packed)
    packed = packed.reshape(-1)
    size_f, size_q = 8 * width, 2 * local_heads * HD
    feature_grads = lax.dynamic_slice_in_dim(
        packed[:size_f].reshape(4, 2, width), z * part, part, 2
    )
    qv_grads = lax.dynamic_slice_in_dim(
        packed[size_f : size_f + size_q].reshape(2, local_heads, HD), z * unit_lanes, unit_lanes, 2
    )
    up_grads = lax.dynamic_slice_in_dim(
        packed[size_f + size_q :].reshape(-1, HD), z * unit_lanes, unit_lanes, 1
    )

    d_qkv = in_rep_order([g.reshape(part, 3, q_cols) for g in grad_qkv], 2)
    return (
        block_out,
        tokens_grad,
        feature_grads[0][None],
        feature_grads[1][None],
        d_qkv[None],
        qv_grads[None],
        in_rep_order(grad_out, 0)[None],
        in_rep_order(grad_up, 1)[None],
        up_grads[None],
        in_rep_order(grad_down, 0)[None],
        feature_grads[2][None],
        feature_grads[3][None],
    )


def solution(mesh):
    n, reps, tp = mesh.shape["fsdp"], mesh.shape["rep"], mesh.shape["tp"]
    assert n == reps and tp == 2
    by_token = P(("rep", "fsdp"), None)
    by_feature = P(None, None, "fsdp")
    by_row = P(None, "fsdp", "tp")
    by_column = P(None, "tp", "fsdp")
    placed = (
        by_token,
        P(("rep", "fsdp")),
        P(("rep", "fsdp")),
        by_feature,
        by_feature,
        P(None, "fsdp", None, "tp"),
        P(None, None, "tp", "fsdp"),
        by_column,
        by_row,
        by_column,
        by_column,
        by_feature,
        by_feature,
        by_token,
    )
    return jax.shard_map(
        functools.partial(local, n, reps),
        mesh=mesh,
        in_specs=placed,
        out_specs=(
            by_token,
            by_token,
            by_feature,
            by_feature,
            P(None, "fsdp", None, "tp"),
            P(None, None, "tp", "fsdp"),
            by_column,
            by_row,
            by_column,
            by_column,
            by_feature,
            by_feature,
        ),
        check_vma=False,
    )
```

time: 1500 us -> 585 us (0.39)
  waiting for transfers between devices: 1120 us -> 310 us
  starting transfers between devices: 1.04 us -> 122 us
  matrix products: 158 us -> 50.4 us
  blocking collectives: 86.7 us -> 0 us
  local copies, waits for them, and re-layouts: 79.9 us -> 28.6 us
  Pallas kernels: 0 us -> 31.8 us
    reduce_scatter x5 -> x0, waiting for transfers between devices: 541 us -> none  [the longest x1 147 us: local(): lax.psum_scatter(d_down, 'fsdp', scatter_dimension=1, tiled=True)]
    ppermute x0 -> x83, waiting for transfers between devices: none -> 310 us  [the longest x45 151 us: z_pull(): return lax.ppermute(x, 'fsdp', [((j + s) % n, j) for j in range(n)])]
    all_gather x5 -> x0, waiting for transfers between devices: 231 us -> none  [the longest x1 80.2 us: gather_forward(): lax.all_gather(w_up, 'fsdp', axis=0, tiled=True)]
    psum x4 -> x0, waiting for transfers between devices: 219 us -> none  [the longest x3 111 us: sum_heads(): return lax.psum(partial_value, 'tp')]
    unnamed x26 -> x0, waiting for transfers between devices: 128 us -> none
    ppermute x0 -> x83, starting transfers between devices: none -> 122 us  [the longest x45 95.7 us: z_pull(): return lax.ppermute(x, 'fsdp', [((j + s) % n, j) for j in range(n)])]
    dot_general x68 -> x16, matrix products: 158 us -> 50.4 us  [the longest x8 22.3 us: dot_tn(): lax.dot_general(a, b, (((0,), (0,)), ((), ())), preferred_element_type=F32)]
    all_gather x6 -> x0, blocking collectives: 65.7 us -> none  [the longest x1 14.8 us: gather_forward(): lax.all_gather(qv_part, 'fsdp', axis=2, tiled=True)]
  transfers between devices with their start and end apart: 20 -> 83, of which waited for: 19 -> 33; matrix products, arithmetic and copies ran while one was open for 9% -> 13% of each run, Pallas kernels for 0% -> 6%
where the time goes in v1:
time: 585 us; the launch traced here: 577 us
  waiting for transfers between devices  310 us (53%)
  starting transfers between devices  122 us (21%)
  matrix products  50.4 us (9%)
  Pallas kernels  31.8 us (5%)
  other arithmetic  30.3 us (5%)
  local copies, waits for them, and re-layouts  28.6 us (5%)
    ppermute x45, waiting for transfers between devices, z_pull(): return lax.ppermute(x, 'fsdp', [((j + s) % n, j) for j in range(n)])  151 us
    ppermute x13, waiting for transfers between devices, y_pull(): lax.ppermute(x, 'rep', [((a + d) % ys * 2 + c, a * 2 + c) for a in range(...  97.7 us
    ppermute x45, starting transfers between devices, z_pull(): return lax.ppermute(x, 'fsdp', [((j + s) % n, j) for j in range(n)])  95.7 us
    ppermute x4, waiting for transfers between devices, sum_tp(): return mine + lax.ppermute(mine, 'tp', [(0, 1), (1, 0)])  61.6 us
    dot_general x8, matrix products, dot_tn(): lax.dot_general(a, b, (((0,), (0,)), ((), ())), preferred_element_type=F32)  22.3 us
    ppermute x13, starting transfers between devices, y_pull(): lax.ppermute(x, 'rep', [((a + d) % ys * 2 + c, a * 2 + c) for a in range(...  17.9 us
    dot_general x4, matrix products, dot_nt(): lax.dot_general(a, b, (((1,), (1,)), ((), ())), preferred_element_type=F32)  16.4 us
    pallas_call x1, Pallas kernels, attend_backward(): pl.pallas_call(functools.partial(backward_kernel, heads), out_shape=(jax....  16.1 us
  transfers between devices with their start and end apart: 83, of which 33 were waited for; matrix products, arithmetic and copies ran while one was open for 13% of the time, Pallas kernels for 6%

profile of v1, /device:TPU:0, one launch (start us, length us, event | category | flops | bytes accessed | tf_op | source)
XLA Modules:
  0.0 576.6 jit_solution(14191849584204383170)
XLA Ops:
  2.2 3.1 collective-permute-start.2
  16.7 3.1 collective-permute-start
  23.3 2.9 collective-permute-done.3
  26.1 10.9 %collective-permute-done.4 = bf16[256,384]{0,1:T(8,128)(2,1)S(1)} collective-permute-done((bf16[256,384]{0,1:T(8,128)(2,1)S(1)}, bf16[256,384]{0,1:T(8,128)(2,1)S(1)}, u32[]{:S(2)}, u32[]{:S(2)}) %collective-permute-start.4) | collective-permute-done | bytes 196640 | tf_op jit(solution)/shard_map/ppermute | solution.py:236
  39.1 15.3 %collective-permute-done.6 = bf16[1024,384]{0,1:T(8,128)(2,1)} collective-permute-done((bf16[1024,384]{0,1:T(8,128)(2,1)S(1)}, bf16[1024,384]{0,1:T(8,128)(2,1)}, u32[]{:S(2)}, u32[]{:S(2)}) %collective-permute-start.6) | collective-permute-done | bytes 786464 | tf_op jit(solution)/shard_map/ppermute | solution.py:242
  56.5 3.3 collective-permute-start.26
  62.6 7.2 %collective-permute-done.18 = bf16[128,256]{1,0:T(8,128)(2,1)S(1)} collective-permute-done((bf16[128,256]{1,0:T(8,128)(2,1)S(1)}, bf16[128,256]{1,0:T(8,128)(2,1)S(1)}, u32[]{:S(2)}, u32[]{:S(2)}) %collective-permute-start.18) | collective-permute-done | bytes 65568 | tf_op jit(solution)/shard_map/ppermute | solution.py:236
  69.8 9.2 %collective-permute-start.19 = (bf16[128,256]{1,0:T(8,128)(2,1)S(1)}, bf16[128,256]{1,0:T(8,128)(2,1)S(1)}, u32[]{:S(2)}, u32[]{:S(2)}) collective-permute-start(bf16[128,256]{1,0:T(8,128)(2,1)S(1)} %dynamic-slice_bitcast_fusion.26), channel_id=1, source_target_pairs={{4,0},{6,2},{0,4},{2,6},{5,1},{7,3},{1,5},{3,7},{12,8},{14,10},{8,... | collective-permute-start | bytes 196616 | tf_op jit(solution)/shard_map/ppermute | solution.py:236
  81.2 3.9 collective-permute-start.20
  95.0 3.1 collective-permute-start.13
  102.0 4.2 collective-permute-done.14
  106.1 8.5 %collective-permute-done.13 = bf16[352,384]{1,0:T(8,128)(2,1)S(1)} collective-permute-done((bf16[352,384]{1,0:T(8,128)(2,1)S(1)}, bf16[352,384]{1,0:T(8,128)(2,1)S(1)}, u32[]{:S(2)}, u32[]{:S(2)}) %collective-permute-start.13) | collective-permute-done | bytes 270368 | tf_op jit(solution)/shard_map/ppermute | solution.py:236
  116.9 15.7 %attend_forward.1 = (bf16[1408,128]{1,0:T(8,128)(2,1)}, f32[11,1,256]{2,1,0:T(1,128)}) custom-call(bf16[1408,384]{1,0:T(8,128)(2,1)} %pad_maximum_fusion.7.x_ref, s32[1408,128]{1,0:T(8,128)} %broadcast_in_dim.18.key_ref, s32[11,1,128]{2,1,0:T(1,128)} %and_select_fusion.seg_ref), custom_call_target="tpu_custom_call" | custom-call | flops 1015021568 | bytes 1441792 | tf_op jit(solution)/shard_map/attend_forward/pallas_call | solution.py:161
  133.6 6.5 %collective-permute-start.15 = (bf16[352,128]{1,0:T(8,128)(2,1)S(1)}, bf16[352,128]{1,0:T(8,128)(2,1)S(1)}, u32[]{:S(2)}, u32[]{:S(2)}) collective-permute-start(bf16[352,128]{1,0:T(8,128)(2,1)S(1)} %get-tuple-element.106), channel_id=1, source_target_pairs={{2,0},{4,2},{6,4},{0,6},{3,1},{5,3},{7,5},{1,7},{10,8},{12,10},{14... | collective-permute-start | bytes 270344 | tf_op jit(solution)/shard_map/ppermute | solution.py:236
  142.8 4.5 collective-permute-start.17
  147.4 3.3 collective-permute-done.16
  159.4 12.8 %collective-permute-done.32 = bf16[512,256]{1,0:T(8,128)(2,1)S(1)} collective-permute-done((bf16[512,256]{1,0:T(8,128)(2,1)S(1)}, bf16[512,256]{1,0:T(8,128)(2,1)S(1)}, u32[]{:S(2)}, u32[]{:S(2)}) %collective-permute-start.32) | collective-permute-done | bytes 262176 | tf_op jit(solution)/shard_map/ppermute | solution.py:236
  176.1 21.2 %collective-permute-done.34 = bf16[512,1024]{1,0:T(8,128)(2,1)} collective-permute-done((bf16[512,1024]{1,0:T(8,128)(2,1)}, bf16[512,1024]{1,0:T(8,128)(2,1)}, u32[]{:S(2)}, u32[]{:S(2)}) %collective-permute-start.34) | collective-permute-done | bytes 1048608 | tf_op jit(solution)/shard_map/ppermute | solution.py:242
  199.8 3.4 multiply_convert_fusion
  203.3 3.8 fusion.39
  208.7 32.5 %collective-permute-done.37 = f32[352,1024]{1,0:T(8,128)S(1)} collective-permute-done((f32[352,1024]{1,0:T(8,128)S(1)}, f32[352,1024]{1,0:T(8,128)S(1)}, u32[]{:S(2)}, u32[]{:S(2)}) %collective-permute-start.37) | collective-permute-done | bytes 1441824 | tf_op jit(solution)/shard_map/ppermute | solution.py:282
  242.8 7.2 %fusion.103 = (f32[2048]{0:T(1024)S(1)}, bf16[352,2048]{1,0:T(8,128)(2,1)S(1)}) fusion(f32[352,2048]{1,0:T(8,128)S(1)} %get-tuple-element.136, bf16[512,1024]{1,0:T(8,128)(2,1)S(1)} %collective-permute-done.36, bf16[512,1024]{1,0:T(8,128)(2,1)S(1)} %collective-permute-done.35, bf16[512,1024]{1,0:T(8,128)(2,1)} %collective-permute-done.34, ...), kind=kOutput, calls=%fused_computation.310 | convolution fusion | flops 1502181376 | bytes 9252864 | tf_op jit(solution)/shard_map/dot_general | solution.py:52
  250.0 4.9 fusion.40
  257.8 4.5 fusion.33
  262.3 3.5 fusion.36
  265.8 22.5 %collective-permute-done.38 = f32[352,1024]{1,0:T(8,128)} collective-permute-done((f32[352,1024]{1,0:T(8,128)}, f32[352,1024]{1,0:T(8,128)}, u32[]{:S(2)}, u32[]{:S(2)}) %collective-permute-start.38) | collective-permute-done | bytes 1441824 | tf_op jit(solution)/shard_map/ppermute | solution.py:282
  299.5 2.8 collective-permute-start.39
  306.9 16.1 %attend_backward.1 = (bf16[1408,384]{1,0:T(8,128)(2,1)}, f32[2,128]{1,0:T(2,128)}) custom-call(bf16[1408,384]{1,0:T(8,128)(2,1)} %pad_maximum_fusion.7.x_ref, bf16[1408,128]{1,0:T(8,128)(2,1)} %get-tuple-element.19.o_ref, bf16[1408,128]{1,0:T(8,128)(2,1)} %pad_maximum_fusion.16.g_ref, f32[11,1,256]{2,1,0:T(1,128)} %get-tuple-element.23.lse_ref, ...), custom_call_target="tpu_custom_call" | custom-call | flops 2537553920 | bytes 3604480 | tf_op jit(solution)/shard_map/attend_backward/pallas_call | solution.py:180
  324.3 3.4 collective-permute-start.42
  329.0 5.3 collective-permute-done.42
  334.4 15.3 %collective-permute-done.43 = bf16[352,384]{1,0:T(8,128)(2,1)S(1)} collective-permute-done((bf16[352,384]{1,0:T(8,128)(2,1)S(1)}, bf16[352,384]{1,0:T(8,128)(2,1)S(1)}, u32[]{:S(2)}, u32[]{:S(2)}) %collective-permute-start.43) | collective-permute-done | bytes 270368 | tf_op jit(solution)/shard_map/ppermute | solution.py:236
  364.7 7.5 %collective-permute-done.62 = f32[128,256]{1,0:T(8,128)S(1)} collective-permute-done((f32[128,256]{1,0:T(8,128)S(1)}, f32[128,256]{1,0:T(8,128)S(1)}, u32[]{:S(2)}, u32[]{:S(2)}) %collective-permute-start.62) | collective-permute-done | bytes 131104 | tf_op jit(solution)/shard_map/ppermute | solution.py:236
  374.2 3.1 collective-permute-done.64
  381.6 6.5 %collective-permute-done.45 = f32[352,1024]{1,0:T(8,128)S(1)} collective-permute-done((f32[352,1024]{1,0:T(8,128)S(1)}, f32[352,1024]{1,0:T(8,128)S(1)}, u32[]{:S(2)}, u32[]{:S(2)}) %collective-permute-start.45) | collective-permute-done | bytes 1441824 | tf_op jit(solution)/shard_map/ppermute | solution.py:282
  395.4 4.8 collective-permute-done.48
  400.3 3.9 convolution_add_fusion.3
  405.6 3.5 convolution_add_fusion.2
  410.3 3.1 convolution_add_fusion.4
  414.7 15.8 %collective-permute-done.68 = bf16[1024,512]{0,1:T(8,128)(2,1)S(1)} collective-permute-done((bf16[1024,512]{0,1:T(8,128)(2,1)S(1)}, bf16[1024,512]{0,1:T(8,128)(2,1)S(1)}, u32[]{:S(2)}, u32[]{:S(2)}) %collective-permute-start.68) | collective-permute-done | bytes 1048608 | tf_op jit(solution)/shard_map/ppermute | solution.py:242
  434.3 18.7 %collective-permute-done.76 = bf16[512,1024]{1,0:T(8,128)(2,1)S(1)} collective-permute-done((bf16[512,1024]{1,0:T(8,128)(2,1)S(1)}, bf16[512,1024]{1,0:T(8,128)(2,1)S(1)}, u32[]{:S(2)}, u32[]{:S(2)}) %collective-permute-start.76) | collective-permute-done | bytes 1048608 | tf_op jit(solution)/shard_map/ppermute | solution.py:242
  454.2 11.0 %collective-permute-done.52 = bf16[1024,384]{0,1:T(8,128)(2,1)S(1)} collective-permute-done((bf16[1024,384]{0,1:T(8,128)(2,1)S(1)}, bf16[1024,384]{0,1:T(8,128)(2,1)S(1)}, u32[]{:S(2)}, u32[]{:S(2)}) %collective-permute-start.52) | collective-permute-done | bytes 786464 | tf_op jit(solution)/shard_map/ppermute | solution.py:242
  467.9 24.7 %collective-permute-done.70 = f32[256,512]{0,1:T(8,128)S(1)} collective-permute-done((f32[256,512]{0,1:T(8,128)S(1)}, f32[256,512]{0,1:T(8,128)S(1)}, u32[]{:S(2)}, u32[]{:S(2)}) %collective-permute-start.70) | collective-permute-done | bytes 524320 | tf_op jit(solution)/shard_map/ppermute | solution.py:236
  492.6 3.8 collective-permute-start.55
  498.1 13.1 %collective-permute-start.53 = (f32[256,384]{0,1:T(8,128)S(1)}, f32[256,384]{0,1:T(8,128)S(1)}, u32[]{:S(2)}, u32[]{:S(2)}) collective-permute-start(f32[256,384]{0,1:T(8,128)S(1)} %get-tuple-element.71), channel_id=1, source_target_pairs={{6,0},{0,2},{2,4},{4,6},{7,1},{1,3},{3,5},{5,7},{14,8},{8,10},{10,... | collective-permute-start | bytes 1179656 | tf_op jit(solution)/shard_map/ppermute | solution.py:236
  511.2 26.3 %collective-permute-done.78 = f32[512,256]{1,0:T(8,128)S(1)} collective-permute-done((f32[512,256]{1,0:T(8,128)S(1)}, f32[512,256]{1,0:T(8,128)S(1)}, u32[]{:S(2)}, u32[]{:S(2)}) %collective-permute-start.78) | collective-permute-done | bytes 524320 | tf_op jit(solution)/shard_map/ppermute | solution.py:236
  540.6 7.0 %collective-permute-done.54 = f32[256,384]{0,1:T(8,128)S(1)} collective-permute-done((f32[256,384]{0,1:T(8,128)S(1)}, f32[256,384]{0,1:T(8,128)S(1)}, u32[]{:S(2)}, u32[]{:S(2)}) %collective-permute-start.54) | collective-permute-done | bytes 393248 | tf_op jit(solution)/shard_map/ppermute | solution.py:236
  556.4 5.9 %collective-permute-done.80 = f32[512,256]{1,0:T(8,128)} collective-permute-done((f32[512,256]{1,0:T(8,128)S(1)}, f32[512,256]{1,0:T(8,128)}, u32[]{:S(2)}, u32[]{:S(2)}) %collective-permute-start.80) | collective-permute-done | bytes 524320 | tf_op jit(solution)/shard_map/ppermute | solution.py:242
  562.3 4.2 collective-permute-done.56
  (405 shorter events, 146.2 us)
Async XLA Ops:
  2.2 36.5 %collective-permute-start.2 = (bf16[10,256]{1,0:T(8,128)(2,1)S(1)}, bf16[10,256]{1,0:T(8,128)(2,1)S(1)}, u32[]{:S(2)}, u32[]{:S(2)}) collective-permute-start(bf16[10,256]{1,0:T(8,128)(2,1)S(1)} %concatenate.126), channel_id=1, source_target_pairs={{6,0},{0,2},{2,4},{4,6},{7,1},{1,3},{3,5},{5,7},{14,8},{8,10},{10,... | collective-permute-start | bytes 15368 | tf_op jit(solution)/shard_map/ppermute | solution.py:236
  5.3 17.9 %collective-permute-start.1 = (bf16[10,256]{1,0:T(8,128)(2,1)S(1)}, bf16[10,256]{1,0:T(8,128)(2,1)S(1)}, u32[]{:S(2)}, u32[]{:S(2)}) collective-permute-start(bf16[10,256]{1,0:T(8,128)(2,1)S(1)} %concatenate.126), channel_id=1, source_target_pairs={{4,0},{6,2},{0,4},{2,6},{5,1},{7,3},{1,5},{3,7},{12,8},{14,10},{8,... | collective-permute-start | bytes 15368 | tf_op jit(solution)/shard_map/ppermute | solution.py:236
  20.8 16.2 %collective-permute-start.4 = (bf16[256,384]{0,1:T(8,128)(2,1)S(1)}, bf16[256,384]{0,1:T(8,128)(2,1)S(1)}, u32[]{:S(2)}, u32[]{:S(2)}) collective-permute-start(bf16[256,384]{0,1:T(8,128)(2,1)S(1)} %bitcast.231), channel_id=1, source_target_pairs={{4,0},{6,2},{0,4},{2,6},{5,1},{7,3},{1,5},{3,7},{12,8},{14,10},{8,... | collective-permute-start | bytes 589832 | tf_op jit(solution)/shard_map/ppermute | solution.py:236
  21.3 15.8 %collective-permute-start.5 = (bf16[256,384]{0,1:T(8,128)(2,1)S(1)}, bf16[256,384]{0,1:T(8,128)(2,1)S(1)}, u32[]{:S(2)}, u32[]{:S(2)}) collective-permute-start(bf16[256,384]{0,1:T(8,128)(2,1)S(1)} %bitcast.232), channel_id=1, source_target_pairs={{6,0},{0,2},{2,4},{4,6},{7,1},{1,3},{3,5},{5,7},{14,8},{8,10},{10,... | collective-permute-start | bytes 589832 | tf_op jit(solution)/shard_map/ppermute | solution.py:236
  37.1 17.2 %collective-permute-start.6 = (bf16[1024,384]{0,1:T(8,128)(2,1)S(1)}, bf16[1024,384]{0,1:T(8,128)(2,1)}, u32[]{:S(2)}, u32[]{:S(2)}) collective-permute-start(bf16[1024,384]{0,1:T(8,128)(2,1)S(1)} %pad_maximum_fusion.9), channel_id=1, source_target_pairs={{16,0},{24,8},{0,16},{8,24},{17,1},{25,9},{1,17},{9,25},{18,2},{26... | collective-permute-start | bytes 2359304 | tf_op jit(solution)/shard_map/ppermute | solution.py:242
  39.0 51.1 %collective-permute-start.7 = (bf16[1024,384]{0,1:T(8,128)(2,1)S(1)}, bf16[1024,384]{0,1:T(8,128)(2,1)S(1)}, u32[]{:S(2)}, u32[]{:S(2)}) collective-permute-start(bf16[1024,384]{0,1:T(8,128)(2,1)S(1)} %pad_maximum_fusion.9), channel_id=1, source_target_pairs={{0,8},{8,0},{16,24},{24,16},{1,9},{9,1},{17,25},{25,17},{2,10},{10... | collective-permute-start | bytes 2359304 | tf_op jit(solution)/shard_map/ppermute | solution.py:250
  54.3 37.3 %collective-permute-start.8 = (bf16[1024,384]{0,1:T(8,128)(2,1)}, bf16[1024,384]{0,1:T(8,128)(2,1)S(1)}, u32[]{:S(2)}, u32[]{:S(2)}) collective-permute-start(bf16[1024,384]{0,1:T(8,128)(2,1)} %collective-permute-done.6), channel_id=1, source_target_pairs={{0,8},{8,0},{16,24},{24,16},{1,9},{9,1},{17,25},{25,17},{2,10},{10... | collective-permute-start | bytes 2359304 | tf_op jit(solution)/shard_map/ppermute | solution.py:250
  54.9 40.0 %collective-permute-start.25 = (bf16[256,512]{1,0:T(8,128)(2,1)S(1)}, bf16[256,512]{1,0:T(8,128)(2,1)S(1)}, u32[]{:S(2)}, u32[]{:S(2)}) collective-permute-start(bf16[256,512]{1,0:T(8,128)(2,1)S(1)} %dynamic-slice_bitcast_fusion.13), channel_id=1, source_target_pairs={{2,0},{4,2},{6,4},{0,6},{3,1},{5,3},{7,5},{1,7},{10,8},{12,10},{14... | collective-permute-start | bytes 786440 | tf_op jit(solution)/shard_map/ppermute | solution.py:236
  56.5 41.6 %collective-permute-start.26 = (bf16[256,512]{1,0:T(8,128)(2,1)S(1)}, bf16[256,512]{1,0:T(8,128)(2,1)S(1)}, u32[]{:S(2)}, u32[]{:S(2)}) collective-permute-start(bf16[256,512]{1,0:T(8,128)(2,1)S(1)} %dynamic-slice_bitcast_fusion.13), channel_id=1, source_target_pairs={{4,0},{6,2},{0,4},{2,6},{5,1},{7,3},{1,5},{3,7},{12,8},{14,10},{8,... | collective-permute-start | bytes 786440 | tf_op jit(solution)/shard_map/ppermute | solution.py:236
  95.0 19.7 %collective-permute-start.13 = (bf16[352,384]{1,0:T(8,128)(2,1)S(1)}, bf16[352,384]{1,0:T(8,128)(2,1)S(1)}, u32[]{:S(2)}, u32[]{:S(2)}) collective-permute-start(bf16[352,384]{1,0:T(8,128)(2,1)S(1)} %get-tuple-element.79), channel_id=1, source_target_pairs={{4,0},{6,2},{0,4},{2,6},{5,1},{7,3},{1,5},{3,7},{12,8},{14,10},{8,... | collective-permute-start | bytes 811016 | tf_op jit(solution)/shard_map/ppermute | solution.py:236
  98.1 16.5 %collective-permute-start.12 = (bf16[352,384]{1,0:T(8,128)(2,1)S(1)}, bf16[352,384]{1,0:T(8,128)(2,1)S(1)}, u32[]{:S(2)}, u32[]{:S(2)}) collective-permute-start(bf16[352,384]{1,0:T(8,128)(2,1)S(1)} %get-tuple-element.80), channel_id=1, source_target_pairs={{2,0},{4,2},{6,4},{0,6},{3,1},{5,3},{7,5},{1,7},{10,8},{12,10},{14... | collective-permute-start | bytes 811016 | tf_op jit(solution)/shard_map/ppermute | solution.py:236
  100.7 51.7 %collective-permute-start.22 = (bf16[128,1024]{1,0:T(8,128)(2,1)}, bf16[128,1024]{1,0:T(8,128)(2,1)}, u32[]{:S(2)}, u32[]{:S(2)}) collective-permute-start(bf16[128,1024]{1,0:T(8,128)(2,1)} %constant_dynamic-update-slice_fusion.1), channel_id=1, source_target_pairs={{0,8},{8,0},{16,24},{24,16},{1,9},{9,1},{17,25},{25,17},{2,10},{10... | collective-permute-start | bytes 786440 | tf_op jit(solution)/shard_map/ppermute | solution.py:250
  101.5 74.0 %collective-permute-start.28 = (bf16[1024,512]{1,0:T(8,128)(2,1)}, bf16[1024,512]{1,0:T(8,128)(2,1)}, u32[]{:S(2)}, u32[]{:S(2)}) collective-permute-start(bf16[1024,512]{1,0:T(8,128)(2,1)} %constant_dynamic-update-slice_fusion.5), channel_id=1, source_target_pairs={{16,0},{24,8},{0,16},{8,24},{17,1},{25,9},{1,17},{9,25},{18,2},{26... | collective-permute-start | bytes 3145736 | tf_op jit(solution)/shard_map/ppermute | solution.py:242
  106.1 47.8 %collective-permute-start.23 = (bf16[128,1024]{1,0:T(8,128)(2,1)}, bf16[128,1024]{1,0:T(8,128)(2,1)S(1)}, u32[]{:S(2)}, u32[]{:S(2)}) collective-permute-start(bf16[128,1024]{1,0:T(8,128)(2,1)} %collective-permute-done.21), channel_id=1, source_target_pairs={{0,8},{8,0},{16,24},{24,16},{1,9},{9,1},{17,25},{25,17},{2,10},{10... | collective-permute-start | bytes 786440 | tf_op jit(solution)/shard_map/ppermute | solution.py:250
  150.7 21.6 %collective-permute-start.32 = (bf16[512,256]{1,0:T(8,128)(2,1)S(1)}, bf16[512,256]{1,0:T(8,128)(2,1)S(1)}, u32[]{:S(2)}, u32[]{:S(2)}) collective-permute-start(bf16[512,256]{1,0:T(8,128)(2,1)S(1)} %dynamic-slice_bitcast_fusion.12), channel_id=1, source_target_pairs={{4,0},{6,2},{0,4},{2,6},{5,1},{7,3},{1,5},{3,7},{12,8},{14,10},{8,... | collective-permute-start | bytes 786440 | tf_op jit(solution)/shard_map/ppermute | solution.py:236
  152.4 20.6 %collective-permute-start.33 = (bf16[512,256]{1,0:T(8,128)(2,1)S(1)}, bf16[512,256]{1,0:T(8,128)(2,1)S(1)}, u32[]{:S(2)}, u32[]{:S(2)}) collective-permute-start(bf16[512,256]{1,0:T(8,128)(2,1)S(1)} %dynamic-slice_bitcast_fusion.12), channel_id=1, source_target_pairs={{6,0},{0,2},{2,4},{4,6},{7,1},{1,3},{3,5},{5,7},{14,8},{8,10},{10,... | collective-permute-start | bytes 786440 | tf_op jit(solution)/shard_map/ppermute | solution.py:236
  156.4 40.9 %collective-permute-start.24 = (f32[352,1024]{1,0:T(8,128)S(1)}, f32[352,1024]{1,0:T(8,128)}, u32[]{:S(2)}, u32[]{:S(2)}) collective-permute-start(f32[352,1024]{1,0:T(8,128)S(1)} %fusion.57), channel_id=1, source_target_pairs={{0,1},{1,0},{2,3},{3,2},{4,5},{5,4},{6,7},{7,6},{8,9},{9,8},{10,11... | collective-permute-start | bytes 4325384 | tf_op jit(solution)/shard_map/ppermute | solution.py:282
  173.7 23.6 %collective-permute-start.34 = (bf16[512,1024]{1,0:T(8,128)(2,1)}, bf16[512,1024]{1,0:T(8,128)(2,1)}, u32[]{:S(2)}, u32[]{:S(2)}) collective-permute-start(bf16[512,1024]{1,0:T(8,128)(2,1)} %constant_dynamic-update-slice_fusion.9), channel_id=1, source_target_pairs={{16,0},{24,8},{0,16},{8,24},{17,1},{25,9},{1,17},{9,25},{18,2},{26... | collective-permute-start | bytes 3145736 | tf_op jit(solution)/shard_map/ppermute | solution.py:242
  175.4 24.4 %collective-permute-start.29 = (bf16[1024,512]{1,0:T(8,128)(2,1)}, bf16[1024,512]{1,0:T(8,128)(2,1)S(1)}, u32[]{:S(2)}, u32[]{:S(2)}) collective-permute-start(bf16[1024,512]{1,0:T(8,128)(2,1)} %constant_dynamic-update-slice_fusion.5), channel_id=1, source_target_pairs={{0,8},{8,0},{16,24},{24,16},{1,9},{9,1},{17,25},{25,17},{2,10},{10... | collective-permute-start | bytes 3145736 | tf_op jit(solution)/shard_map/ppermute | solution.py:250
  175.5 24.3 %collective-permute-start.30 = (bf16[1024,512]{1,0:T(8,128)(2,1)}, bf16[1024,512]{1,0:T(8,128)(2,1)S(1)}, u32[]{:S(2)}, u32[]{:S(2)}) collective-permute-start(bf16[1024,512]{1,0:T(8,128)(2,1)} %collective-permute-done.28), channel_id=1, source_target_pairs={{0,8},{8,0},{16,24},{24,16},{1,9},{9,1},{17,25},{25,17},{2,10},{10... | collective-permute-start | bytes 3145736 | tf_op jit(solution)/shard_map/ppermute | solution.py:250
  175.9 27.3 %collective-permute-start.35 = (bf16[512,1024]{1,0:T(8,128)(2,1)}, bf16[512,1024]{1,0:T(8,128)(2,1)S(1)}, u32[]{:S(2)}, u32[]{:S(2)}) collective-permute-start(bf16[512,1024]{1,0:T(8,128)(2,1)} %constant_dynamic-update-slice_fusion.9), channel_id=1, source_target_pairs={{0,8},{8,0},{16,24},{24,16},{1,9},{9,1},{17,25},{25,17},{2,10},{10... | collective-permute-start | bytes 3145736 | tf_op jit(solution)/shard_map/ppermute | solution.py:250
  207.1 34.1 %collective-permute-start.37 = (f32[352,1024]{1,0:T(8,128)S(1)}, f32[352,1024]{1,0:T(8,128)S(1)}, u32[]{:S(2)}, u32[]{:S(2)}) collective-permute-start(f32[352,1024]{1,0:T(8,128)S(1)} %fusion.39), channel_id=1, source_target_pairs={{0,1},{1,0},{2,3},{3,2},{4,5},{5,4},{6,7},{7,6},{8,9},{9,8},{10,11... | collective-permute-start | bytes 4325384 | tf_op jit(solution)/shard_map/ppermute | solution.py:282
  254.9 33.4 %collective-permute-start.38 = (f32[352,1024]{1,0:T(8,128)}, f32[352,1024]{1,0:T(8,128)}, u32[]{:S(2)}, u32[]{:S(2)}) collective-permute-start(f32[352,1024]{1,0:T(8,128)} %fusion.40), channel_id=1, source_target_pairs={{0,1},{1,0},{2,3},{3,2},{4,5},{5,4},{6,7},{7,6},{8,9},{9,8},{10,11... | collective-permute-start | bytes 4325384 | tf_op jit(solution)/shard_map/ppermute | solution.py:282
  302.4 97.9 %collective-permute-start.67 = (f32[1024,1024]{0,1:T(8,128)}, f32[1024,1024]{0,1:T(8,128)}, u32[]{:S(2)}, u32[]{:S(2)}) collective-permute-start(f32[1024,1024]{0,1:T(8,128)} %fusion.36), channel_id=1, source_target_pairs={{0,8},{8,0},{16,24},{24,16},{1,9},{9,1},{17,25},{25,17},{2,10},{10... | collective-permute-start | bytes 12582920 | tf_op jit(solution)/shard_map/ppermute | solution.py:250
  328.2 22.1 %collective-permute-start.59 = (f32[256,1024]{1,0:T(8,128)S(1)}, f32[256,1024]{1,0:T(8,128)S(1)}, u32[]{:S(2)}, u32[]{:S(2)}) collective-permute-start(f32[256,1024]{1,0:T(8,128)S(1)} %fusion.68), channel_id=1, source_target_pairs={{0,8},{8,0},{16,24},{24,16},{1,9},{9,1},{17,25},{25,17},{2,10},{10... | collective-permute-start | bytes 3145736 | tf_op jit(solution)/shard_map/ppermute | solution.py:250
  328.3 21.4 %collective-permute-start.43 = (bf16[352,384]{1,0:T(8,128)(2,1)S(1)}, bf16[352,384]{1,0:T(8,128)(2,1)S(1)}, u32[]{:S(2)}, u32[]{:S(2)}) collective-permute-start(bf16[352,384]{1,0:T(8,128)(2,1)S(1)} %get-tuple-element.75), channel_id=1, source_target_pairs={{4,0},{6,2},{0,4},{2,6},{5,1},{7,3},{1,5},{3,7},{12,8},{14,10},{8,... | collective-permute-start | bytes 811016 | tf_op jit(solution)/shard_map/ppermute | solution.py:236
  328.4 21.3 %collective-permute-start.44 = (bf16[352,384]{1,0:T(8,128)(2,1)S(1)}, bf16[352,384]{1,0:T(8,128)(2,1)S(1)}, u32[]{:S(2)}, u32[]{:S(2)}) collective-permute-start(bf16[352,384]{1,0:T(8,128)(2,1)S(1)} %get-tuple-element.74), channel_id=1, source_target_pairs={{6,0},{0,2},{2,4},{4,6},{7,1},{1,3},{3,5},{5,7},{14,8},{8,10},{10,... | collective-permute-start | bytes 811016 | tf_op jit(solution)/shard_map/ppermute | solution.py:236
  355.8 32.2 %collective-permute-start.45 = (f32[352,1024]{1,0:T(8,128)S(1)}, f32[352,1024]{1,0:T(8,128)S(1)}, u32[]{:S(2)}, u32[]{:S(2)}) collective-permute-start(f32[352,1024]{1,0:T(8,128)S(1)} %fusion.22), channel_id=1, source_target_pairs={{0,1},{1,0},{2,3},{3,2},{4,5},{5,4},{6,7},{7,6},{8,9},{9,8},{10,11... | collective-permute-start | bytes 4325384 | tf_op jit(solution)/shard_map/ppermute | solution.py:282
  364.7 40.4 %collective-permute-start.75 = (f32[1024,1024]{1,0:T(8,128)}, f32[1024,1024]{1,0:T(8,128)}, u32[]{:S(2)}, u32[]{:S(2)}) collective-permute-start(f32[1024,1024]{1,0:T(8,128)} %fusion.33), channel_id=1, source_target_pairs={{0,8},{8,0},{16,24},{24,16},{1,9},{9,1},{17,25},{25,17},{2,10},{10... | collective-permute-start | bytes 12582920 | tf_op jit(solution)/shard_map/ppermute | solution.py:250
  380.1 30.1 %collective-permute-start.51 = (f32[1024,768]{0,1:T(8,128)}, f32[1024,768]{0,1:T(8,128)}, u32[]{:S(2)}, u32[]{:S(2)}) collective-permute-start(f32[1024,768]{0,1:T(8,128)} %fusion.47), channel_id=1, source_target_pairs={{0,8},{8,0},{16,24},{24,16},{1,9},{9,1},{17,25},{25,17},{2,10},{10... | collective-permute-start | bytes 9437192 | tf_op jit(solution)/shard_map/ppermute | solution.py:250
  404.4 26.1 %collective-permute-start.68 = (bf16[1024,512]{0,1:T(8,128)(2,1)S(1)}, bf16[1024,512]{0,1:T(8,128)(2,1)S(1)}, u32[]{:S(2)}, u32[]{:S(2)}) collective-permute-start(bf16[1024,512]{0,1:T(8,128)(2,1)S(1)} %slice.515), channel_id=1, source_target_pairs={{16,0},{24,8},{0,16},{8,24},{17,1},{25,9},{1,17},{9,25},{18,2},{26... | collective-permute-start | bytes 3145736 | tf_op jit(solution)/shard_map/ppermute | solution.py:242
  409.3 43.7 %collective-permute-start.76 = (bf16[512,1024]{1,0:T(8,128)(2,1)S(1)}, bf16[512,1024]{1,0:T(8,128)(2,1)S(1)}, u32[]{:S(2)}, u32[]{:S(2)}) collective-permute-start(bf16[512,1024]{1,0:T(8,128)(2,1)S(1)} %slice.514), channel_id=1, source_target_pairs={{16,0},{24,8},{0,16},{8,24},{17,1},{25,9},{1,17},{9,25},{18,2},{26... | collective-permute-start | bytes 3145736 | tf_op jit(solution)/shard_map/ppermute | solution.py:242
  413.5 51.7 %collective-permute-start.52 = (bf16[1024,384]{0,1:T(8,128)(2,1)S(1)}, bf16[1024,384]{0,1:T(8,128)(2,1)S(1)}, u32[]{:S(2)}, u32[]{:S(2)}) collective-permute-start(bf16[1024,384]{0,1:T(8,128)(2,1)S(1)} %slice.516), channel_id=1, source_target_pairs={{16,0},{24,8},{0,16},{8,24},{17,1},{25,9},{1,17},{9,25},{18,2},{26... | collective-permute-start | bytes 2359304 | tf_op jit(solution)/shard_map/ppermute | solution.py:242
  431.1 36.1 %collective-permute-start.71 = (f32[256,512]{0,1:T(8,128)S(1)}, f32[256,512]{0,1:T(8,128)S(1)}, u32[]{:S(2)}, u32[]{:S(2)}) collective-permute-start(f32[256,512]{0,1:T(8,128)S(1)} %get-tuple-element.65), channel_id=1, source_target_pairs={{2,0},{4,2},{6,4},{0,6},{3,1},{5,3},{7,5},{1,7},{10,8},{12,10},{14... | collective-permute-start | bytes 1572872 | tf_op jit(solution)/shard_map/ppermute | solution.py:236
  431.7 60.9 %collective-permute-start.70 = (f32[256,512]{0,1:T(8,128)S(1)}, f32[256,512]{0,1:T(8,128)S(1)}, u32[]{:S(2)}, u32[]{:S(2)}) collective-permute-start(f32[256,512]{0,1:T(8,128)S(1)} %get-tuple-element.66), channel_id=1, source_target_pairs={{4,0},{6,2},{0,4},{2,6},{5,1},{7,3},{1,5},{3,7},{12,8},{14,10},{8,... | collective-permute-start | bytes 1572872 | tf_op jit(solution)/shard_map/ppermute | solution.py:236
  432.3 60.3 %collective-permute-start.69 = (f32[256,512]{0,1:T(8,128)S(1)}, f32[256,512]{0,1:T(8,128)S(1)}, u32[]{:S(2)}, u32[]{:S(2)}) collective-permute-start(f32[256,512]{0,1:T(8,128)S(1)} %get-tuple-element.64), channel_id=1, source_target_pairs={{6,0},{0,2},{2,4},{4,6},{7,1},{1,3},{3,5},{5,7},{14,8},{8,10},{10,... | collective-permute-start | bytes 1572872 | tf_op jit(solution)/shard_map/ppermute | solution.py:236
  453.5 44.6 %collective-permute-start.79 = (f32[512,256]{1,0:T(8,128)S(1)}, f32[512,256]{1,0:T(8,128)S(1)}, u32[]{:S(2)}, u32[]{:S(2)}) collective-permute-start(f32[512,256]{1,0:T(8,128)S(1)} %get-tuple-element.58), channel_id=1, source_target_pairs={{2,0},{4,2},{6,4},{0,6},{3,1},{5,3},{7,5},{1,7},{10,8},{12,10},{14... | collective-permute-start | bytes 1572872 | tf_op jit(solution)/shard_map/ppermute | solution.py:236
  465.2 72.3 %collective-permute-start.78 = (f32[512,256]{1,0:T(8,128)S(1)}, f32[512,256]{1,0:T(8,128)S(1)}, u32[]{:S(2)}, u32[]{:S(2)}) collective-permute-start(f32[512,256]{1,0:T(8,128)S(1)} %get-tuple-element.59), channel_id=1, source_target_pairs={{4,0},{6,2},{0,4},{2,6},{5,1},{7,3},{1,5},{3,7},{12,8},{14,10},{8,... | collective-permute-start | bytes 1572872 | tf_op jit(solution)/shard_map/ppermute | solution.py:236
  467.1 29.5 %collective-permute-start.49 = (f32[88,128]{1,0:T(8,128)S(1)}, f32[88,128]{1,0:T(8,128)S(1)}, u32[]{:S(2)}, u32[]{:S(2)}) collective-permute-start(f32[88,128]{1,0:T(8,128)S(1)} %dynamic-slice_reduce_fusion), channel_id=1, source_target_pairs={{16,0},{24,8},{0,16},{8,24},{17,1},{25,9},{1,17},{9,25},{18,2},{26... | collective-permute-start | bytes 135176 | tf_op jit(solution)/shard_map/ppermute | solution.py:242
  492.6 47.1 %collective-permute-start.77 = (f32[512,256]{1,0:T(8,128)S(1)}, f32[512,256]{1,0:T(8,128)S(1)}, u32[]{:S(2)}, u32[]{:S(2)}) collective-permute-start(f32[512,256]{1,0:T(8,128)S(1)} %get-tuple-element.57), channel_id=1, source_target_pairs={{6,0},{0,2},{2,4},{4,6},{7,1},{1,3},{3,5},{5,7},{14,8},{8,10},{10,... | collective-permute-start | bytes 1572872 | tf_op jit(solution)/shard_map/ppermute | solution.py:236
  492.6 47.4 %collective-permute-start.55 = (f32[256,384]{0,1:T(8,128)S(1)}, f32[256,384]{0,1:T(8,128)S(1)}, u32[]{:S(2)}, u32[]{:S(2)}) collective-permute-start(f32[256,384]{0,1:T(8,128)S(1)} %get-tuple-element.72), channel_id=1, source_target_pairs={{2,0},{4,2},{6,4},{0,6},{3,1},{5,3},{7,5},{1,7},{10,8},{12,10},{14... | collective-permute-start | bytes 1179656 | tf_op jit(solution)/shard_map/ppermute | solution.py:236
  496.6 50.9 %collective-permute-start.54 = (f32[256,384]{0,1:T(8,128)S(1)}, f32[256,384]{0,1:T(8,128)S(1)}, u32[]{:S(2)}, u32[]{:S(2)}) collective-permute-start(f32[256,384]{0,1:T(8,128)S(1)} %get-tuple-element.73), channel_id=1, source_target_pairs={{4,0},{6,2},{0,4},{2,6},{5,1},{7,3},{1,5},{3,7},{12,8},{14,10},{8,... | collective-permute-start | bytes 1179656 | tf_op jit(solution)/shard_map/ppermute | solution.py:236
  498.1 52.1 %collective-permute-start.53 = (f32[256,384]{0,1:T(8,128)S(1)}, f32[256,384]{0,1:T(8,128)S(1)}, u32[]{:S(2)}, u32[]{:S(2)}) collective-permute-start(f32[256,384]{0,1:T(8,128)S(1)} %get-tuple-element.71), channel_id=1, source_target_pairs={{6,0},{0,2},{2,4},{4,6},{7,1},{1,3},{3,5},{5,7},{14,8},{8,10},{10,... | collective-permute-start | bytes 1179656 | tf_op jit(solution)/shard_map/ppermute | solution.py:236
  540.0 16.1 %collective-permute-start.73 = (f32[256,512]{0,1:T(8,128)S(1)}, f32[256,512]{0,1:T(8,128)S(1)}, u32[]{:S(2)}, u32[]{:S(2)}) collective-permute-start(f32[256,512]{0,1:T(8,128)S(1)} %fusion.54), channel_id=1, source_target_pairs={{0,8},{8,0},{16,24},{24,16},{1,9},{9,1},{17,25},{25,17},{2,10},{10... | collective-permute-start | bytes 1572872 | tf_op jit(solution)/shard_map/ppermute | solution.py:250
  547.6 14.7 %collective-permute-start.80 = (f32[512,256]{1,0:T(8,128)S(1)}, f32[512,256]{1,0:T(8,128)}, u32[]{:S(2)}, u32[]{:S(2)}) collective-permute-start(f32[512,256]{1,0:T(8,128)S(1)} %fusion.52), channel_id=1, source_target_pairs={{16,0},{24,8},{0,16},{8,24},{17,1},{25,9},{1,17},{9,25},{18,2},{26... | collective-permute-start | bytes 1572872 | tf_op jit(solution)/shard_map/ppermute | solution.py:242
  550.2 16.3 %collective-permute-start.74 = (f32[256,512]{0,1:T(8,128)S(1)}, f32[256,512]{0,1:T(8,128)S(1)}, u32[]{:S(2)}, u32[]{:S(2)}) collective-permute-start(f32[256,512]{0,1:T(8,128)S(1)} %collective-permute-done.72), channel_id=1, source_target_pairs={{0,8},{8,0},{16,24},{24,16},{1,9},{9,1},{17,25},{25,17},{2,10},{10... | collective-permute-start | bytes 1572872 | tf_op jit(solution)/shard_map/ppermute | solution.py:250
  550.3 16.2 %collective-permute-start.56 = (f32[256,384]{0,1:T(8,128)S(1)}, f32[256,384]{0,1:T(8,128)}, u32[]{:S(2)}, u32[]{:S(2)}) collective-permute-start(f32[256,384]{0,1:T(8,128)S(1)} %fusion.56), channel_id=1, source_target_pairs={{16,0},{24,8},{0,16},{8,24},{17,1},{25,9},{1,17},{9,25},{18,2},{26... | collective-permute-start | bytes 1179656 | tf_op jit(solution)/shard_map/ppermute | solution.py:242
  556.1 16.2 %collective-permute-start.57 = (f32[256,384]{0,1:T(8,128)S(1)}, f32[256,384]{0,1:T(8,128)}, u32[]{:S(2)}, u32[]{:S(2)}) collective-permute-start(f32[256,384]{0,1:T(8,128)S(1)} %fusion.56), channel_id=1, source_target_pairs={{0,8},{8,0},{16,24},{24,16},{1,9},{9,1},{17,25},{25,17},{2,10},{10... | collective-permute-start | bytes 1179656 | tf_op jit(solution)/shard_map/ppermute | solution.py:250
  (78 other events, 1017.9 us)

commit v2 on v1

--- a/solution.py
+++ b/solution.py
@@ -6,6 +6,7 @@
 from jax.experimental import pallas as pl
 from jax.experimental.pallas import tpu as pltpu
 from jax.sharding import PartitionSpec as P
+
 
 HD = 64
 QB = 128
@@ -231,6 +232,7 @@
     z = lax.axis_index("fsdp")
     rep = lax.axis_index("rep")
     y, core = rep // 2, rep % 2
+    first_tp = lax.axis_index("tp") == 0
 
     def z_pull(x, s):
         return lax.ppermute(x, "fsdp", [((j + s) % n, j) for j in range(n)])
@@ -277,16 +279,19 @@
             jnp.concatenate([x, x], axis=axis), ((n - z) % n) * block, x.shape[axis], axis
         )
 
-    def sum_tp(x):
-        mine = x
-        return mine + lax.ppermute(mine, "tp", [(0, 1), (1, 0)])
+    def tp_swap(x):
+        return lax.ppermute(x, "tp", [(0, 1), (1, 0)])
+
+    def both_tp(x, other):
+        return jnp.where(first_tp, x, other), jnp.where(first_tp, other, x)
 
     def exchange_heads(slots):
         stacked = jnp.stack(slots)
-        blocks = [lax.dynamic_index_in_dim(stacked, z, 0, keepdims=False)]
-        for s in range(1, n):
-            out = lax.dynamic_index_in_dim(stacked, (z + n - s) % n, 0, keepdims=False)
-            blocks.append(z_pull(out, s))
+        outs = [
+            lax.dynamic_index_in_dim(stacked, (z + n - s) % n, 0, keepdims=False)
+            for s in range(n)
+        ]
+        blocks = [outs[0]] + [z_pull(outs[s], s) for s in range(1, n)]
         return jnp.concatenate(blocks, axis=0)
 
     def return_heads(x):
@@ -297,37 +302,42 @@
     piece_qkv = lax.dynamic_slice_in_dim(qkv_weight[0], rep * q_cols, q_cols, 2).reshape(
         part, 3 * q_cols
     )
-    piece_out = lax.dynamic_slice_in_dim(out_weight[0], rep * q_cols, q_cols, 0)
-    piece_up = lax.dynamic_slice_in_dim(up_weight[0], rep * unit_cols, unit_cols, 1)
-    piece_down = lax.dynamic_slice_in_dim(down_weight[0], rep * unit_cols, unit_cols, 0)
+    gathered_qkv = gather_z(piece_qkv)
 
     codes = (segment_ids * 2 + valid_keys).astype(F32).astype(BF)
     code_rows = -(-rows // part)
     codes = jnp.pad(codes, (0, code_rows * part - rows)).reshape(code_rows, part)
-    features = jnp.concatenate([norm_gain[0], norm_bias[0], out_bias[0], layer_scale[0], codes])
     units = jnp.concatenate([qv_bias.reshape(2 * local_heads, -1), up_bias[0]])
-
-    gathered_qkv = gather_z(piece_qkv)
-    gathered_features = gather_z(features)
-    gathered_units = gather_z(units)
+    unit_shape = units.shape
+    features = jnp.concatenate(
+        [norm_gain[0], norm_bias[0], out_bias[0], layer_scale[0], codes, units.reshape(-1, part)]
+    )
+    gathered_features = gather_z(after(features, piece_qkv))
+
+    piece_up = jnp.concatenate(
+        [
+            lax.dynamic_slice_in_dim(up_weight[0], rep * unit_cols, unit_cols, 1),
+            lax.dynamic_slice_in_dim(out_weight[0], rep * q_cols, q_cols, 0).T,
+        ],
+        axis=1,
+    )
+    piece_down = lax.dynamic_slice_in_dim(down_weight[0], rep * unit_cols, unit_cols, 0)
     slots_qkv = gather_rep(jnp.concatenate(gathered_qkv, axis=0))
-    w_qkv = jnp.concatenate(slots_qkv, axis=1)
-
-    piece_out = after(piece_out, *gathered_qkv)
-    piece_up = after(piece_up, *gathered_qkv)
-    w_out = jnp.concatenate(gather_rep(jnp.concatenate(gather_z(piece_out), axis=1)), axis=0)
-    w_up = jnp.concatenate(gather_rep(jnp.concatenate(gather_z(piece_up), axis=0)), axis=1)
+    gathered_up = gather_z(piece_up)
 
     small = jnp.concatenate([f[:8] for f in gathered_features], axis=1).astype(F32)
     gains, shifts, biases, scales = small[0:2], small[2:4], small[4:6], small[6:8]
-    all_codes = jnp.concatenate([f[8:].reshape(-1)[:rows] for f in gathered_features])
+    all_codes = jnp.concatenate(
+        [f[8 : 8 + code_rows].reshape(-1)[:rows] for f in gathered_features]
+    )
     all_codes = all_codes.astype(jnp.int32)
     group_seg = all_codes // 2
     key_codes = jnp.where(all_codes % 2 == 1, group_seg, -1)
     group_rows = all_codes.shape[0]
     key_codes = jnp.broadcast_to(key_codes[:, None], (group_rows, QB))
     seg_rows = group_seg.reshape(group_rows // QB, 1, QB)
-    unit_lanes = units.shape[1]
+    unit_lanes = unit_shape[1]
+    gathered_units = [f[8 + code_rows :].reshape(unit_shape) for f in gathered_features]
     units_full = to_plain(jnp.concatenate(gathered_units, axis=1), 1, unit_lanes).astype(F32)
     qv_full = units_full[: 2 * local_heads].reshape(2, local_heads * HD)
     up_full = units_full[2 * local_heads :].reshape(-1)
@@ -335,84 +345,131 @@
     up_slots = jnp.concatenate(
         [lax.dynamic_slice_in_dim(up_full, r * unit_cols, unit_cols, 0) for r in slot_rep]
     )
-    bias_qkv = jnp.concatenate(
-        [jnp.concatenate([b[0], jnp.zeros((q_cols,), F32), b[1]]) for b in qv_slots]
-    )
+    bias_qkv = [jnp.concatenate([b[0], jnp.zeros((q_cols,), F32), b[1]]) for b in qv_slots]
 
     resid = from_own(tokens, 1, part).astype(F32)
     upstream = from_own(cotangent, 1, part).astype(F32)
 
     normed, part_one, inv_one = norm_forward(resid, gains[0], shifts[0])
     first_in = normed.astype(BF)
-    project = (dot(first_in, w_qkv) + bias_qkv).astype(BF)
-    slot_cols = 3 * head_cols
-    x_heads = exchange_heads([project[:, k * slot_cols : (k + 1) * slot_cols] for k in range(n)])
-    piece_down = after(piece_down, x_heads)
-    w_down = jnp.concatenate(gather_rep(jnp.concatenate(gather_z(piece_down), axis=1)), axis=0)
+    project = [(dot(first_in, w) + b).astype(BF) for w, b in zip(slots_qkv, bias_qkv)]
+    x_heads = exchange_heads(project)
+    quarter_up = jnp.concatenate(gathered_up, axis=0)
+    quarter_out = quarter_up[:, unit_cols:]
+    out_halves = both_tp(quarter_out, tp_swap(quarter_out))
+    slots_up = gather_rep(jnp.concatenate([quarter_up[:, :unit_cols], *out_halves], axis=1))
+    gathered_down = gather_z(piece_down)
     mixed, lse = attend_forward(x_heads, key_codes, seg_rows, heads)
-    mixed_slots = to_plain(jnp.stack(return_heads(mixed)), 0, 1)
+    mixed_back = return_heads(mixed)
+    slots_down = gather_rep(jnp.concatenate(gathered_down, axis=1))
+    mixed_slots = to_plain(jnp.stack(mixed_back), 0, 1)
     mixed_flat = jnp.concatenate([mixed_slots[k] for k in range(n)], axis=1)
-    branch_one = sum_tp(dot(mixed_flat, w_out)) + biases[0]
+    mixed_halves = both_tp(mixed_flat, tp_swap(mixed_flat))
+    mixed_full = jnp.concatenate(
+        [m[:, k * q_cols : (k + 1) * q_cols] for k in range(reps) for m in mixed_halves],
+        axis=1,
+    )
+    w_out_full = jnp.concatenate([w[:, unit_cols:] for w in slots_up], axis=1)
+    w_out = jnp.concatenate(
+        [
+            jnp.where(first_tp, w[:, unit_cols : unit_cols + q_cols], w[:, unit_cols + q_cols :])
+            for w in slots_up
+        ],
+        axis=1,
+    )
+    w_up = jnp.concatenate([w[:, :unit_cols] for w in slots_up], axis=1)
+    branch_one = dot_nt(mixed_full, w_out_full) + biases[0]
     resid_one = resid + scales[0] * branch_one
     normed_two, part_two, inv_two = norm_forward(resid_one, gains[1], shifts[1])
     second_in = normed_two.astype(BF)
+    w_down = jnp.concatenate(slots_down, axis=0)
     hidden_pre = dot(second_in, w_up) + up_slots
     hidden_act = gelu_value(hidden_pre).astype(BF)
-    branch_two = sum_tp(dot(hidden_act, w_down)) + biases[1]
-    block_out = to_plain((resid_one + scales[1] * branch_two).astype(BF), 1, part)
-
-    def reduce_grad(lead, tail, slot_axis, z_axis):
+
+    def sum_rep(lead, tail, slot_axis, sent=BF):
         total = lead + core_swap(tail)
         step = total.shape[slot_axis] // ys
         cuts = [lax.slice_in_dim(total, d * step, (d + 1) * step, axis=slot_axis) for d in range(ys)]
         mine = cuts[0]
         for d in range(1, ys):
-            mine = mine + y_push(cuts[d].astype(BF), d).astype(F32)
+            moved = y_push(cuts[d].astype(sent), d)
+            mine = mine + moved.astype(F32)
+        return mine
+
+    def scatter_z(mine, z_axis, sent=F32):
         block = mine.shape[z_axis] // n
         blocks = [lax.slice_in_dim(mine, s * block, (s + 1) * block, axis=z_axis) for s in range(n)]
         result = blocks[0]
         for s in range(1, n):
-            result = result + z_push(blocks[s], s)
+            moved = z_push(blocks[s].astype(sent), s)
+            result = result + moved.astype(F32)
         return gather_rep(result)
 
-    scale_two = jnp.sum(upstream * branch_two, axis=0)
-    bias_two = jnp.sum(upstream * scales[1], axis=0)
     branch_grad = (upstream * scales[1]).astype(BF)
+    d_hidden = dot_nt(branch_grad, w_down) * gelu_slope(hidden_pre)
+    d_hidden_half = d_hidden.astype(BF)
+    partial_second = dot_nt(d_hidden_half, w_up)
+    d_second = partial_second + tp_swap(partial_second)
+
     half = hidden // 2
-    grad_down = reduce_grad(
-        dot_tn(hidden_act[:, :half], branch_grad), dot_tn(hidden_act[:, half:], branch_grad), 0, 1
-    )
-    d_hidden = dot_nt(branch_grad, w_down) * gelu_slope(hidden_pre)
+    down_far = dot_tn(hidden_act[:, half:], branch_grad)
+    up_far = dot_tn(second_in, d_hidden_half[:, half:])
+    down_near = dot_tn(hidden_act[:, :half], branch_grad)
+    up_near = dot_tn(second_in, d_hidden_half[:, :half])
+    own_down = sum_rep(down_near, down_far, 0, F32)
+    own_up = sum_rep(up_near, up_far, 1, F32)
+
+    partial_two = dot(after(hidden_act, partial_second), w_down)
+    other_two = tp_swap(partial_two)
     d_up_bias = jnp.sum(d_hidden, axis=0)
-    d_hidden_half = d_hidden.astype(BF)
-    grad_up = reduce_grad(
-        dot_tn(second_in, d_hidden_half[:, :half]), dot_tn(second_in, d_hidden_half[:, half:]), 1, 0
-    )
-    d_second = sum_tp(dot_nt(d_hidden_half, w_up))
-    d_norm_two, gain_two, shift_two = norm_backward(d_second, part_two, inv_two, gains[1])
+
+    d_norm_two = norm_backward(d_second, part_two, inv_two, gains[1])[0]
     upstream_one = upstream + d_norm_two
-    scale_one = jnp.sum(upstream_one * branch_one, axis=0)
-    bias_one = jnp.sum(upstream_one * scales[0], axis=0)
     branch_grad_one = (upstream_one * scales[0]).astype(BF)
+    d_mixed = dot(branch_grad_one, w_out).astype(BF)
+    g_heads = exchange_heads([d_mixed[:, k * head_cols : (k + 1) * head_cols] for k in range(n)])
     half = mixed_flat.shape[1] // 2
-    grad_out = reduce_grad(
-        dot_tn(mixed_flat[:, :half], branch_grad_one),
-        dot_tn(mixed_flat[:, half:], branch_grad_one),
-        0,
-        1,
-    )
-    d_mixed = dot_nt(branch_grad_one, w_out).astype(BF)
-    g_heads = exchange_heads([d_mixed[:, k * head_cols : (k + 1) * head_cols] for k in range(n)])
-    dx_heads, head_sums = attend_backward(
-        x_heads, mixed, g_heads, lse, key_codes, seg_rows, heads
-    )
-    dx_slots = to_plain(jnp.stack(return_heads(dx_heads)), 0, 1)
+    out_far = dot_tn(mixed_flat[:, half:], branch_grad_one)
+    out_near = dot_tn(mixed_flat[:, :half], branch_grad_one)
+    own_out = sum_rep(out_near, out_far, 0)
+    grad_down = scatter_z(own_down, 1, BF)
+    dx_heads, head_sums = attend_backward(x_heads, mixed, g_heads, lse, key_codes, seg_rows, heads)
+    dx_back = return_heads(dx_heads)
+
+    late = lax.optimization_barrier(
+        (
+            upstream,
+            upstream_one,
+            branch_one,
+            resid_one,
+            partial_two,
+            other_two,
+            d_second,
+            part_two,
+            dx_heads,
+        )
+    )
+    late_up, late_up_one, late_one, late_resid, late_two, late_other, late_second, late_part = late[:8]
+    branch_two = late_two + late_other + biases[1]
+    block_out = to_plain((late_resid + scales[1] * branch_two).astype(BF), 1, part)
+    scale_two = jnp.sum(late_up * branch_two, axis=0)
+    bias_two = jnp.sum(late_up, axis=0) * scales[1]
+    scale_one = jnp.sum(late_up_one * late_one, axis=0)
+    bias_one = jnp.sum(late_up_one, axis=0) * scales[0]
+    gain_two = jnp.sum(late_second * late_part, axis=0)
+    shift_two = jnp.sum(late_second, axis=0)
+
+    grad_up = scatter_z(own_up, 0, BF)
+    grad_out = scatter_z(own_out, 1)
+    dx_slots = to_plain(jnp.stack(dx_back), 0, 1)
     d_project = jnp.concatenate([dx_slots[k] for k in range(n)], axis=1)
     half = d_project.shape[1] // 2
-    grad_qkv = reduce_grad(
-        dot_tn(first_in, d_project[:, :half]), dot_tn(first_in, d_project[:, half:]), 1, 0
-    )
-    d_first = sum_tp(dot_nt(d_project, w_qkv))
+    qkv_far = dot_tn(first_in, d_project[:, half:])
+    qkv_near = dot_tn(first_in, d_project[:, :half])
+    grad_qkv = scatter_z(sum_rep(qkv_near, qkv_far, 1), 0)
+    w_qkv = jnp.concatenate(slots_qkv, axis=1)
+    partial_first = dot_nt(d_project, w_qkv)
+    d_first = partial_first + tp_swap(partial_first)
     d_norm_one, gain_one, shift_one = norm_backward(d_first, part_one, inv_one, gains[0])
     tokens_grad = to_plain(upstream_one + d_norm_one, 1, part)
 

time: 585 us -> 506 us (0.86)
  the two profiles are of different devices: /device:TPU:0 before, /device:TPU:19 now
where the time goes in v2:
time: 506 us; the launch traced here: 498 us
  waiting for transfers between devices  209 us (41%)
  starting transfers between devices  131 us (26%)
  matrix products  56.7 us (11%)
  other arithmetic  36.5 us (7%)
  Pallas kernels  31.6 us (6%)
  local copies, waits for them, and re-layouts  29.5 us (6%)
    ppermute x12, waiting for transfers between devices, y_pull(): lax.ppermute(x, 'rep', [((a + d) % ys * 2 + c, a * 2 + c) for a in range(...  112 us
    ppermute x39, waiting for transfers between devices, z_pull(): return lax.ppermute(x, 'fsdp', [((j + s) % n, j) for j in range(n)])  82.3 us
    ppermute x19, starting transfers between devices, core_swap(): return lax.ppermute(x, 'rep', [(r, r ^ 1) for r in range(reps)])  62.2 us
    ppermute x39, starting transfers between devices, z_pull(): return lax.ppermute(x, 'fsdp', [((j + s) % n, j) for j in range(n)])  55.4 us
    dot_general x8, matrix products, dot_tn(): lax.dot_general(a, b, (((0,), (0,)), ((), ())), preferred_element_type=F32)  23 us
    dot_general x4, matrix products, dot_nt(): lax.dot_general(a, b, (((1,), (1,)), ((), ())), preferred_element_type=F32)  17.7 us
    dot_general x7, matrix products, dot(): return jnp.dot(a, b, preferred_element_type=F32)  16 us
    pallas_call x1, Pallas kernels, attend_backward(): pl.pallas_call(functools.partial(backward_kernel, heads), out_shape=(jax....  15.9 us
  transfers between devices with their start and end apart: 75, of which 28 were waited for; matrix products, arithmetic and copies ran while one was open for 19% of the time, Pallas kernels for 6%

profile of v2, /device:TPU:19, one launch (start us, length us, event | category | flops | bytes accessed | tf_op | source)
XLA Modules:
  0.0 497.7 jit_solution(1822073178730223969)
XLA Ops:
  23.7 3.9 collective-permute-start.25
  27.6 13.7 %collective-permute-done.3 = bf16[256,384]{0,1:T(8,128)(2,1)} collective-permute-done((bf16[256,384]{0,1:T(8,128)(2,1)S(1)}, bf16[256,384]{0,1:T(8,128)(2,1)}, u32[]{:S(2)}, u32[]{:S(2)}) %collective-permute-start.3) | collective-permute-done | bytes 196640 | tf_op jit(solution)/shard_map/ppermute | solution.py:238
  43.8 3.5 collective-permute-done.18
  47.3 12.1 %collective-permute-done.17 = bf16[256,640]{1,0:T(8,128)(2,1)S(1)} collective-permute-done((bf16[256,640]{1,0:T(8,128)(2,1)S(1)}, bf16[256,640]{1,0:T(8,128)(2,1)S(1)}, u32[]{:S(2)}, u32[]{:S(2)}) %collective-permute-start.17) | collective-permute-done | bytes 327712 | tf_op jit(solution)/shard_map/ppermute | solution.py:238
  61.2 5.3 %collective-permute-done.16 = bf16[256,640]{1,0:T(8,128)(2,1)S(1)} collective-permute-done((bf16[256,640]{1,0:T(8,128)(2,1)S(1)}, bf16[256,640]{1,0:T(8,128)(2,1)S(1)}, u32[]{:S(2)}, u32[]{:S(2)}) %collective-permute-start.16) | collective-permute-done | bytes 327712 | tf_op jit(solution)/shard_map/ppermute | solution.py:238
  68.1 3.1 collective-permute-done.25
  72.2 5.6 %collective-permute-done.23 = bf16[512,256]{1,0:T(8,128)(2,1)S(1)} collective-permute-done((bf16[512,256]{1,0:T(8,128)(2,1)S(1)}, bf16[512,256]{1,0:T(8,128)(2,1)S(1)}, u32[]{:S(2)}, u32[]{:S(2)}) %collective-permute-start.23) | collective-permute-done | bytes 262176 | tf_op jit(solution)/shard_map/ppermute | solution.py:238
  92.1 12.8 %collective-permute-done.26 = bf16[512,1024]{1,0:T(8,128)(2,1)} collective-permute-done((bf16[512,1024]{1,0:T(8,128)(2,1)}, bf16[512,1024]{1,0:T(8,128)(2,1)}, u32[]{:S(2)}, u32[]{:S(2)}) %collective-permute-start.26) | collective-permute-done | bytes 1048608 | tf_op jit(solution)/shard_map/ppermute | solution.py:244
  107.4 3.8 collective-permute-done.9
  113.4 15.7 %attend_forward.1 = (bf16[1408,128]{1,0:T(8,128)(2,1)}, f32[11,1,256]{2,1,0:T(1,128)}) custom-call(bf16[1408,384]{1,0:T(8,128)(2,1)} %pad_maximum_fusion.7.x_ref, s32[1408,128]{1,0:T(8,128)} %broadcast_in_dim.18.key_ref, s32[11,1,128]{2,1,0:T(1,128)} %and_select_fusion.seg_ref), custom_call_target="tpu_custom_call" | custom-call | flops 1015021568 | bytes 1441792 | tf_op jit(solution)/shard_map/attend_forward/pallas_call | solution.py:162
  133.3 3.7 collective-permute-done.12
  138.0 3.2 collective-permute-done.13
  141.2 3.3 collective-permute-start.14
  150.0 3.1 collective-permute-start.22
  162.6 10.6 %fusion.124 = (f32[2048]{0:T(1024)S(1)}, bf16[352,2048]{1,0:T(8,128)(2,1)S(1)}) fusion(f32[352,2048]{1,0:T(8,128)S(1)} %get-tuple-element.175, bf16[352,1024]{1,0:T(8,128)(2,1)S(1)} %copy-done.8, bf16[512,1024]{1,0:T(8,128)(2,1)} %collective-permute-done.28, bf16[512,1024]{1,0:T(8,128)(2,1)} %collective-permute-done.27, ...), kind=kOutput, calls=%fused_computation.346 | convolution fusion | flops 1513682944 | bytes 9248768 | tf_op jit(solution)/shard_map/dot_general | solution.py:53
  173.3 2.4 fusion.64
  177.0 10.2 %fusion.111 = f32[352,1024]{1,0:T(8,128)} fusion(bf16[352,2048]{1,0:T(8,128)(2,1)S(1)} %get-tuple-element.28, bf16[512,1024]{1,0:T(8,128)(2,1)} %collective-permute-done.28, bf16[512,1024]{1,0:T(8,128)(2,1)} %collective-permute-done.27, bf16[512,1024]{1,0:T(8,128)(2,1)} %collective-permute-done.26, bf16[512,256]{1,0:T(8,128)(2,1)S(1)} %copy-done.27, ...), kind=kOutput, calls=%fused_computation.341 | convolution fusion | flops 1505755136 | bytes 7077888 | tf_op jit(solution)/shard_map/dot_general | solution.py:49
  187.5 3.4 fusion.58
  190.9 3.0 collective-permute-start.67
  194.0 3.3 fusion.61
  197.3 9.2 %collective-permute-done.29 = f32[352,1024]{1,0:T(8,128)S(1)} collective-permute-done((f32[352,1024]{1,0:T(8,128)S(1)}, f32[352,1024]{1,0:T(8,128)S(1)}, u32[]{:S(2)}, u32[]{:S(2)}) %collective-permute-start.29) | collective-permute-done | bytes 1441824 | tf_op jit(solution)/shard_map/ppermute | solution.py:283
  210.4 2.5 collective-permute-start.33
  218.8 5.7 %collective-permute-start.51 = (f32[256,1024]{1,0:T(8,128)}, f32[256,1024]{1,0:T(8,128)}, u32[]{:S(2)}, u32[]{:S(2)}) collective-permute-start(f32[256,1024]{1,0:T(8,128)} %fusion.81), channel_id=1, source_target_pairs={{0,8},{8,0},{16,24},{24,16},{1,9},{9,1},{17,25},{25,17},{2,10},{10... | collective-permute-start | bytes 3145736 | tf_op jit(solution)/shard_map/ppermute | solution.py:252
  225.3 15.9 %attend_backward.1 = (bf16[1408,384]{1,0:T(8,128)(2,1)}, f32[2,128]{1,0:T(2,128)}) custom-call(bf16[1408,384]{1,0:T(8,128)(2,1)} %pad_maximum_fusion.7.x_ref, bf16[1408,128]{1,0:T(8,128)(2,1)} %get-tuple-element.27.o_ref, bf16[1408,128]{1,0:T(8,128)(2,1)} %pad_maximum_fusion.19.g_ref, f32[11,1,256]{2,1,0:T(1,128)} %get-tuple-element.29.lse_ref, ...), custom_call_target="tpu_custom_call" | custom-call | flops 2537553920 | bytes 3604480 | tf_op jit(solution)/shard_map/attend_backward/pallas_call | solution.py:181
  247.7 4.2 multiply_reduce_fusion
  251.9 16.3 %collective-permute-done.34 = bf16[352,384]{1,0:T(8,128)(2,1)S(1)} collective-permute-done((bf16[352,384]{1,0:T(8,128)(2,1)S(1)}, bf16[352,384]{1,0:T(8,128)(2,1)S(1)}, u32[]{:S(2)}, u32[]{:S(2)}) %collective-permute-start.34) | collective-permute-done | bytes 270368 | tf_op jit(solution)/shard_map/ppermute | solution.py:238
  272.7 2.4 fusion
  275.4 3.5 collective-permute-done.52
  279.1 2.7 collective-permute-start.55
  284.0 9.3 %collective-permute-start.59 = (f32[1024,1024]{0,1:T(8,128)}, f32[1024,1024]{0,1:T(8,128)}, u32[]{:S(2)}, u32[]{:S(2)}) collective-permute-start(f32[1024,1024]{0,1:T(8,128)} %fusion.61), channel_id=1, source_target_pairs={{0,8},{8,0},{16,24},{24,16},{1,9},{9,1},{17,25},{25,17},{2,10},{10... | collective-permute-start | bytes 12582920 | tf_op jit(solution)/shard_map/ppermute | solution.py:252
  295.2 3.2 collective-permute-done.56
  299.3 2.8 fusion.68
  303.0 3.7 collective-permute-done.37
  311.2 3.4 collective-permute-start.39
  316.6 3.2 convolution_add_fusion.3
  321.2 3.5 convolution_add_fusion.1
  326.7 3.5 convolution_add_fusion.2
  331.4 3.9 collective-permute-done.44
  337.2 44.0 %collective-permute-done.41 = f32[88,128]{1,0:T(8,128)S(1)} collective-permute-done((f32[88,128]{1,0:T(8,128)S(1)}, f32[88,128]{1,0:T(8,128)S(1)}, u32[]{:S(2)}, u32[]{:S(2)}) %collective-permute-start.41) | collective-permute-done | bytes 45088 | tf_op jit(solution)/shard_map/ppermute | solution.py:244
  383.1 10.9 %collective-permute-start.42 = (f32[88,128]{1,0:T(8,128)S(1)}, f32[88,128]{1,0:T(8,128)S(1)}, u32[]{:S(2)}, u32[]{:S(2)}) collective-permute-start(f32[88,128]{1,0:T(8,128)S(1)} %fusion.90), channel_id=1, source_target_pairs={{0,8},{8,0},{16,24},{24,16},{1,9},{9,1},{17,25},{25,17},{2,10},{10... | collective-permute-start | bytes 135176 | tf_op jit(solution)/shard_map/ppermute | solution.py:252
  397.7 28.4 %collective-permute-done.60 = f32[1024,512]{0,1:T(8,128)S(1)} collective-permute-done((f32[1024,512]{0,1:T(8,128)S(1)}, f32[1024,512]{0,1:T(8,128)S(1)}, u32[]{:S(2)}, u32[]{:S(2)}) %collective-permute-start.60) | collective-permute-done | bytes 2097184 | tf_op jit(solution)/shard_map/ppermute | solution.py:244
  430.0 6.1 %collective-permute-done.70 = bf16[512,256]{1,0:T(8,128)(2,1)S(1)} collective-permute-done((bf16[512,256]{1,0:T(8,128)(2,1)S(1)}, bf16[512,256]{1,0:T(8,128)(2,1)S(1)}, u32[]{:S(2)}, u32[]{:S(2)}) %collective-permute-start.70) | collective-permute-done | bytes 262176 | tf_op jit(solution)/shard_map/ppermute | solution.py:238
  436.0 2.9 collective-permute-start.62
  439.0 15.6 %collective-permute-start.49 = (f32[256,384]{0,1:T(8,128)S(1)}, f32[256,384]{0,1:T(8,128)S(1)}, u32[]{:S(2)}, u32[]{:S(2)}) collective-permute-start(f32[256,384]{0,1:T(8,128)S(1)} %fusion.77), channel_id=1, source_target_pairs={{0,8},{8,0},{16,24},{24,16},{1,9},{9,1},{17,25},{25,17},{2,10},{10... | collective-permute-start | bytes 1179656 | tf_op jit(solution)/shard_map/ppermute | solution.py:252
  454.6 5.6 %collective-permute-start.50 = (f32[256,384]{0,1:T(8,128)S(1)}, f32[256,384]{0,1:T(8,128)S(1)}, u32[]{:S(2)}, u32[]{:S(2)}) collective-permute-start(f32[256,384]{0,1:T(8,128)S(1)} %collective-permute-done.48), channel_id=1, source_target_pairs={{0,8},{8,0},{16,24},{24,16},{1,9},{9,1},{17,25},{25,17},{2,10},{10... | collective-permute-start | bytes 1179656 | tf_op jit(solution)/shard_map/ppermute | solution.py:252
  466.5 7.3 %collective-permute-done.72 = f32[512,256]{1,0:T(8,128)} collective-permute-done((f32[512,256]{1,0:T(8,128)S(1)}, f32[512,256]{1,0:T(8,128)}, u32[]{:S(2)}, u32[]{:S(2)}) %collective-permute-start.72) | collective-permute-done | bytes 524320 | tf_op jit(solution)/shard_map/ppermute | solution.py:244
  475.8 9.1 %collective-permute-done.64 = f32[256,512]{0,1:T(8,128)S(1)} collective-permute-done((f32[256,512]{0,1:T(8,128)S(1)}, f32[256,512]{0,1:T(8,128)S(1)}, u32[]{:S(2)}, u32[]{:S(2)}) %collective-permute-start.64) | collective-permute-done | bytes 524320 | tf_op jit(solution)/shard_map/ppermute | solution.py:244
  493.0 3.0 maximum_bitcast_fusion.1
  (407 shorter events, 136.9 us)
Async XLA Ops:
  8.1 15.6 %collective-permute-start.4 = (bf16[256,384]{0,1:T(8,128)(2,1)S(1)}, bf16[256,384]{0,1:T(8,128)(2,1)}, u32[]{:S(2)}, u32[]{:S(2)}) collective-permute-start(bf16[256,384]{0,1:T(8,128)(2,1)S(1)} %bitcast.248), channel_id=1, source_target_pairs={{4,0},{6,2},{0,4},{2,6},{5,1},{7,3},{1,5},{3,7},{12,8},{14,10},{8,... | collective-permute-start | bytes 589832 | tf_op jit(solution)/shard_map/ppermute | solution.py:238
  14.8 26.4 %collective-permute-start.3 = (bf16[256,384]{0,1:T(8,128)(2,1)S(1)}, bf16[256,384]{0,1:T(8,128)(2,1)}, u32[]{:S(2)}, u32[]{:S(2)}) collective-permute-start(bf16[256,384]{0,1:T(8,128)(2,1)S(1)} %bitcast.249), channel_id=1, source_target_pairs={{2,0},{4,2},{6,4},{0,6},{3,1},{5,3},{7,5},{1,7},{10,8},{12,10},{14... | collective-permute-start | bytes 589832 | tf_op jit(solution)/shard_map/ppermute | solution.py:238
  16.8 30.5 %collective-permute-start.18 = (bf16[256,640]{1,0:T(8,128)(2,1)S(1)}, bf16[256,640]{1,0:T(8,128)(2,1)S(1)}, u32[]{:S(2)}, u32[]{:S(2)}) collective-permute-start(bf16[256,640]{1,0:T(8,128)(2,1)S(1)} %pad_maximum_fusion.20), channel_id=1, source_target_pairs={{6,0},{0,2},{2,4},{4,6},{7,1},{1,3},{3,5},{5,7},{14,8},{8,10},{10,... | collective-permute-start | bytes 983048 | tf_op jit(solution)/shard_map/ppermute | solution.py:238
  16.9 42.6 %collective-permute-start.17 = (bf16[256,640]{1,0:T(8,128)(2,1)S(1)}, bf16[256,640]{1,0:T(8,128)(2,1)S(1)}, u32[]{:S(2)}, u32[]{:S(2)}) collective-permute-start(bf16[256,640]{1,0:T(8,128)(2,1)S(1)} %pad_maximum_fusion.20), channel_id=1, source_target_pairs={{4,0},{6,2},{0,4},{2,6},{5,1},{7,3},{1,5},{3,7},{12,8},{14,10},{8,... | collective-permute-start | bytes 983048 | tf_op jit(solution)/shard_map/ppermute | solution.py:238
  21.6 44.9 %collective-permute-start.16 = (bf16[256,640]{1,0:T(8,128)(2,1)S(1)}, bf16[256,640]{1,0:T(8,128)(2,1)S(1)}, u32[]{:S(2)}, u32[]{:S(2)}) collective-permute-start(bf16[256,640]{1,0:T(8,128)(2,1)S(1)} %pad_maximum_fusion.20), channel_id=1, source_target_pairs={{2,0},{4,2},{6,4},{0,6},{3,1},{5,3},{7,5},{1,7},{10,8},{12,10},{14... | collective-permute-start | bytes 983048 | tf_op jit(solution)/shard_map/ppermute | solution.py:238
  23.7 47.5 %collective-permute-start.25 = (bf16[512,256]{1,0:T(8,128)(2,1)S(1)}, bf16[512,256]{1,0:T(8,128)(2,1)S(1)}, u32[]{:S(2)}, u32[]{:S(2)}) collective-permute-start(bf16[512,256]{1,0:T(8,128)(2,1)S(1)} %dynamic-slice_bitcast_fusion.12), channel_id=1, source_target_pairs={{6,0},{0,2},{2,4},{4,6},{7,1},{1,3},{3,5},{5,7},{14,8},{8,10},{10,... | collective-permute-start | bytes 786440 | tf_op jit(solution)/shard_map/ppermute | solution.py:238
  42.4 38.9 %collective-permute-start.6 = (bf16[1024,384]{0,1:T(8,128)(2,1)S(1)}, bf16[1024,384]{0,1:T(8,128)(2,1)S(1)}, u32[]{:S(2)}, u32[]{:S(2)}) collective-permute-start(bf16[1024,384]{0,1:T(8,128)(2,1)S(1)} %pad_maximum_fusion.13), channel_id=1, source_target_pairs={{16,0},{24,8},{0,16},{8,24},{17,1},{25,9},{1,17},{9,25},{18,2},{26... | collective-permute-start | bytes 2359304 | tf_op jit(solution)/shard_map/ppermute | solution.py:244
  47.3 24.8 %collective-permute-start.24 = (bf16[512,256]{1,0:T(8,128)(2,1)S(1)}, bf16[512,256]{1,0:T(8,128)(2,1)S(1)}, u32[]{:S(2)}, u32[]{:S(2)}) collective-permute-start(bf16[512,256]{1,0:T(8,128)(2,1)S(1)} %dynamic-slice_bitcast_fusion.12), channel_id=1, source_target_pairs={{4,0},{6,2},{0,4},{2,6},{5,1},{7,3},{1,5},{3,7},{12,8},{14,10},{8,... | collective-permute-start | bytes 786440 | tf_op jit(solution)/shard_map/ppermute | solution.py:238
  59.5 18.3 %collective-permute-start.23 = (bf16[512,256]{1,0:T(8,128)(2,1)S(1)}, bf16[512,256]{1,0:T(8,128)(2,1)S(1)}, u32[]{:S(2)}, u32[]{:S(2)}) collective-permute-start(bf16[512,256]{1,0:T(8,128)(2,1)S(1)} %dynamic-slice_bitcast_fusion.12), channel_id=1, source_target_pairs={{2,0},{4,2},{6,4},{0,6},{3,1},{5,3},{7,5},{1,7},{10,8},{12,10},{14... | collective-permute-start | bytes 786440 | tf_op jit(solution)/shard_map/ppermute | solution.py:238
  66.5 17.4 %collective-permute-start.7 = (bf16[1024,384]{0,1:T(8,128)(2,1)S(1)}, bf16[1024,384]{0,1:T(8,128)(2,1)S(1)}, u32[]{:S(2)}, u32[]{:S(2)}) collective-permute-start(bf16[1024,384]{0,1:T(8,128)(2,1)S(1)} %pad_maximum_fusion.13), channel_id=1, source_target_pairs={{0,8},{8,0},{16,24},{24,16},{1,9},{9,1},{17,25},{25,17},{2,10},{10... | collective-permute-start | bytes 2359304 | tf_op jit(solution)/shard_map/ppermute | solution.py:252
  78.9 83.7 %collective-permute-start.27 = (bf16[512,1024]{1,0:T(8,128)(2,1)}, bf16[512,1024]{1,0:T(8,128)(2,1)}, u32[]{:S(2)}, u32[]{:S(2)}) collective-permute-start(bf16[512,1024]{1,0:T(8,128)(2,1)} %pad_maximum_fusion.12), channel_id=1, source_target_pairs={{0,8},{8,0},{16,24},{24,16},{1,9},{9,1},{17,25},{25,17},{2,10},{10... | collective-permute-start | bytes 3145736 | tf_op jit(solution)/shard_map/ppermute | solution.py:252
  79.9 25.1 %collective-permute-start.26 = (bf16[512,1024]{1,0:T(8,128)(2,1)}, bf16[512,1024]{1,0:T(8,128)(2,1)}, u32[]{:S(2)}, u32[]{:S(2)}) collective-permute-start(bf16[512,1024]{1,0:T(8,128)(2,1)} %pad_maximum_fusion.12), channel_id=1, source_target_pairs={{16,0},{24,8},{0,16},{8,24},{17,1},{25,9},{1,17},{9,25},{18,2},{26... | collective-permute-start | bytes 3145736 | tf_op jit(solution)/shard_map/ppermute | solution.py:244
  86.7 19.2 %collective-permute-start.11 = (bf16[352,384]{1,0:T(8,128)(2,1)S(1)}, bf16[352,384]{1,0:T(8,128)(2,1)S(1)}, u32[]{:S(2)}, u32[]{:S(2)}) collective-permute-start(bf16[352,384]{1,0:T(8,128)(2,1)S(1)} %get-tuple-element.97), channel_id=1, source_target_pairs={{6,0},{0,2},{2,4},{4,6},{7,1},{1,3},{3,5},{5,7},{14,8},{8,10},{10,... | collective-permute-start | bytes 811016 | tf_op jit(solution)/shard_map/ppermute | solution.py:238
  87.8 19.3 %collective-permute-start.10 = (bf16[352,384]{1,0:T(8,128)(2,1)S(1)}, bf16[352,384]{1,0:T(8,128)(2,1)S(1)}, u32[]{:S(2)}, u32[]{:S(2)}) collective-permute-start(bf16[352,384]{1,0:T(8,128)(2,1)S(1)} %get-tuple-element.98), channel_id=1, source_target_pairs={{4,0},{6,2},{0,4},{2,6},{5,1},{7,3},{1,5},{3,7},{12,8},{14,10},{8,... | collective-permute-start | bytes 811016 | tf_op jit(solution)/shard_map/ppermute | solution.py:238
  90.1 21.1 %collective-permute-start.9 = (bf16[352,384]{1,0:T(8,128)(2,1)S(1)}, bf16[352,384]{1,0:T(8,128)(2,1)S(1)}, u32[]{:S(2)}, u32[]{:S(2)}) collective-permute-start(bf16[352,384]{1,0:T(8,128)(2,1)S(1)} %get-tuple-element.99), channel_id=1, source_target_pairs={{2,0},{4,2},{6,4},{0,6},{3,1},{5,3},{7,5},{1,7},{10,8},{12,10},{14... | collective-permute-start | bytes 811016 | tf_op jit(solution)/shard_map/ppermute | solution.py:238
  105.0 42.5 %collective-permute-start.21 = (bf16[1024,768]{1,0:T(8,128)(2,1)}, bf16[1024,768]{1,0:T(8,128)(2,1)}, u32[]{:S(2)}, u32[]{:S(2)}) collective-permute-start(bf16[1024,768]{1,0:T(8,128)(2,1)} %pad_maximum_fusion.4), channel_id=1, source_target_pairs={{0,8},{8,0},{16,24},{24,16},{1,9},{9,1},{17,25},{25,17},{2,10},{10... | collective-permute-start | bytes 4718600 | tf_op jit(solution)/shard_map/ppermute | solution.py:252
  105.9 44.0 %collective-permute-start.20 = (bf16[1024,768]{1,0:T(8,128)(2,1)}, bf16[1024,768]{1,0:T(8,128)(2,1)S(1)}, u32[]{:S(2)}, u32[]{:S(2)}) collective-permute-start(bf16[1024,768]{1,0:T(8,128)(2,1)} %pad_maximum_fusion.4), channel_id=1, source_target_pairs={{16,0},{24,8},{0,16},{8,24},{17,1},{25,9},{1,17},{9,25},{18,2},{26... | collective-permute-start | bytes 4718600 | tf_op jit(solution)/shard_map/ppermute | solution.py:244
  107.1 55.5 %collective-permute-start.28 = (bf16[512,1024]{1,0:T(8,128)(2,1)}, bf16[512,1024]{1,0:T(8,128)(2,1)}, u32[]{:S(2)}, u32[]{:S(2)}) collective-permute-start(bf16[512,1024]{1,0:T(8,128)(2,1)} %collective-permute-done.26), channel_id=1, source_target_pairs={{0,8},{8,0},{16,24},{24,16},{1,9},{9,1},{17,25},{25,17},{2,10},{10... | collective-permute-start | bytes 3145736 | tf_op jit(solution)/shard_map/ppermute | solution.py:252
  175.7 30.8 %collective-permute-start.29 = (f32[352,1024]{1,0:T(8,128)S(1)}, f32[352,1024]{1,0:T(8,128)S(1)}, u32[]{:S(2)}, u32[]{:S(2)}) collective-permute-start(f32[352,1024]{1,0:T(8,128)S(1)} %fusion.64), channel_id=1, source_target_pairs={{0,1},{1,0},{2,3},{3,2},{4,5},{5,4},{6,7},{7,6},{8,9},{9,8},{10,11... | collective-permute-start | bytes 4325384 | tf_op jit(solution)/shard_map/ppermute | solution.py:283
  187.2 56.3 %collective-permute-start.30 = (f32[352,1024]{1,0:T(8,128)}, f32[352,1024]{1,0:T(8,128)}, u32[]{:S(2)}, u32[]{:S(2)}) collective-permute-start(f32[352,1024]{1,0:T(8,128)} %fusion.111), channel_id=1, source_target_pairs={{0,1},{1,0},{2,3},{3,2},{4,5},{5,4},{6,7},{7,6},{8,9},{9,8},{10,11... | collective-permute-start | bytes 4325384 | tf_op jit(solution)/shard_map/ppermute | solution.py:283
  190.9 130.4 %collective-permute-start.67 = (f32[1024,1024]{1,0:T(8,128)}, f32[1024,1024]{1,0:T(8,128)}, u32[]{:S(2)}, u32[]{:S(2)}) collective-permute-start(f32[1024,1024]{1,0:T(8,128)} %fusion.58), channel_id=1, source_target_pairs={{0,8},{8,0},{16,24},{24,16},{1,9},{9,1},{17,25},{25,17},{2,10},{10... | collective-permute-start | bytes 12582920 | tf_op jit(solution)/shard_map/ppermute | solution.py:252
  218.8 51.0 %collective-permute-start.51 = (f32[256,1024]{1,0:T(8,128)}, f32[256,1024]{1,0:T(8,128)}, u32[]{:S(2)}, u32[]{:S(2)}) collective-permute-start(f32[256,1024]{1,0:T(8,128)} %fusion.81), channel_id=1, source_target_pairs={{0,8},{8,0},{16,24},{24,16},{1,9},{9,1},{17,25},{25,17},{2,10},{10... | collective-permute-start | bytes 3145736 | tf_op jit(solution)/shard_map/ppermute | solution.py:252
  243.5 24.9 %collective-permute-start.36 = (bf16[352,384]{1,0:T(8,128)(2,1)S(1)}, bf16[352,384]{1,0:T(8,128)(2,1)S(1)}, u32[]{:S(2)}, u32[]{:S(2)}) collective-permute-start(bf16[352,384]{1,0:T(8,128)(2,1)S(1)} %get-tuple-element.93), channel_id=1, source_target_pairs={{6,0},{0,2},{2,4},{4,6},{7,1},{1,3},{3,5},{5,7},{14,8},{8,10},{10,... | collective-permute-start | bytes 811016 | tf_op jit(solution)/shard_map/ppermute | solution.py:238
  243.5 24.8 %collective-permute-start.35 = (bf16[352,384]{1,0:T(8,128)(2,1)S(1)}, bf16[352,384]{1,0:T(8,128)(2,1)S(1)}, u32[]{:S(2)}, u32[]{:S(2)}) collective-permute-start(bf16[352,384]{1,0:T(8,128)(2,1)S(1)} %get-tuple-element.94), channel_id=1, source_target_pairs={{4,0},{6,2},{0,4},{2,6},{5,1},{7,3},{1,5},{3,7},{12,8},{14,10},{8,... | collective-permute-start | bytes 811016 | tf_op jit(solution)/shard_map/ppermute | solution.py:238
  245.4 22.8 %collective-permute-start.34 = (bf16[352,384]{1,0:T(8,128)(2,1)S(1)}, bf16[352,384]{1,0:T(8,128)(2,1)S(1)}, u32[]{:S(2)}, u32[]{:S(2)}) collective-permute-start(bf16[352,384]{1,0:T(8,128)(2,1)S(1)} %get-tuple-element.95), channel_id=1, source_target_pairs={{2,0},{4,2},{6,4},{0,6},{3,1},{5,3},{7,5},{1,7},{10,8},{12,10},{14... | collective-permute-start | bytes 811016 | tf_op jit(solution)/shard_map/ppermute | solution.py:238
  275.1 31.6 %collective-permute-start.37 = (f32[352,1024]{1,0:T(8,128)S(1)}, f32[352,1024]{1,0:T(8,128)S(1)}, u32[]{:S(2)}, u32[]{:S(2)}) collective-permute-start(f32[352,1024]{1,0:T(8,128)S(1)} %fusion), channel_id=1, source_target_pairs={{0,1},{1,0},{2,3},{3,2},{4,5},{5,4},{6,7},{7,6},{8,9},{9,8},{10,11... | collective-permute-start | bytes 4325384 | tf_op jit(solution)/shard_map/ppermute | solution.py:283
  279.1 14.1 %collective-permute-start.55 = (f32[128,256]{1,0:T(8,128)S(1)}, f32[128,256]{1,0:T(8,128)S(1)}, u32[]{:S(2)}, u32[]{:S(2)}) collective-permute-start(f32[128,256]{1,0:T(8,128)S(1)} %get-tuple-element.117), channel_id=1, source_target_pairs={{2,0},{4,2},{6,4},{0,6},{3,1},{5,3},{7,5},{1,7},{10,8},{12,10},{14... | collective-permute-start | bytes 393224 | tf_op jit(solution)/shard_map/ppermute | solution.py:238
  284.0 42.7 %collective-permute-start.59 = (f32[1024,1024]{0,1:T(8,128)}, f32[1024,1024]{0,1:T(8,128)}, u32[]{:S(2)}, u32[]{:S(2)}) collective-permute-start(f32[1024,1024]{0,1:T(8,128)} %fusion.61), channel_id=1, source_target_pairs={{0,8},{8,0},{16,24},{24,16},{1,9},{9,1},{17,25},{25,17},{2,10},{10... | collective-permute-start | bytes 12582920 | tf_op jit(solution)/shard_map/ppermute | solution.py:252
  302.1 14.5 %collective-permute-start.43 = (f32[1024,768]{0,1:T(8,128)}, f32[1024,768]{0,1:T(8,128)}, u32[]{:S(2)}, u32[]{:S(2)}) collective-permute-start(f32[1024,768]{0,1:T(8,128)} %fusion.68), channel_id=1, source_target_pairs={{0,8},{8,0},{16,24},{24,16},{1,9},{9,1},{17,25},{25,17},{2,10},{10... | collective-permute-start | bytes 9437192 | tf_op jit(solution)/shard_map/ppermute | solution.py:252
  319.9 15.4 %collective-permute-start.44 = (bf16[1024,384]{0,1:T(8,128)(2,1)S(1)}, bf16[1024,384]{0,1:T(8,128)(2,1)S(1)}, u32[]{:S(2)}, u32[]{:S(2)}) collective-permute-start(bf16[1024,384]{0,1:T(8,128)(2,1)S(1)} %slice.650), channel_id=1, source_target_pairs={{16,0},{24,8},{0,16},{8,24},{17,1},{25,9},{1,17},{9,25},{18,2},{26... | collective-permute-start | bytes 2359304 | tf_op jit(solution)/shard_map/ppermute | solution.py:244
  325.0 70.4 %collective-permute-start.68 = (f32[512,1024]{1,0:T(8,128)S(1)}, f32[512,1024]{1,0:T(8,128)S(1)}, u32[]{:S(2)}, u32[]{:S(2)}) collective-permute-start(f32[512,1024]{1,0:T(8,128)S(1)} %slice.572), channel_id=1, source_target_pairs={{16,0},{24,8},{0,16},{8,24},{17,1},{25,9},{1,17},{9,25},{18,2},{26... | collective-permute-start | bytes 6291464 | tf_op jit(solution)/shard_map/ppermute | solution.py:244
  326.0 55.2 %collective-permute-start.41 = (f32[88,128]{1,0:T(8,128)S(1)}, f32[88,128]{1,0:T(8,128)S(1)}, u32[]{:S(2)}, u32[]{:S(2)}) collective-permute-start(f32[88,128]{1,0:T(8,128)S(1)} %dynamic-slice_reduce_fusion), channel_id=1, source_target_pairs={{16,0},{24,8},{0,16},{8,24},{17,1},{25,9},{1,17},{9,25},{18,2},{26... | collective-permute-start | bytes 135176 | tf_op jit(solution)/shard_map/ppermute | solution.py:244
  330.5 95.7 %collective-permute-start.60 = (f32[1024,512]{0,1:T(8,128)S(1)}, f32[1024,512]{0,1:T(8,128)S(1)}, u32[]{:S(2)}, u32[]{:S(2)}) collective-permute-start(f32[1024,512]{0,1:T(8,128)S(1)} %slice.563), channel_id=1, source_target_pairs={{16,0},{24,8},{0,16},{8,24},{17,1},{25,9},{1,17},{9,25},{18,2},{26... | collective-permute-start | bytes 6291464 | tf_op jit(solution)/shard_map/ppermute | solution.py:244
  335.7 47.5 %collective-permute-start.45 = (f32[256,384]{0,1:T(8,128)S(1)}, f32[256,384]{0,1:T(8,128)S(1)}, u32[]{:S(2)}, u32[]{:S(2)}) collective-permute-start(f32[256,384]{0,1:T(8,128)S(1)} %get-tuple-element.90), channel_id=1, source_target_pairs={{6,0},{0,2},{2,4},{4,6},{7,1},{1,3},{3,5},{5,7},{14,8},{8,10},{10,... | collective-permute-start | bytes 1179656 | tf_op jit(solution)/shard_map/ppermute | solution.py:238
  336.0 58.0 %collective-permute-start.47 = (f32[256,384]{0,1:T(8,128)S(1)}, f32[256,384]{0,1:T(8,128)S(1)}, u32[]{:S(2)}, u32[]{:S(2)}) collective-permute-start(f32[256,384]{0,1:T(8,128)S(1)} %get-tuple-element.91), channel_id=1, source_target_pairs={{2,0},{4,2},{6,4},{0,6},{3,1},{5,3},{7,5},{1,7},{10,8},{12,10},{14... | collective-permute-start | bytes 1179656 | tf_op jit(solution)/shard_map/ppermute | solution.py:238
  383.1 80.1 %collective-permute-start.42 = (f32[88,128]{1,0:T(8,128)S(1)}, f32[88,128]{1,0:T(8,128)S(1)}, u32[]{:S(2)}, u32[]{:S(2)}) collective-permute-start(f32[88,128]{1,0:T(8,128)S(1)} %fusion.90), channel_id=1, source_target_pairs={{0,8},{8,0},{16,24},{24,16},{1,9},{9,1},{17,25},{25,17},{2,10},{10... | collective-permute-start | bytes 135176 | tf_op jit(solution)/shard_map/ppermute | solution.py:252
  394.1 44.8 %collective-permute-start.48 = (f32[256,384]{0,1:T(8,128)S(1)}, f32[256,384]{0,1:T(8,128)S(1)}, u32[]{:S(2)}, u32[]{:S(2)}) collective-permute-start(f32[256,384]{0,1:T(8,128)S(1)} %fusion.77), channel_id=1, source_target_pairs={{16,0},{24,8},{0,16},{8,24},{17,1},{25,9},{1,17},{9,25},{18,2},{26... | collective-permute-start | bytes 1179656 | tf_op jit(solution)/shard_map/ppermute | solution.py:244
  396.2 32.0 %collective-permute-start.69 = (bf16[512,256]{1,0:T(8,128)(2,1)S(1)}, bf16[512,256]{1,0:T(8,128)(2,1)S(1)}, u32[]{:S(2)}, u32[]{:S(2)}) collective-permute-start(bf16[512,256]{1,0:T(8,128)(2,1)S(1)} %get-tuple-element.100), channel_id=1, source_target_pairs={{6,0},{0,2},{2,4},{4,6},{7,1},{1,3},{3,5},{5,7},{14,8},{8,10},{10,... | collective-permute-start | bytes 786440 | tf_op jit(solution)/shard_map/ppermute | solution.py:238
  396.3 32.1 %collective-permute-start.71 = (bf16[512,256]{1,0:T(8,128)(2,1)S(1)}, bf16[512,256]{1,0:T(8,128)(2,1)S(1)}, u32[]{:S(2)}, u32[]{:S(2)}) collective-permute-start(bf16[512,256]{1,0:T(8,128)(2,1)S(1)} %get-tuple-element.101), channel_id=1, source_target_pairs={{2,0},{4,2},{6,4},{0,6},{3,1},{5,3},{7,5},{1,7},{10,8},{12,10},{14... | collective-permute-start | bytes 786440 | tf_op jit(solution)/shard_map/ppermute | solution.py:238
  428.3 26.3 %collective-permute-start.61 = (bf16[256,512]{0,1:T(8,128)(2,1)S(1)}, bf16[256,512]{0,1:T(8,128)(2,1)S(1)}, u32[]{:S(2)}, u32[]{:S(2)}) collective-permute-start(bf16[256,512]{0,1:T(8,128)(2,1)S(1)} %get-tuple-element.103), channel_id=1, source_target_pairs={{6,0},{0,2},{2,4},{4,6},{7,1},{1,3},{3,5},{5,7},{14,8},{8,10},{10,... | collective-permute-start | bytes 786440 | tf_op jit(solution)/shard_map/ppermute | solution.py:238
  428.4 31.8 %collective-permute-start.63 = (bf16[256,512]{0,1:T(8,128)(2,1)S(1)}, bf16[256,512]{0,1:T(8,128)(2,1)S(1)}, u32[]{:S(2)}, u32[]{:S(2)}) collective-permute-start(bf16[256,512]{0,1:T(8,128)(2,1)S(1)} %get-tuple-element.104), channel_id=1, source_target_pairs={{2,0},{4,2},{6,4},{0,6},{3,1},{5,3},{7,5},{1,7},{10,8},{12,10},{14... | collective-permute-start | bytes 786440 | tf_op jit(solution)/shard_map/ppermute | solution.py:238
  436.0 25.4 %collective-permute-start.62 = (bf16[256,512]{0,1:T(8,128)(2,1)S(1)}, bf16[256,512]{0,1:T(8,128)(2,1)S(1)}, u32[]{:S(2)}, u32[]{:S(2)}) collective-permute-start(bf16[256,512]{0,1:T(8,128)(2,1)S(1)} %get-tuple-element.105), channel_id=1, source_target_pairs={{4,0},{6,2},{0,4},{2,6},{5,1},{7,3},{1,5},{3,7},{12,8},{14,10},{8,... | collective-permute-start | bytes 786440 | tf_op jit(solution)/shard_map/ppermute | solution.py:238
  439.0 36.7 %collective-permute-start.49 = (f32[256,384]{0,1:T(8,128)S(1)}, f32[256,384]{0,1:T(8,128)S(1)}, u32[]{:S(2)}, u32[]{:S(2)}) collective-permute-start(f32[256,384]{0,1:T(8,128)S(1)} %fusion.77), channel_id=1, source_target_pairs={{0,8},{8,0},{16,24},{24,16},{1,9},{9,1},{17,25},{25,17},{2,10},{10... | collective-permute-start | bytes 1179656 | tf_op jit(solution)/shard_map/ppermute | solution.py:252
  454.6 21.1 %collective-permute-start.50 = (f32[256,384]{0,1:T(8,128)S(1)}, f32[256,384]{0,1:T(8,128)S(1)}, u32[]{:S(2)}, u32[]{:S(2)}) collective-permute-start(f32[256,384]{0,1:T(8,128)S(1)} %collective-permute-done.48), channel_id=1, source_target_pairs={{0,8},{8,0},{16,24},{24,16},{1,9},{9,1},{17,25},{25,17},{2,10},{10... | collective-permute-start | bytes 1179656 | tf_op jit(solution)/shard_map/ppermute | solution.py:252
  461.6 23.4 %collective-permute-start.64 = (f32[256,512]{0,1:T(8,128)S(1)}, f32[256,512]{0,1:T(8,128)S(1)}, u32[]{:S(2)}, u32[]{:S(2)}) collective-permute-start(f32[256,512]{0,1:T(8,128)S(1)} %fusion.75), channel_id=1, source_target_pairs={{16,0},{24,8},{0,16},{8,24},{17,1},{25,9},{1,17},{9,25},{18,2},{26... | collective-permute-start | bytes 1572872 | tf_op jit(solution)/shard_map/ppermute | solution.py:244
  464.9 22.9 %collective-permute-start.73 = (f32[512,256]{1,0:T(8,128)S(1)}, f32[512,256]{1,0:T(8,128)}, u32[]{:S(2)}, u32[]{:S(2)}) collective-permute-start(f32[512,256]{1,0:T(8,128)S(1)} %fusion.73), channel_id=1, source_target_pairs={{0,8},{8,0},{16,24},{24,16},{1,9},{9,1},{17,25},{25,17},{2,10},{10... | collective-permute-start | bytes 1572872 | tf_op jit(solution)/shard_map/ppermute | solution.py:252
  473.8 14.0 %collective-permute-start.74 = (f32[512,256]{1,0:T(8,128)}, f32[512,256]{1,0:T(8,128)}, u32[]{:S(2)}, u32[]{:S(2)}) collective-permute-start(f32[512,256]{1,0:T(8,128)} %collective-permute-done.72), channel_id=1, source_target_pairs={{0,8},{8,0},{16,24},{24,16},{1,9},{9,1},{17,25},{25,17},{2,10},{10... | collective-permute-start | bytes 1572872 | tf_op jit(solution)/shard_map/ppermute | solution.py:252
  475.7 15.0 %collective-permute-start.65 = (f32[256,512]{0,1:T(8,128)S(1)}, f32[256,512]{0,1:T(8,128)}, u32[]{:S(2)}, u32[]{:S(2)}) collective-permute-start(f32[256,512]{0,1:T(8,128)S(1)} %fusion.75), channel_id=1, source_target_pairs={{0,8},{8,0},{16,24},{24,16},{1,9},{9,1},{17,25},{25,17},{2,10},{10... | collective-permute-start | bytes 1572872 | tf_op jit(solution)/shard_map/ppermute | solution.py:252
  (66 other events, 516.1 us)

commit v3 on v2

--- a/solution.py
+++ b/solution.py
@@ -323,7 +323,7 @@
     )
     piece_down = lax.dynamic_slice_in_dim(down_weight[0], rep * unit_cols, unit_cols, 0)
     slots_qkv = gather_rep(jnp.concatenate(gathered_qkv, axis=0))
-    gathered_up = gather_z(piece_up)
+    gathered_up = gather_z(after(piece_up, *gathered_qkv))
 
     small = jnp.concatenate([f[:8] for f in gathered_features], axis=1).astype(F32)
     gains, shifts, biases, scales = small[0:2], small[2:4], small[4:6], small[6:8]
@@ -358,7 +358,7 @@
     quarter_out = quarter_up[:, unit_cols:]
     out_halves = both_tp(quarter_out, tp_swap(quarter_out))
     slots_up = gather_rep(jnp.concatenate([quarter_up[:, :unit_cols], *out_halves], axis=1))
-    gathered_down = gather_z(piece_down)
+    gathered_down = gather_z(after(piece_down, x_heads))
     mixed, lse = attend_forward(x_heads, key_codes, seg_rows, heads)
     mixed_back = return_heads(mixed)
     slots_down = gather_rep(jnp.concatenate(gathered_down, axis=1))
@@ -382,7 +382,6 @@
     resid_one = resid + scales[0] * branch_one
     normed_two, part_two, inv_two = norm_forward(resid_one, gains[1], shifts[1])
     second_in = normed_two.astype(BF)
-    w_down = jnp.concatenate(slots_down, axis=0)
     hidden_pre = dot(second_in, w_up) + up_slots
     hidden_act = gelu_value(hidden_pre).astype(BF)
 
@@ -398,15 +397,23 @@
 
     def scatter_z(mine, z_axis, sent=F32):
         block = mine.shape[z_axis] // n
-        blocks = [lax.slice_in_dim(mine, s * block, (s + 1) * block, axis=z_axis) for s in range(n)]
-        result = blocks[0]
+        wire = mine.astype(sent)
+        result = lax.slice_in_dim(mine, 0, block, axis=z_axis)
         for s in range(1, n):
-            moved = z_push(blocks[s].astype(sent), s)
+            cut = lax.slice_in_dim(wire, s * block, (s + 1) * block, axis=z_axis)
+            moved = z_push(cut, s)
             result = result + moved.astype(F32)
         return gather_rep(result)
 
     branch_grad = (upstream * scales[1]).astype(BF)
-    d_hidden = dot_nt(branch_grad, w_down) * gelu_slope(hidden_pre)
+    d_hidden = jnp.concatenate(
+        [
+            dot_nt(branch_grad, w)
+            * gelu_slope(hidden_pre[:, k * unit_cols : (k + 1) * unit_cols])
+            for k, w in enumerate(slots_down)
+        ],
+        axis=1,
+    )
     d_hidden_half = d_hidden.astype(BF)
     partial_second = dot_nt(d_hidden_half, w_up)
     d_second = partial_second + tp_swap(partial_second)
@@ -419,10 +426,15 @@
     own_down = sum_rep(down_near, down_far, 0, F32)
     own_up = sum_rep(up_near, up_far, 1, F32)
 
-    partial_two = dot(after(hidden_act, partial_second), w_down)
+    late_act = after(hidden_act, partial_second)
+    partial_two = functools.reduce(
+        jnp.add,
+        [
+            dot(late_act[:, k * unit_cols : (k + 1) * unit_cols], w)
+            for k, w in enumerate(slots_down)
+        ],
+    )
     other_two = tp_swap(partial_two)
-    d_up_bias = jnp.sum(d_hidden, axis=0)
-
     d_norm_two = norm_backward(d_second, part_two, inv_two, gains[1])[0]
     upstream_one = upstream + d_norm_two
     branch_grad_one = (upstream_one * scales[0]).astype(BF)
@@ -446,10 +458,12 @@
             other_two,
             d_second,
             part_two,
+            d_hidden,
             dx_heads,
         )
     )
     late_up, late_up_one, late_one, late_resid, late_two, late_other, late_second, late_part = late[:8]
+    late_hidden = late[8]
     branch_two = late_two + late_other + biases[1]
     block_out = to_plain((late_resid + scales[1] * branch_two).astype(BF), 1, part)
     scale_two = jnp.sum(late_up * branch_two, axis=0)
@@ -458,6 +472,7 @@
     bias_one = jnp.sum(late_up_one, axis=0) * scales[0]
     gain_two = jnp.sum(late_second * late_part, axis=0)
     shift_two = jnp.sum(late_second, axis=0)
+    d_up_bias = jnp.sum(late_hidden, axis=0)
 
     grad_up = scatter_z(own_up, 0, BF)
     grad_out = scatter_z(own_out, 1)

time: 506 us -> 569 us (1.12)
  the two profiles are of different devices: /device:TPU:19 before, /device:TPU:0 now
where the time goes in v3:
time: 569 us; the launch traced here: 560 us
  waiting for transfers between devices  318 us (56%)
  starting transfers between devices  81.4 us (14%)
  other arithmetic  42 us (7%)
  matrix products  41.8 us (7%)
  local copies, waits for them, and re-layouts  41.3 us (7%)
  Pallas kernels  31.6 us (6%)
    ppermute x39, waiting for transfers between devices, z_pull(): return lax.ppermute(x, 'fsdp', [((j + s) % n, j) for j in range(n)])  157 us
    ppermute x12, waiting for transfers between devices, y_pull(): lax.ppermute(x, 'rep', [((a + d) % ys * 2 + c, a * 2 + c) for a in range(...  129 us
    ppermute x39, starting transfers between devices, z_pull(): return lax.ppermute(x, 'fsdp', [((j + s) % n, j) for j in range(n)])  61.1 us
    ppermute x5, waiting for transfers between devices, tp_swap(): return lax.ppermute(x, 'tp', [(0, 1), (1, 0)])  32.6 us
    dot_general x8, matrix products, dot_tn(): lax.dot_general(a, b, (((0,), (0,)), ((), ())), preferred_element_type=F32)  23.4 us
    pallas_call x1, Pallas kernels, attend_backward(): pl.pallas_call(functools.partial(backward_kernel, heads), out_shape=(jax....  15.9 us
    pallas_call x1, Pallas kernels, attend_forward(): pl.pallas_call(functools.partial(forward_kernel, heads), out_shape=(jax.S...  15.7 us
    unnamed x157, local copies, waits for them, and re-layouts  15.5 us
  transfers between devices with their start and end apart: 75, of which 30 were waited for; matrix products, arithmetic and copies ran while one was open for 20% of the time, Pallas kernels for 6%

profile of v3, /device:TPU:0, one launch (start us, length us, event | category | flops | bytes accessed | tf_op | source)
XLA Modules:
  0.0 560.3 jit_solution(13361268110610094818)
XLA Ops:
  5.2 3.1 collective-permute-start.2
  8.3 2.6 collective-permute-start.1
  18.2 2.9 collective-permute-start.3
  25.7 2.7 collective-permute-done.4
  31.0 3.1 collective-permute-start.16
  36.6 5.6 %collective-permute-done.16 = bf16[256,640]{1,0:T(8,128)(2,1)S(1)} collective-permute-done((bf16[256,640]{1,0:T(8,128)(2,1)S(1)}, bf16[256,640]{1,0:T(8,128)(2,1)S(1)}, u32[]{:S(2)}, u32[]{:S(2)}) %collective-permute-start.16) | collective-permute-done | bytes 327712 | tf_op jit(solution)/shard_map/ppermute | solution.py:238
  42.3 21.4 %collective-permute-done.17 = bf16[256,640]{1,0:T(8,128)(2,1)S(1)} collective-permute-done((bf16[256,640]{1,0:T(8,128)(2,1)S(1)}, bf16[256,640]{1,0:T(8,128)(2,1)S(1)}, u32[]{:S(2)}, u32[]{:S(2)}) %collective-permute-start.17) | collective-permute-done | bytes 327712 | tf_op jit(solution)/shard_map/ppermute | solution.py:238
  66.2 4.3 collective-permute-done.19
  75.4 2.8 collective-permute-start.9
  81.5 3.0 collective-permute-done.11
  84.5 8.2 %collective-permute-done.10 = bf16[352,384]{1,0:T(8,128)(2,1)S(1)} collective-permute-done((bf16[352,384]{1,0:T(8,128)(2,1)S(1)}, bf16[352,384]{1,0:T(8,128)(2,1)S(1)}, u32[]{:S(2)}, u32[]{:S(2)}) %collective-permute-start.10) | collective-permute-done | bytes 270368 | tf_op jit(solution)/shard_map/ppermute | solution.py:238
  93.8 6.3 %collective-permute-start.25 = (bf16[512,256]{1,0:T(8,128)(2,1)S(1)}, bf16[512,256]{1,0:T(8,128)(2,1)S(1)}, u32[]{:S(2)}, u32[]{:S(2)}) collective-permute-start(bf16[512,256]{1,0:T(8,128)(2,1)S(1)} %dynamic-slice_bitcast_fusion.12), channel_id=1, source_target_pairs={{6,0},{0,2},{2,4},{4,6},{7,1},{1,3},{3,5},{5,7},{14,8},{8,10},{10,... | collective-permute-start | bytes 786440 | tf_op jit(solution)/shard_map/ppermute | solution.py:238
  100.1 2.8 collective-permute-start.24
  103.9 15.7 %attend_forward.1 = (bf16[1408,128]{1,0:T(8,128)(2,1)}, f32[11,1,256]{2,1,0:T(1,128)}) custom-call(bf16[1408,384]{1,0:T(8,128)(2,1)} %pad_maximum_fusion.7.x_ref, s32[1408,128]{1,0:T(8,128)} %broadcast_in_dim.18.key_ref, s32[11,1,128]{2,1,0:T(1,128)} %and_select_fusion.seg_ref), custom_call_target="tpu_custom_call" | custom-call | flops 1015021568 | bytes 1441792 | tf_op jit(solution)/shard_map/attend_forward/pallas_call | solution.py:162
  121.6 4.5 collective-permute-done.12
  126.3 5.7 %collective-permute-done.13 = bf16[352,128]{1,0:T(8,128)(2,1)S(1)} collective-permute-done((bf16[352,128]{1,0:T(8,128)(2,1)S(1)}, bf16[352,128]{1,0:T(8,128)(2,1)S(1)}, u32[]{:S(2)}, u32[]{:S(2)}) %collective-permute-start.13) | collective-permute-done | bytes 90144 | tf_op jit(solution)/shard_map/ppermute | solution.py:238
  132.0 7.3 %collective-permute-done.14 = bf16[352,128]{1,0:T(8,128)(2,1)S(1)} collective-permute-done((bf16[352,128]{1,0:T(8,128)(2,1)S(1)}, bf16[352,128]{1,0:T(8,128)(2,1)S(1)}, u32[]{:S(2)}, u32[]{:S(2)}) %collective-permute-start.14) | collective-permute-done | bytes 90144 | tf_op jit(solution)/shard_map/ppermute | solution.py:238
  140.8 5.3 collective-permute-done.23
  155.3 19.0 %collective-permute-done.26 = bf16[512,1024]{1,0:T(8,128)(2,1)S(1)} collective-permute-done((bf16[512,1024]{1,0:T(8,128)(2,1)S(1)}, bf16[512,1024]{1,0:T(8,128)(2,1)S(1)}, u32[]{:S(2)}, u32[]{:S(2)}) %collective-permute-start.26) | collective-permute-done | bytes 1048608 | tf_op jit(solution)/shard_map/ppermute | solution.py:244
  175.1 3.7 fusion.138
  183.0 3.4 fusion.68
  190.0 2.6 fusion.74
  199.8 3.3 fusion.71
  203.2 24.0 %collective-permute-done.29 = f32[352,1024]{1,0:T(8,128)S(1)} collective-permute-done((f32[352,1024]{1,0:T(8,128)S(1)}, f32[352,1024]{1,0:T(8,128)S(1)}, u32[]{:S(2)}, u32[]{:S(2)}) %collective-permute-start.29) | collective-permute-done | bytes 1441824 | tf_op jit(solution)/shard_map/ppermute | solution.py:283
  240.4 15.9 %attend_backward.1 = (bf16[1408,384]{1,0:T(8,128)(2,1)}, f32[2,128]{1,0:T(2,128)}) custom-call(bf16[1408,384]{1,0:T(8,128)(2,1)} %pad_maximum_fusion.7.x_ref, bf16[1408,128]{1,0:T(8,128)(2,1)} %get-tuple-element.30.o_ref, bf16[1408,128]{1,0:T(8,128)(2,1)} %pad_maximum_fusion.14.g_ref, f32[11,1,256]{2,1,0:T(1,128)} %get-tuple-element.34.lse_ref, ...), custom_call_target="tpu_custom_call" | custom-call | flops 2537553920 | bytes 3604480 | tf_op jit(solution)/shard_map/attend_backward/pallas_call | solution.py:181
  264.1 4.7 multiply_reduce_fusion
  271.3 17.9 %collective-permute-done.35 = bf16[352,384]{1,0:T(8,128)(2,1)S(1)} collective-permute-done((bf16[352,384]{1,0:T(8,128)(2,1)S(1)}, bf16[352,384]{1,0:T(8,128)(2,1)S(1)}, u32[]{:S(2)}, u32[]{:S(2)}) %collective-permute-start.35) | collective-permute-done | bytes 270368 | tf_op jit(solution)/shard_map/ppermute | solution.py:238
  296.0 5.5 collective-permute-done.52
  301.7 4.0 collective-permute-start.55
  305.7 4.2 collective-permute-done.53
  309.9 4.8 collective-permute-done.54
  316.7 3.2 collective-permute-done.56
  319.9 2.8 fusion.78
  324.2 4.3 collective-permute-done.37
  330.4 3.8 collective-permute-start.38
  337.3 3.6 collective-permute-done.39
  341.0 3.8 convolution_add_fusion.1
  346.6 3.1 convolution_add_fusion.3
  351.0 3.5 convolution_add_fusion.2
  357.6 94.1 %collective-permute-done.41 = f32[88,128]{1,0:T(8,128)S(1)} collective-permute-done((f32[88,128]{1,0:T(8,128)S(1)}, f32[88,128]{1,0:T(8,128)S(1)}, u32[]{:S(2)}, u32[]{:S(2)}) %collective-permute-start.41) | collective-permute-done | bytes 45088 | tf_op jit(solution)/shard_map/ppermute | solution.py:244
  457.4 8.7 %collective-permute-done.45 = f32[256,384]{0,1:T(8,128)S(1)} collective-permute-done((f32[256,384]{0,1:T(8,128)S(1)}, f32[256,384]{0,1:T(8,128)S(1)}, u32[]{:S(2)}, u32[]{:S(2)}) %collective-permute-start.45) | collective-permute-done | bytes 393248 | tf_op jit(solution)/shard_map/ppermute | solution.py:238
  466.0 7.6 %collective-permute-done.47 = f32[256,384]{0,1:T(8,128)S(1)} collective-permute-done((f32[256,384]{0,1:T(8,128)S(1)}, f32[256,384]{0,1:T(8,128)S(1)}, u32[]{:S(2)}, u32[]{:S(2)}) %collective-permute-start.47) | collective-permute-done | bytes 393248 | tf_op jit(solution)/shard_map/ppermute | solution.py:238
  473.6 3.5 collective-permute-start.71
  477.1 19.6 %collective-permute-done.46 = f32[256,384]{0,1:T(8,128)S(1)} collective-permute-done((f32[256,384]{0,1:T(8,128)S(1)}, f32[256,384]{0,1:T(8,128)S(1)}, u32[]{:S(2)}, u32[]{:S(2)}) %collective-permute-start.46) | collective-permute-done | bytes 393248 | tf_op jit(solution)/shard_map/ppermute | solution.py:238
  499.9 6.0 %collective-permute-start.61 = (bf16[256,512]{0,1:T(8,128)(2,1)}, bf16[256,512]{0,1:T(8,128)(2,1)S(1)}, u32[]{:S(2)}, u32[]{:S(2)}) collective-permute-start(bf16[256,512]{0,1:T(8,128)(2,1)} %get-tuple-element.107), channel_id=1, source_target_pairs={{6,0},{0,2},{2,4},{4,6},{7,1},{1,3},{3,5},{5,7},{14,8},{8,10},{10,... | collective-permute-start | bytes 786440 | tf_op jit(solution)/shard_map/ppermute | solution.py:238
  505.8 13.3 %collective-permute-done.70 = bf16[512,256]{1,0:T(8,128)(2,1)S(1)} collective-permute-done((bf16[512,256]{1,0:T(8,128)(2,1)S(1)}, bf16[512,256]{1,0:T(8,128)(2,1)S(1)}, u32[]{:S(2)}, u32[]{:S(2)}) %collective-permute-start.70) | collective-permute-done | bytes 262176 | tf_op jit(solution)/shard_map/ppermute | solution.py:238
  530.8 7.7 %collective-permute-done.62 = bf16[256,512]{0,1:T(8,128)(2,1)} collective-permute-done((bf16[256,512]{0,1:T(8,128)(2,1)}, bf16[256,512]{0,1:T(8,128)(2,1)}, u32[]{:S(2)}, u32[]{:S(2)}) %collective-permute-start.62) | collective-permute-done | bytes 262176 | tf_op jit(solution)/shard_map/ppermute | solution.py:238
  545.5 7.3 %collective-permute-done.64 = f32[256,512]{0,1:T(8,128)} collective-permute-done((f32[256,512]{0,1:T(8,128)S(1)}, f32[256,512]{0,1:T(8,128)}, u32[]{:S(2)}, u32[]{:S(2)}) %collective-permute-start.64) | collective-permute-done | bytes 524320 | tf_op jit(solution)/shard_map/ppermute | solution.py:244
  (449 shorter events, 140.5 us)
Async XLA Ops:
  5.2 13.0 %collective-permute-start.2 = (bf16[13,256]{1,0:T(8,128)(2,1)S(1)}, bf16[13,256]{1,0:T(8,128)(2,1)S(1)}, u32[]{:S(2)}, u32[]{:S(2)}) collective-permute-start(bf16[13,256]{1,0:T(8,128)(2,1)S(1)} %concatenate.144), channel_id=1, source_target_pairs={{6,0},{0,2},{2,4},{4,6},{7,1},{1,3},{3,5},{5,7},{14,8},{8,10},{10,... | collective-permute-start | bytes 19976 | tf_op jit(solution)/shard_map/ppermute | solution.py:238
  8.3 12.8 %collective-permute-start.1 = (bf16[13,256]{1,0:T(8,128)(2,1)S(1)}, bf16[13,256]{1,0:T(8,128)(2,1)S(1)}, u32[]{:S(2)}, u32[]{:S(2)}) collective-permute-start(bf16[13,256]{1,0:T(8,128)(2,1)S(1)} %concatenate.144), channel_id=1, source_target_pairs={{4,0},{6,2},{0,4},{2,6},{5,1},{7,3},{1,5},{3,7},{12,8},{14,10},{8,... | collective-permute-start | bytes 19976 | tf_op jit(solution)/shard_map/ppermute | solution.py:238
  12.2 13.4 %collective-permute-start.5 = (bf16[256,384]{0,1:T(8,128)(2,1)S(1)}, bf16[256,384]{0,1:T(8,128)(2,1)S(1)}, u32[]{:S(2)}, u32[]{:S(2)}) collective-permute-start(bf16[256,384]{0,1:T(8,128)(2,1)S(1)} %bitcast.257), channel_id=1, source_target_pairs={{6,0},{0,2},{2,4},{4,6},{7,1},{1,3},{3,5},{5,7},{14,8},{8,10},{10,... | collective-permute-start | bytes 589832 | tf_op jit(solution)/shard_map/ppermute | solution.py:238
  12.9 15.5 %collective-permute-start.4 = (bf16[256,384]{0,1:T(8,128)(2,1)S(1)}, bf16[256,384]{0,1:T(8,128)(2,1)S(1)}, u32[]{:S(2)}, u32[]{:S(2)}) collective-permute-start(bf16[256,384]{0,1:T(8,128)(2,1)S(1)} %bitcast.258), channel_id=1, source_target_pairs={{4,0},{6,2},{0,4},{2,6},{5,1},{7,3},{1,5},{3,7},{12,8},{14,10},{8,... | collective-permute-start | bytes 589832 | tf_op jit(solution)/shard_map/ppermute | solution.py:238
  29.3 36.1 %collective-permute-start.6 = (bf16[1024,384]{0,1:T(8,128)(2,1)S(1)}, bf16[1024,384]{0,1:T(8,128)(2,1)S(1)}, u32[]{:S(2)}, u32[]{:S(2)}) collective-permute-start(bf16[1024,384]{0,1:T(8,128)(2,1)S(1)} %pad_maximum_fusion.8), channel_id=1, source_target_pairs={{16,0},{24,8},{0,16},{8,24},{17,1},{25,9},{1,17},{9,25},{18,2},{26... | collective-permute-start | bytes 2359304 | tf_op jit(solution)/shard_map/ppermute | solution.py:244
  34.7 29.0 %collective-permute-start.17 = (bf16[256,640]{1,0:T(8,128)(2,1)S(1)}, bf16[256,640]{1,0:T(8,128)(2,1)S(1)}, u32[]{:S(2)}, u32[]{:S(2)}) collective-permute-start(bf16[256,640]{1,0:T(8,128)(2,1)S(1)} %pad_maximum_fusion.15), channel_id=1, source_target_pairs={{4,0},{6,2},{0,4},{2,6},{5,1},{7,3},{1,5},{3,7},{12,8},{14,10},{8,... | collective-permute-start | bytes 983048 | tf_op jit(solution)/shard_map/ppermute | solution.py:238
  36.5 27.3 %collective-permute-start.18 = (bf16[256,640]{1,0:T(8,128)(2,1)S(1)}, bf16[256,640]{1,0:T(8,128)(2,1)S(1)}, u32[]{:S(2)}, u32[]{:S(2)}) collective-permute-start(bf16[256,640]{1,0:T(8,128)(2,1)S(1)} %pad_maximum_fusion.15), channel_id=1, source_target_pairs={{6,0},{0,2},{2,4},{4,6},{7,1},{1,3},{3,5},{5,7},{14,8},{8,10},{10,... | collective-permute-start | bytes 983048 | tf_op jit(solution)/shard_map/ppermute | solution.py:238
  36.5 34.7 %collective-permute-start.7 = (bf16[1024,384]{0,1:T(8,128)(2,1)S(1)}, bf16[1024,384]{0,1:T(8,128)(2,1)S(1)}, u32[]{:S(2)}, u32[]{:S(2)}) collective-permute-start(bf16[1024,384]{0,1:T(8,128)(2,1)S(1)} %pad_maximum_fusion.8), channel_id=1, source_target_pairs={{0,8},{8,0},{16,24},{24,16},{1,9},{9,1},{17,25},{25,17},{2,10},{10... | collective-permute-start | bytes 2359304 | tf_op jit(solution)/shard_map/ppermute | solution.py:252
  73.4 19.3 %collective-permute-start.10 = (bf16[352,384]{1,0:T(8,128)(2,1)S(1)}, bf16[352,384]{1,0:T(8,128)(2,1)S(1)}, u32[]{:S(2)}, u32[]{:S(2)}) collective-permute-start(bf16[352,384]{1,0:T(8,128)(2,1)S(1)} %get-tuple-element.102), channel_id=1, source_target_pairs={{4,0},{6,2},{0,4},{2,6},{5,1},{7,3},{1,5},{3,7},{12,8},{14,10},{8,... | collective-permute-start | bytes 811016 | tf_op jit(solution)/shard_map/ppermute | solution.py:238
  75.4 17.3 %collective-permute-start.9 = (bf16[352,384]{1,0:T(8,128)(2,1)S(1)}, bf16[352,384]{1,0:T(8,128)(2,1)S(1)}, u32[]{:S(2)}, u32[]{:S(2)}) collective-permute-start(bf16[352,384]{1,0:T(8,128)(2,1)S(1)} %get-tuple-element.103), channel_id=1, source_target_pairs={{2,0},{4,2},{6,4},{0,6},{3,1},{5,3},{7,5},{1,7},{10,8},{12,10},{14... | collective-permute-start | bytes 811016 | tf_op jit(solution)/shard_map/ppermute | solution.py:238
  79.6 69.7 %collective-permute-start.21 = (bf16[1024,768]{1,0:T(8,128)(2,1)}, bf16[1024,768]{1,0:T(8,128)(2,1)}, u32[]{:S(2)}, u32[]{:S(2)}) collective-permute-start(bf16[1024,768]{1,0:T(8,128)(2,1)} %pad_maximum_fusion.4), channel_id=1, source_target_pairs={{0,8},{8,0},{16,24},{24,16},{1,9},{9,1},{17,25},{25,17},{2,10},{10... | collective-permute-start | bytes 4718600 | tf_op jit(solution)/shard_map/ppermute | solution.py:252
  79.6 72.1 %collective-permute-start.20 = (bf16[1024,768]{1,0:T(8,128)(2,1)}, bf16[1024,768]{1,0:T(8,128)(2,1)S(1)}, u32[]{:S(2)}, u32[]{:S(2)}) collective-permute-start(bf16[1024,768]{1,0:T(8,128)(2,1)} %pad_maximum_fusion.4), channel_id=1, source_target_pairs={{16,0},{24,8},{0,16},{8,24},{17,1},{25,9},{1,17},{9,25},{18,2},{26... | collective-permute-start | bytes 4718600 | tf_op jit(solution)/shard_map/ppermute | solution.py:244
  93.8 54.8 %collective-permute-start.25 = (bf16[512,256]{1,0:T(8,128)(2,1)S(1)}, bf16[512,256]{1,0:T(8,128)(2,1)S(1)}, u32[]{:S(2)}, u32[]{:S(2)}) collective-permute-start(bf16[512,256]{1,0:T(8,128)(2,1)S(1)} %dynamic-slice_bitcast_fusion.12), channel_id=1, source_target_pairs={{6,0},{0,2},{2,4},{4,6},{7,1},{1,3},{3,5},{5,7},{14,8},{8,10},{10,... | collective-permute-start | bytes 786440 | tf_op jit(solution)/shard_map/ppermute | solution.py:238
  100.1 47.6 %collective-permute-start.24 = (bf16[512,256]{1,0:T(8,128)(2,1)S(1)}, bf16[512,256]{1,0:T(8,128)(2,1)}, u32[]{:S(2)}, u32[]{:S(2)}) collective-permute-start(bf16[512,256]{1,0:T(8,128)(2,1)S(1)} %dynamic-slice_bitcast_fusion.12), channel_id=1, source_target_pairs={{4,0},{6,2},{0,4},{2,6},{5,1},{7,3},{1,5},{3,7},{12,8},{14,10},{8,... | collective-permute-start | bytes 786440 | tf_op jit(solution)/shard_map/ppermute | solution.py:238
  148.7 39.7 %collective-permute-start.27 = (bf16[512,1024]{1,0:T(8,128)(2,1)S(1)}, bf16[512,1024]{1,0:T(8,128)(2,1)S(1)}, u32[]{:S(2)}, u32[]{:S(2)}) collective-permute-start(bf16[512,1024]{1,0:T(8,128)(2,1)S(1)} %constant_dynamic-update-slice_fusion.22), channel_id=1, source_target_pairs={{0,8},{8,0},{16,24},{24,16},{1,9},{9,1},{17,25},{25,17},{2,10},{10... | collective-permute-start | bytes 3145736 | tf_op jit(solution)/shard_map/ppermute | solution.py:252
  148.7 25.6 %collective-permute-start.26 = (bf16[512,1024]{1,0:T(8,128)(2,1)S(1)}, bf16[512,1024]{1,0:T(8,128)(2,1)S(1)}, u32[]{:S(2)}, u32[]{:S(2)}) collective-permute-start(bf16[512,1024]{1,0:T(8,128)(2,1)S(1)} %constant_dynamic-update-slice_fusion.22), channel_id=1, source_target_pairs={{16,0},{24,8},{0,16},{8,24},{17,1},{25,9},{1,17},{9,25},{18,2},{26... | collective-permute-start | bytes 3145736 | tf_op jit(solution)/shard_map/ppermute | solution.py:244
  151.8 22.5 %collective-permute-start.22 = (bf16[1024,768]{1,0:T(8,128)(2,1)S(1)}, bf16[1024,768]{1,0:T(8,128)(2,1)S(1)}, u32[]{:S(2)}, u32[]{:S(2)}) collective-permute-start(bf16[1024,768]{1,0:T(8,128)(2,1)S(1)} %collective-permute-done.20), channel_id=1, source_target_pairs={{0,8},{8,0},{16,24},{24,16},{1,9},{9,1},{17,25},{25,17},{2,10},{10... | collective-permute-start | bytes 4718600 | tf_op jit(solution)/shard_map/ppermute | solution.py:252
  174.3 14.8 %collective-permute-start.28 = (bf16[512,1024]{1,0:T(8,128)(2,1)S(1)}, bf16[512,1024]{1,0:T(8,128)(2,1)S(1)}, u32[]{:S(2)}, u32[]{:S(2)}) collective-permute-start(bf16[512,1024]{1,0:T(8,128)(2,1)S(1)} %collective-permute-done.26), channel_id=1, source_target_pairs={{0,8},{8,0},{16,24},{24,16},{1,9},{9,1},{17,25},{25,17},{2,10},{10... | collective-permute-start | bytes 3145736 | tf_op jit(solution)/shard_map/ppermute | solution.py:252
  186.4 154.5 %collective-permute-start.67 = (f32[1024,1024]{1,0:T(8,128)}, f32[1024,1024]{1,0:T(8,128)}, u32[]{:S(2)}, u32[]{:S(2)}) collective-permute-start(f32[1024,1024]{1,0:T(8,128)} %fusion.68), channel_id=1, source_target_pairs={{0,8},{8,0},{16,24},{24,16},{1,9},{9,1},{17,25},{25,17},{2,10},{10... | collective-permute-start | bytes 12582920 | tf_op jit(solution)/shard_map/ppermute | solution.py:252
  192.6 34.5 %collective-permute-start.29 = (f32[352,1024]{1,0:T(8,128)S(1)}, f32[352,1024]{1,0:T(8,128)S(1)}, u32[]{:S(2)}, u32[]{:S(2)}) collective-permute-start(f32[352,1024]{1,0:T(8,128)S(1)} %fusion.74), channel_id=1, source_target_pairs={{0,1},{1,0},{2,3},{3,2},{4,5},{5,4},{6,7},{7,6},{8,9},{9,8},{10,11... | collective-permute-start | bytes 4325384 | tf_op jit(solution)/shard_map/ppermute | solution.py:283
  196.5 63.4 %collective-permute-start.30 = (f32[352,1024]{1,0:T(8,128)}, f32[352,1024]{1,0:T(8,128)}, u32[]{:S(2)}, u32[]{:S(2)}) collective-permute-start(f32[352,1024]{1,0:T(8,128)} %convolution_add_fusion.4), channel_id=1, source_target_pairs={{0,1},{1,0},{2,3},{3,2},{4,5},{5,4},{6,7},{7,6},{8,9},{9,8},{10,11... | collective-permute-start | bytes 4325384 | tf_op jit(solution)/shard_map/ppermute | solution.py:283
  237.8 53.0 %collective-permute-start.51 = (f32[256,1024]{1,0:T(8,128)}, f32[256,1024]{1,0:T(8,128)}, u32[]{:S(2)}, u32[]{:S(2)}) collective-permute-start(f32[256,1024]{1,0:T(8,128)} %fusion.97), channel_id=1, source_target_pairs={{0,8},{8,0},{16,24},{24,16},{1,9},{9,1},{17,25},{25,17},{2,10},{10... | collective-permute-start | bytes 3145736 | tf_op jit(solution)/shard_map/ppermute | solution.py:252
  269.8 19.5 %collective-permute-start.36 = (bf16[352,384]{1,0:T(8,128)(2,1)S(1)}, bf16[352,384]{1,0:T(8,128)(2,1)S(1)}, u32[]{:S(2)}, u32[]{:S(2)}) collective-permute-start(bf16[352,384]{1,0:T(8,128)(2,1)S(1)} %get-tuple-element.97), channel_id=1, source_target_pairs={{6,0},{0,2},{2,4},{4,6},{7,1},{1,3},{3,5},{5,7},{14,8},{8,10},{10,... | collective-permute-start | bytes 811016 | tf_op jit(solution)/shard_map/ppermute | solution.py:238
  269.9 19.3 %collective-permute-start.35 = (bf16[352,384]{1,0:T(8,128)(2,1)S(1)}, bf16[352,384]{1,0:T(8,128)(2,1)S(1)}, u32[]{:S(2)}, u32[]{:S(2)}) collective-permute-start(bf16[352,384]{1,0:T(8,128)(2,1)S(1)} %copy-done.24), channel_id=1, source_target_pairs={{4,0},{6,2},{0,4},{2,6},{5,1},{7,3},{1,5},{3,7},{12,8},{14,10},{8,... | collective-permute-start | bytes 811016 | tf_op jit(solution)/shard_map/ppermute | solution.py:238
  295.4 33.0 %collective-permute-start.37 = (f32[352,1024]{1,0:T(8,128)S(1)}, f32[352,1024]{1,0:T(8,128)S(1)}, u32[]{:S(2)}, u32[]{:S(2)}) collective-permute-start(f32[352,1024]{1,0:T(8,128)S(1)} %fusion), channel_id=1, source_target_pairs={{0,1},{1,0},{2,3},{3,2},{4,5},{5,4},{6,7},{7,6},{8,9},{9,8},{10,11... | collective-permute-start | bytes 4325384 | tf_op jit(solution)/shard_map/ppermute | solution.py:283
  309.9 40.6 %collective-permute-start.59 = (f32[1024,1024]{0,1:T(8,128)}, f32[1024,1024]{0,1:T(8,128)}, u32[]{:S(2)}, u32[]{:S(2)}) collective-permute-start(f32[1024,1024]{0,1:T(8,128)} %fusion.71), channel_id=1, source_target_pairs={{0,8},{8,0},{16,24},{24,16},{1,9},{9,1},{17,25},{25,17},{2,10},{10... | collective-permute-start | bytes 12582920 | tf_op jit(solution)/shard_map/ppermute | solution.py:252
  322.7 23.9 %collective-permute-start.43 = (f32[1024,768]{0,1:T(8,128)}, f32[1024,768]{0,1:T(8,128)}, u32[]{:S(2)}, u32[]{:S(2)}) collective-permute-start(f32[1024,768]{0,1:T(8,128)} %fusion.78), channel_id=1, source_target_pairs={{0,8},{8,0},{16,24},{24,16},{1,9},{9,1},{17,25},{25,17},{2,10},{10... | collective-permute-start | bytes 9437192 | tf_op jit(solution)/shard_map/ppermute | solution.py:252
  345.0 111.1 %collective-permute-start.68 = (f32[512,1024]{1,0:T(8,128)S(1)}, f32[512,1024]{1,0:T(8,128)S(1)}, u32[]{:S(2)}, u32[]{:S(2)}) collective-permute-start(f32[512,1024]{1,0:T(8,128)S(1)} %slice.604), channel_id=1, source_target_pairs={{16,0},{24,8},{0,16},{8,24},{17,1},{25,9},{1,17},{9,25},{18,2},{26... | collective-permute-start | bytes 6291464 | tf_op jit(solution)/shard_map/ppermute | solution.py:244
  349.8 102.0 %collective-permute-start.44 = (bf16[1024,384]{0,1:T(8,128)(2,1)S(1)}, bf16[1024,384]{0,1:T(8,128)(2,1)S(1)}, u32[]{:S(2)}, u32[]{:S(2)}) collective-permute-start(bf16[1024,384]{0,1:T(8,128)(2,1)S(1)} %slice.696), channel_id=1, source_target_pairs={{16,0},{24,8},{0,16},{8,24},{17,1},{25,9},{1,17},{9,25},{18,2},{26... | collective-permute-start | bytes 2359304 | tf_op jit(solution)/shard_map/ppermute | solution.py:244
  354.9 142.0 %collective-permute-start.60 = (f32[1024,512]{0,1:T(8,128)S(1)}, f32[1024,512]{0,1:T(8,128)S(1)}, u32[]{:S(2)}, u32[]{:S(2)}) collective-permute-start(f32[1024,512]{0,1:T(8,128)S(1)} %slice.595), channel_id=1, source_target_pairs={{16,0},{24,8},{0,16},{8,24},{17,1},{25,9},{1,17},{9,25},{18,2},{26... | collective-permute-start | bytes 6291464 | tf_op jit(solution)/shard_map/ppermute | solution.py:244
  355.8 95.8 %collective-permute-start.41 = (f32[88,128]{1,0:T(8,128)S(1)}, f32[88,128]{1,0:T(8,128)S(1)}, u32[]{:S(2)}, u32[]{:S(2)}) collective-permute-start(f32[88,128]{1,0:T(8,128)S(1)} %dynamic-slice_reduce_fusion), channel_id=1, source_target_pairs={{16,0},{24,8},{0,16},{8,24},{17,1},{25,9},{1,17},{9,25},{18,2},{26... | collective-permute-start | bytes 135176 | tf_op jit(solution)/shard_map/ppermute | solution.py:244
  451.7 69.4 %collective-permute-start.42 = (f32[88,128]{1,0:T(8,128)S(1)}, f32[88,128]{1,0:T(8,128)S(1)}, u32[]{:S(2)}, u32[]{:S(2)}) collective-permute-start(f32[88,128]{1,0:T(8,128)S(1)} %fusion.106), channel_id=1, source_target_pairs={{0,8},{8,0},{16,24},{24,16},{1,9},{9,1},{17,25},{25,17},{2,10},{10... | collective-permute-start | bytes 135176 | tf_op jit(solution)/shard_map/ppermute | solution.py:252
  452.1 13.9 %collective-permute-start.45 = (f32[256,384]{0,1:T(8,128)S(1)}, f32[256,384]{0,1:T(8,128)S(1)}, u32[]{:S(2)}, u32[]{:S(2)}) collective-permute-start(f32[256,384]{0,1:T(8,128)S(1)} %get-tuple-element.94), channel_id=1, source_target_pairs={{6,0},{0,2},{2,4},{4,6},{7,1},{1,3},{3,5},{5,7},{14,8},{8,10},{10,... | collective-permute-start | bytes 1179656 | tf_op jit(solution)/shard_map/ppermute | solution.py:238
  453.9 19.7 %collective-permute-start.47 = (f32[256,384]{0,1:T(8,128)S(1)}, f32[256,384]{0,1:T(8,128)S(1)}, u32[]{:S(2)}, u32[]{:S(2)}) collective-permute-start(f32[256,384]{0,1:T(8,128)S(1)} %get-tuple-element.95), channel_id=1, source_target_pairs={{2,0},{4,2},{6,4},{0,6},{3,1},{5,3},{7,5},{1,7},{10,8},{12,10},{14... | collective-permute-start | bytes 1179656 | tf_op jit(solution)/shard_map/ppermute | solution.py:238
  456.1 40.6 %collective-permute-start.46 = (f32[256,384]{0,1:T(8,128)S(1)}, f32[256,384]{0,1:T(8,128)S(1)}, u32[]{:S(2)}, u32[]{:S(2)}) collective-permute-start(f32[256,384]{0,1:T(8,128)S(1)} %get-tuple-element.96), channel_id=1, source_target_pairs={{4,0},{6,2},{0,4},{2,6},{5,1},{7,3},{1,5},{3,7},{12,8},{14,10},{8,... | collective-permute-start | bytes 1179656 | tf_op jit(solution)/shard_map/ppermute | solution.py:238
  466.0 33.9 %collective-permute-start.69 = (bf16[512,256]{1,0:T(8,128)(2,1)S(1)}, bf16[512,256]{1,0:T(8,128)(2,1)S(1)}, u32[]{:S(2)}, u32[]{:S(2)}) collective-permute-start(bf16[512,256]{1,0:T(8,128)(2,1)S(1)} %get-tuple-element.104), channel_id=1, source_target_pairs={{6,0},{0,2},{2,4},{4,6},{7,1},{1,3},{3,5},{5,7},{14,8},{8,10},{10,... | collective-permute-start | bytes 786440 | tf_op jit(solution)/shard_map/ppermute | solution.py:238
  473.6 32.2 %collective-permute-start.71 = (bf16[512,256]{1,0:T(8,128)(2,1)S(1)}, bf16[512,256]{1,0:T(8,128)(2,1)S(1)}, u32[]{:S(2)}, u32[]{:S(2)}) collective-permute-start(bf16[512,256]{1,0:T(8,128)(2,1)S(1)} %get-tuple-element.105), channel_id=1, source_target_pairs={{2,0},{4,2},{6,4},{0,6},{3,1},{5,3},{7,5},{1,7},{10,8},{12,10},{14... | collective-permute-start | bytes 786440 | tf_op jit(solution)/shard_map/ppermute | solution.py:238
  496.7 22.4 %collective-permute-start.70 = (bf16[512,256]{1,0:T(8,128)(2,1)S(1)}, bf16[512,256]{1,0:T(8,128)(2,1)S(1)}, u32[]{:S(2)}, u32[]{:S(2)}) collective-permute-start(bf16[512,256]{1,0:T(8,128)(2,1)S(1)} %get-tuple-element.106), channel_id=1, source_target_pairs={{4,0},{6,2},{0,4},{2,6},{5,1},{7,3},{1,5},{3,7},{12,8},{14,10},{8,... | collective-permute-start | bytes 786440 | tf_op jit(solution)/shard_map/ppermute | solution.py:238
  496.9 28.5 %collective-permute-start.48 = (f32[256,384]{0,1:T(8,128)S(1)}, f32[256,384]{0,1:T(8,128)}, u32[]{:S(2)}, u32[]{:S(2)}) collective-permute-start(f32[256,384]{0,1:T(8,128)S(1)} %fusion.87), channel_id=1, source_target_pairs={{16,0},{24,8},{0,16},{8,24},{17,1},{25,9},{1,17},{9,25},{18,2},{26... | collective-permute-start | bytes 1179656 | tf_op jit(solution)/shard_map/ppermute | solution.py:244
  499.9 25.5 %collective-permute-start.61 = (bf16[256,512]{0,1:T(8,128)(2,1)}, bf16[256,512]{0,1:T(8,128)(2,1)S(1)}, u32[]{:S(2)}, u32[]{:S(2)}) collective-permute-start(bf16[256,512]{0,1:T(8,128)(2,1)} %get-tuple-element.107), channel_id=1, source_target_pairs={{6,0},{0,2},{2,4},{4,6},{7,1},{1,3},{3,5},{5,7},{14,8},{8,10},{10,... | collective-permute-start | bytes 786440 | tf_op jit(solution)/shard_map/ppermute | solution.py:238
  519.3 21.0 %collective-permute-start.72 = (f32[512,256]{1,0:T(8,128)S(1)}, f32[512,256]{1,0:T(8,128)}, u32[]{:S(2)}, u32[]{:S(2)}) collective-permute-start(f32[512,256]{1,0:T(8,128)S(1)} %fusion.83), channel_id=1, source_target_pairs={{16,0},{24,8},{0,16},{8,24},{17,1},{25,9},{1,17},{9,25},{18,2},{26... | collective-permute-start | bytes 1572872 | tf_op jit(solution)/shard_map/ppermute | solution.py:244
  521.1 17.3 %collective-permute-start.62 = (bf16[256,512]{0,1:T(8,128)(2,1)}, bf16[256,512]{0,1:T(8,128)(2,1)}, u32[]{:S(2)}, u32[]{:S(2)}) collective-permute-start(bf16[256,512]{0,1:T(8,128)(2,1)} %get-tuple-element.109), channel_id=1, source_target_pairs={{4,0},{6,2},{0,4},{2,6},{5,1},{7,3},{1,5},{3,7},{12,8},{14,10},{8,... | collective-permute-start | bytes 786440 | tf_op jit(solution)/shard_map/ppermute | solution.py:238
  525.4 16.2 %collective-permute-start.49 = (f32[256,384]{0,1:T(8,128)S(1)}, f32[256,384]{0,1:T(8,128)}, u32[]{:S(2)}, u32[]{:S(2)}) collective-permute-start(f32[256,384]{0,1:T(8,128)S(1)} %fusion.87), channel_id=1, source_target_pairs={{0,8},{8,0},{16,24},{24,16},{1,9},{9,1},{17,25},{25,17},{2,10},{10... | collective-permute-start | bytes 1179656 | tf_op jit(solution)/shard_map/ppermute | solution.py:252
  525.4 16.7 %collective-permute-start.50 = (f32[256,384]{0,1:T(8,128)}, f32[256,384]{0,1:T(8,128)}, u32[]{:S(2)}, u32[]{:S(2)}) collective-permute-start(f32[256,384]{0,1:T(8,128)} %collective-permute-done.48), channel_id=1, source_target_pairs={{0,8},{8,0},{16,24},{24,16},{1,9},{9,1},{17,25},{25,17},{2,10},{10... | collective-permute-start | bytes 1179656 | tf_op jit(solution)/shard_map/ppermute | solution.py:252
  530.7 22.2 %collective-permute-start.73 = (f32[512,256]{1,0:T(8,128)S(1)}, f32[512,256]{1,0:T(8,128)}, u32[]{:S(2)}, u32[]{:S(2)}) collective-permute-start(f32[512,256]{1,0:T(8,128)S(1)} %fusion.83), channel_id=1, source_target_pairs={{0,8},{8,0},{16,24},{24,16},{1,9},{9,1},{17,25},{25,17},{2,10},{10... | collective-permute-start | bytes 1572872 | tf_op jit(solution)/shard_map/ppermute | solution.py:252
  539.7 13.2 %collective-permute-start.64 = (f32[256,512]{0,1:T(8,128)S(1)}, f32[256,512]{0,1:T(8,128)}, u32[]{:S(2)}, u32[]{:S(2)}) collective-permute-start(f32[256,512]{0,1:T(8,128)S(1)} %fusion.85), channel_id=1, source_target_pairs={{16,0},{24,8},{0,16},{8,24},{17,1},{25,9},{1,17},{9,25},{18,2},{26... | collective-permute-start | bytes 1572872 | tf_op jit(solution)/shard_map/ppermute | solution.py:244
  540.3 12.6 %collective-permute-start.74 = (f32[512,256]{1,0:T(8,128)}, f32[512,256]{1,0:T(8,128)}, u32[]{:S(2)}, u32[]{:S(2)}) collective-permute-start(f32[512,256]{1,0:T(8,128)} %collective-permute-done.72), channel_id=1, source_target_pairs={{0,8},{8,0},{16,24},{24,16},{1,9},{9,1},{17,25},{25,17},{2,10},{10... | collective-permute-start | bytes 1572872 | tf_op jit(solution)/shard_map/ppermute | solution.py:252
  541.6 14.4 %collective-permute-start.65 = (f32[256,512]{0,1:T(8,128)S(1)}, f32[256,512]{0,1:T(8,128)}, u32[]{:S(2)}, u32[]{:S(2)}) collective-permute-start(f32[256,512]{0,1:T(8,128)S(1)} %fusion.85), channel_id=1, source_target_pairs={{0,8},{8,0},{16,24},{24,16},{1,9},{9,1},{17,25},{25,17},{2,10},{10... | collective-permute-start | bytes 1572872 | tf_op jit(solution)/shard_map/ppermute | solution.py:252
  (79 other events, 770.5 us)

commit v4 on v3

--- a/solution.py
+++ b/solution.py
@@ -351,7 +351,7 @@
     upstream = from_own(cotangent, 1, part).astype(F32)
 
     normed, part_one, inv_one = norm_forward(resid, gains[0], shifts[0])
-    first_in = normed.astype(BF)
+    first_in = after(normed.astype(BF), key_codes, seg_rows)
     project = [(dot(first_in, w) + b).astype(BF) for w, b in zip(slots_qkv, bias_qkv)]
     x_heads = exchange_heads(project)
     quarter_up = jnp.concatenate(gathered_up, axis=0)
@@ -362,8 +362,9 @@
     mixed, lse = attend_forward(x_heads, key_codes, seg_rows, heads)
     mixed_back = return_heads(mixed)
     slots_down = gather_rep(jnp.concatenate(gathered_down, axis=1))
-    mixed_slots = to_plain(jnp.stack(mixed_back), 0, 1)
-    mixed_flat = jnp.concatenate([mixed_slots[k] for k in range(n)], axis=1)
+    mixed_flat = jnp.concatenate(
+        [lax.select_n((k + n - z) % n, *mixed_back) for k in range(n)], axis=1
+    )
     mixed_halves = both_tp(mixed_flat, tp_swap(mixed_flat))
     mixed_full = jnp.concatenate(
         [m[:, k * q_cols : (k + 1) * q_cols] for k in range(reps) for m in mixed_halves],
@@ -406,15 +407,11 @@
         return gather_rep(result)
 
     branch_grad = (upstream * scales[1]).astype(BF)
-    d_hidden = jnp.concatenate(
-        [
-            dot_nt(branch_grad, w)
-            * gelu_slope(hidden_pre[:, k * unit_cols : (k + 1) * unit_cols])
-            for k, w in enumerate(slots_down)
-        ],
-        axis=1,
-    )
-    d_hidden_half = d_hidden.astype(BF)
+    d_hidden = [
+        dot_nt(branch_grad, w) * gelu_slope(hidden_pre[:, k * unit_cols : (k + 1) * unit_cols])
+        for k, w in enumerate(slots_down)
+    ]
+    d_hidden_half = jnp.concatenate([v.astype(BF) for v in d_hidden], axis=1)
     partial_second = dot_nt(d_hidden_half, w_up)
     d_second = partial_second + tp_swap(partial_second)
 
@@ -458,12 +455,12 @@
             other_two,
             d_second,
             part_two,
-            d_hidden,
+            *d_hidden,
             dx_heads,
         )
     )
     late_up, late_up_one, late_one, late_resid, late_two, late_other, late_second, late_part = late[:8]
-    late_hidden = late[8]
+    late_hidden = late[8:-1]
     branch_two = late_two + late_other + biases[1]
     block_out = to_plain((late_resid + scales[1] * branch_two).astype(BF), 1, part)
     scale_two = jnp.sum(late_up * branch_two, axis=0)
@@ -472,18 +469,30 @@
     bias_one = jnp.sum(late_up_one, axis=0) * scales[0]
     gain_two = jnp.sum(late_second * late_part, axis=0)
     shift_two = jnp.sum(late_second, axis=0)
-    d_up_bias = jnp.sum(late_hidden, axis=0)
 
     grad_up = scatter_z(own_up, 0, BF)
-    grad_out = scatter_z(own_out, 1)
-    dx_slots = to_plain(jnp.stack(dx_back), 0, 1)
-    d_project = jnp.concatenate([dx_slots[k] for k in range(n)], axis=1)
-    half = d_project.shape[1] // 2
-    qkv_far = dot_tn(first_in, d_project[:, half:])
-    qkv_near = dot_tn(first_in, d_project[:, :half])
-    grad_qkv = scatter_z(sum_rep(qkv_near, qkv_far, 1), 0)
-    w_qkv = jnp.concatenate(slots_qkv, axis=1)
-    partial_first = dot_nt(d_project, w_qkv)
+    grad_out = scatter_z(own_out, 1, BF)
+    cut = 2 * head_cols
+    d_pair = jnp.concatenate(
+        [lax.select_n((k + n - z) % n, *[v[:, :cut] for v in dx_back]) for k in range(n)], axis=1
+    )
+    d_value = jnp.concatenate(
+        [lax.select_n((k + n - z) % n, *[v[:, cut:] for v in dx_back]) for k in range(n)], axis=1
+    )
+    half_v, half_p = d_value.shape[1] // 2, d_pair.shape[1] // 2
+    value_far = dot_tn(first_in, d_value[:, half_v:])
+    pair_far = dot_tn(first_in, d_pair[:, half_p:])
+    value_near = dot_tn(first_in, d_value[:, :half_v])
+    pair_near = dot_tn(first_in, d_pair[:, :half_p])
+    own_value = sum_rep(value_near, value_far, 1)
+    own_pair = sum_rep(pair_near, pair_far, 1)
+    grad_value = scatter_z(own_value, 0)
+    grad_pair = scatter_z(own_pair, 0)
+    w_pair = jnp.concatenate([w[:, :cut] for w in slots_qkv], axis=1)
+    w_value = jnp.concatenate([w[:, cut:] for w in slots_qkv], axis=1)
+    partial_first = dot_nt(
+        jnp.concatenate([d_pair, d_value], axis=1), jnp.concatenate([w_pair, w_value], axis=1)
+    )
     d_first = partial_first + tp_swap(partial_first)
     d_norm_one, gain_one, shift_one = norm_backward(d_first, part_one, inv_one, gains[0])
     tokens_grad = to_plain(upstream_one + d_norm_one, 1, part)
@@ -495,13 +504,12 @@
         1,
         part,
     )
+    d_up_bias = [jnp.sum(after(v, own_pair), axis=0) for v in late_hidden]
     own_rep = lax.dynamic_index_in_dim(jnp.stack(slot_rep), z, 0, keepdims=False)
     qv_grads = lax.dynamic_update_slice_in_dim(
         jnp.zeros((2, local_heads * HD), F32), head_sums, own_rep * head_cols, 1
     )
-    up_grads = in_rep_order(
-        [d_up_bias[k * unit_cols : (k + 1) * unit_cols] for k in range(reps)], 0
-    )
+    up_grads = in_rep_order(d_up_bias, 0)
     packed = jnp.concatenate(
         [feature_grads.reshape(-1), qv_grads.reshape(-1), up_grads]
     ).reshape(-1, 128)
@@ -528,7 +536,15 @@
         packed[size_f + size_q :].reshape(-1, HD), z * unit_lanes, unit_lanes, 1
     )
 
-    d_qkv = in_rep_order([g.reshape(part, 3, q_cols) for g in grad_qkv], 2)
+    d_out, d_up = in_rep_order(grad_out, 0), in_rep_order(grad_up, 1)
+    d_down = in_rep_order(grad_down, 0)
+    d_qkv = jnp.concatenate(
+        [
+            in_rep_order([g.reshape(part, 2, q_cols) for g in grad_pair], 2),
+            in_rep_order([g.reshape(part, 1, q_cols) for g in grad_value], 2),
+        ],
+        axis=1,
+    )
     return (
         block_out,
         tokens_grad,
@@ -536,10 +552,10 @@
         feature_grads[1][None],
         d_qkv[None],
         qv_grads[None],
-        in_rep_order(grad_out, 0)[None],
-        in_rep_order(grad_up, 1)[None],
+        d_out[None],
+        d_up[None],
         up_grads[None],
-        in_rep_order(grad_down, 0)[None],
+        d_down[None],
         feature_grads[2][None],
         feature_grads[3][None],
     )

time: 569 us -> 547 us (0.961)
  waiting for transfers between devices: 318 us -> 278 us
  starting transfers between devices: 81.4 us -> 100 us
  other arithmetic: 42 us -> 49.8 us
    ppermute x39 -> x42, waiting for transfers between devices: 157 us -> 129 us  [z_pull(): return lax.ppermute(x, 'fsdp', [((j + s) % n, j) for j in range(n)])]
    ppermute x12 -> x14, waiting for transfers between devices: 129 us -> 104 us  [y_pull(): lax.ppermute(x, 'rep', [((a + d) % ys * 2 + c, a * 2 + c) for a in range(...]
    ppermute x39 -> x42, starting transfers between devices: 61.1 us -> 77.1 us  [z_pull(): return lax.ppermute(x, 'fsdp', [((j + s) % n, j) for j in range(n)])]
    ppermute x5, waiting for transfers between devices: 32.6 us -> 43.7 us  [tp_swap(): return lax.ppermute(x, 'tp', [(0, 1), (1, 0)])]
    dot_general x8 -> x10, matrix products: 23.4 us -> 20.2 us  [dot_tn(): lax.dot_general(a, b, (((0,), (0,)), ((), ())), preferred_element_type=F32)]
    ppermute x12 -> x14, starting transfers between devices: 12 us -> 15 us  [y_pull(): lax.ppermute(x, 'rep', [((a + d) % ys * 2 + c, a * 2 + c) for a in range(...]
    unnamed x157 -> x180, local copies, waits for them, and re-layouts: 15.5 us -> 12.8 us
  transfers between devices with their start and end apart: 75 -> 83, of which waited for: 30 -> 36; matrix products, arithmetic and copies ran while one was open for 20% -> 20% of each run, Pallas kernels for 6% -> 6%
where the time goes in v4:
time: 547 us; the launch traced here: 539 us
  waiting for transfers between devices  278 us (51%)
  starting transfers between devices  100 us (18%)
  other arithmetic  49.8 us (9%)
  matrix products  39.5 us (7%)
  local copies, waits for them, and re-layouts  36.2 us (7%)
  Pallas kernels  31.6 us (6%)
    ppermute x42, waiting for transfers between devices, z_pull(): return lax.ppermute(x, 'fsdp', [((j + s) % n, j) for j in range(n)])  129 us
    ppermute x14, waiting for transfers between devices, y_pull(): lax.ppermute(x, 'rep', [((a + d) % ys * 2 + c, a * 2 + c) for a in range(...  104 us
    ppermute x42, starting transfers between devices, z_pull(): return lax.ppermute(x, 'fsdp', [((j + s) % n, j) for j in range(n)])  77.1 us
    ppermute x5, waiting for transfers between devices, tp_swap(): return lax.ppermute(x, 'tp', [(0, 1), (1, 0)])  43.7 us
    dot_general x10, matrix products, dot_tn(): lax.dot_general(a, b, (((0,), (0,)), ((), ())), preferred_element_type=F32)  20.2 us
    pallas_call x1, Pallas kernels, attend_backward(): pl.pallas_call(functools.partial(backward_kernel, heads), out_shape=(jax....  15.9 us
    pallas_call x1, Pallas kernels, attend_forward(): pl.pallas_call(functools.partial(forward_kernel, heads), out_shape=(jax.S...  15.7 us
    ppermute x14, starting transfers between devices, y_pull(): lax.ppermute(x, 'rep', [((a + d) % ys * 2 + c, a * 2 + c) for a in range(...  15 us
  transfers between devices with their start and end apart: 83, of which 36 were waited for; matrix products, arithmetic and copies ran while one was open for 20% of the time, Pallas kernels for 6%

profile of v4, /device:TPU:0, one launch (start us, length us, event | category | flops | bytes accessed | tf_op | source)
XLA Modules:
  0.0 539.1 jit_solution(9457984094379759146)
XLA Ops:
  5.1 3.1 collective-permute-start.2
  8.2 2.6 collective-permute-start.1
  18.3 2.9 collective-permute-start.3
  29.2 3.0 collective-permute-start.16
  35.9 9.8 %collective-permute-done.16 = bf16[256,640]{1,0:T(8,128)(2,1)S(1)} collective-permute-done((bf16[256,640]{1,0:T(8,128)(2,1)S(1)}, bf16[256,640]{1,0:T(8,128)(2,1)S(1)}, u32[]{:S(2)}, u32[]{:S(2)}) %collective-permute-start.16) | collective-permute-done | bytes 327712 | tf_op jit(solution)/shard_map/ppermute | solution.py:238
  45.8 16.4 %collective-permute-done.17 = bf16[256,640]{1,0:T(8,128)(2,1)S(1)} collective-permute-done((bf16[256,640]{1,0:T(8,128)(2,1)S(1)}, bf16[256,640]{1,0:T(8,128)(2,1)S(1)}, u32[]{:S(2)}, u32[]{:S(2)}) %collective-permute-start.17) | collective-permute-done | bytes 327712 | tf_op jit(solution)/shard_map/ppermute | solution.py:238
  64.5 4.7 collective-permute-done.19
  77.4 3.2 collective-permute-start.10
  81.4 7.3 %collective-permute-done.11 = bf16[352,384]{1,0:T(8,128)(2,1)S(1)} collective-permute-done((bf16[352,384]{1,0:T(8,128)(2,1)S(1)}, bf16[352,384]{1,0:T(8,128)(2,1)S(1)}, u32[]{:S(2)}, u32[]{:S(2)}) %collective-permute-start.11) | collective-permute-done | bytes 270368 | tf_op jit(solution)/shard_map/ppermute | solution.py:238
  88.7 10.8 %collective-permute-done.10 = bf16[352,384]{1,0:T(8,128)(2,1)S(1)} collective-permute-done((bf16[352,384]{1,0:T(8,128)(2,1)S(1)}, bf16[352,384]{1,0:T(8,128)(2,1)S(1)}, u32[]{:S(2)}, u32[]{:S(2)}) %collective-permute-start.10) | collective-permute-done | bytes 270368 | tf_op jit(solution)/shard_map/ppermute | solution.py:238
  100.7 15.7 %attend_forward.1 = (bf16[1408,128]{1,0:T(8,128)(2,1)}, f32[11,1,256]{2,1,0:T(1,128)}) custom-call(bf16[1408,384]{1,0:T(8,128)(2,1)} %pad_maximum_fusion.5.x_ref, s32[1408,128]{1,0:T(8,128)} %broadcast_in_dim.18.key_ref, s32[11,1,128]{2,1,0:T(1,128)} %and_select_fusion.seg_ref), custom_call_target="tpu_custom_call" | custom-call | flops 1015021568 | bytes 1441792 | tf_op jit(solution)/shard_map/attend_forward/pallas_call | solution.py:162
  117.4 4.4 collective-permute-start.12
  125.9 14.6 %collective-permute-start.25 = (bf16[512,256]{1,0:T(8,128)(2,1)}, bf16[512,256]{1,0:T(8,128)(2,1)S(1)}, u32[]{:S(2)}, u32[]{:S(2)}) collective-permute-start(bf16[512,256]{1,0:T(8,128)(2,1)} %dynamic-slice_bitcast_fusion.8), channel_id=1, source_target_pairs={{6,0},{0,2},{2,4},{4,6},{7,1},{1,3},{3,5},{5,7},{14,8},{8,10},{10,... | collective-permute-start | bytes 786440 | tf_op jit(solution)/shard_map/ppermute | solution.py:238
  144.3 7.6 %collective-permute-done.23 = bf16[512,256]{1,0:T(8,128)(2,1)S(1)} collective-permute-done((bf16[512,256]{1,0:T(8,128)(2,1)}, bf16[512,256]{1,0:T(8,128)(2,1)S(1)}, u32[]{:S(2)}, u32[]{:S(2)}) %collective-permute-start.23) | collective-permute-done | bytes 262176 | tf_op jit(solution)/shard_map/ppermute | solution.py:238
  160.3 18.9 %collective-permute-done.26 = bf16[512,1024]{1,0:T(8,128)(2,1)S(1)} collective-permute-done((bf16[512,1024]{1,0:T(8,128)(2,1)S(1)}, bf16[512,1024]{1,0:T(8,128)(2,1)S(1)}, u32[]{:S(2)}, u32[]{:S(2)}) %collective-permute-start.26) | collective-permute-done | bytes 1048608 | tf_op jit(solution)/shard_map/ppermute | solution.py:244
  179.3 2.1 fusion.134
  199.7 29.1 %collective-permute-done.29 = f32[352,1024]{1,0:T(8,128)S(1)} collective-permute-done((f32[352,1024]{1,0:T(8,128)S(1)}, f32[352,1024]{1,0:T(8,128)S(1)}, u32[]{:S(2)}, u32[]{:S(2)}) %collective-permute-start.29) | collective-permute-done | bytes 1441824 | tf_op jit(solution)/shard_map/ppermute | solution.py:283
  233.0 3.4 collective-permute-start.33
  236.4 2.3 collective-permute-start.32
  239.0 3.3 fusion.55
  245.5 15.9 %attend_backward.1 = (bf16[1408,384]{1,0:T(8,128)(2,1)}, f32[2,128]{1,0:T(2,128)}) custom-call(bf16[1408,384]{1,0:T(8,128)(2,1)} %pad_maximum_fusion.5.x_ref, bf16[1408,128]{1,0:T(8,128)(2,1)} %get-tuple-element.39.o_ref, bf16[1408,128]{1,0:T(8,128)(2,1)} %pad_maximum_fusion.14.g_ref, f32[11,1,256]{2,1,0:T(1,128)} %get-tuple-element.43.lse_ref, ...), custom_call_target="tpu_custom_call" | custom-call | flops 2537553920 | bytes 3604480 | tf_op jit(solution)/shard_map/attend_backward/pallas_call | solution.py:181
  262.7 2.6 collective-permute-start.34
  266.2 3.4 fusion.61
  270.1 2.4 collective-permute-done.34
  272.5 6.0 %collective-permute-done.36 = bf16[352,384]{1,0:T(8,128)(2,1)S(1)} collective-permute-done((bf16[352,384]{1,0:T(8,128)(2,1)S(1)}, bf16[352,384]{1,0:T(8,128)(2,1)S(1)}, u32[]{:S(2)}, u32[]{:S(2)}) %collective-permute-start.36) | collective-permute-done | bytes 270368 | tf_op jit(solution)/shard_map/ppermute | solution.py:238
  278.5 11.4 %collective-permute-done.35 = bf16[352,384]{1,0:T(8,128)(2,1)S(1)} collective-permute-done((bf16[352,384]{1,0:T(8,128)(2,1)S(1)}, bf16[352,384]{1,0:T(8,128)(2,1)S(1)}, u32[]{:S(2)}, u32[]{:S(2)}) %collective-permute-start.35) | collective-permute-done | bytes 270368 | tf_op jit(solution)/shard_map/ppermute | solution.py:238
  294.0 6.0 %collective-permute-done.60 = bf16[128,1024]{1,0:T(8,128)(2,1)S(1)} collective-permute-done((bf16[128,1024]{1,0:T(8,128)(2,1)S(1)}, bf16[128,1024]{1,0:T(8,128)(2,1)S(1)}, u32[]{:S(2)}, u32[]{:S(2)}) %collective-permute-start.60) | collective-permute-done | bytes 262176 | tf_op jit(solution)/shard_map/ppermute | solution.py:244
  300.2 3.8 collective-permute-start.63
  306.2 2.9 collective-permute-done.62
  315.1 2.7 collective-permute-done.52
  320.3 4.1 collective-permute-start.55
  328.6 5.5 %collective-permute-done.54 = f32[256,128]{0,1:T(8,128)S(1)} collective-permute-done((f32[256,128]{0,1:T(8,128)S(1)}, f32[256,128]{0,1:T(8,128)S(1)}, u32[]{:S(2)}, u32[]{:S(2)}) %collective-permute-start.54) | collective-permute-done | bytes 131104 | tf_op jit(solution)/shard_map/ppermute | solution.py:238
  334.3 9.9 %collective-permute-done.37 = f32[352,1024]{1,0:T(8,128)S(1)} collective-permute-done((f32[352,1024]{1,0:T(8,128)S(1)}, f32[352,1024]{1,0:T(8,128)S(1)}, u32[]{:S(2)}, u32[]{:S(2)}) %collective-permute-start.37) | collective-permute-done | bytes 1441824 | tf_op jit(solution)/shard_map/ppermute | solution.py:283
  345.4 3.9 fusion.13
  349.5 2.3 fusion.12
  355.5 2.5 convolution_add_fusion.3
  359.0 3.5 convolution_add_fusion.1
  366.3 3.5 convolution_add_fusion.2
  380.3 2.7 collective-permute-start.40
  389.6 28.2 %collective-permute-done.76 = f32[512,1024]{1,0:T(8,128)S(1)} collective-permute-done((f32[512,1024]{1,0:T(8,128)}, f32[512,1024]{1,0:T(8,128)S(1)}, u32[]{:S(2)}, u32[]{:S(2)}) %collective-permute-start.76) | collective-permute-done | bytes 2097184 | tf_op jit(solution)/shard_map/ppermute | solution.py:244
  420.8 42.4 %collective-permute-done.43 = f32[88,128]{1,0:T(8,128)S(1)} collective-permute-done((f32[88,128]{1,0:T(8,128)S(1)}, f32[88,128]{1,0:T(8,128)S(1)}, u32[]{:S(2)}, u32[]{:S(2)}) %collective-permute-start.43) | collective-permute-done | bytes 45088 | tf_op jit(solution)/shard_map/ppermute | solution.py:244
  463.2 3.8 collective-permute-start.79
  467.2 6.9 %collective-permute-done.77 = bf16[512,256]{1,0:T(8,128)(2,1)S(1)} collective-permute-done((bf16[512,256]{1,0:T(8,128)(2,1)S(1)}, bf16[512,256]{1,0:T(8,128)(2,1)S(1)}, u32[]{:S(2)}, u32[]{:S(2)}) %collective-permute-start.77) | collective-permute-done | bytes 262176 | tf_op jit(solution)/shard_map/ppermute | solution.py:238
  476.8 12.4 %collective-permute-done.78 = bf16[512,256]{1,0:T(8,128)(2,1)S(1)} collective-permute-done((bf16[512,256]{1,0:T(8,128)(2,1)S(1)}, bf16[512,256]{1,0:T(8,128)(2,1)S(1)}, u32[]{:S(2)}, u32[]{:S(2)}) %collective-permute-start.78) | collective-permute-done | bytes 262176 | tf_op jit(solution)/shard_map/ppermute | solution.py:238
  494.0 4.1 collective-permute-start.71
  505.2 4.2 collective-permute-done.71
  509.4 8.7 %collective-permute-done.70 = bf16[256,512]{0,1:T(8,128)(2,1)} collective-permute-done((bf16[256,512]{0,1:T(8,128)(2,1)}, bf16[256,512]{0,1:T(8,128)(2,1)}, u32[]{:S(2)}, u32[]{:S(2)}) %collective-permute-start.70) | collective-permute-done | bytes 262176 | tf_op jit(solution)/shard_map/ppermute | solution.py:238
  525.7 6.2 %collective-permute-done.72 = f32[256,512]{0,1:T(8,128)S(1)} collective-permute-done((f32[256,512]{0,1:T(8,128)}, f32[256,512]{0,1:T(8,128)S(1)}, u32[]{:S(2)}, u32[]{:S(2)}) %collective-permute-start.72) | collective-permute-done | bytes 524320 | tf_op jit(solution)/shard_map/ppermute | solution.py:244
  (507 shorter events, 158.4 us)
Async XLA Ops:
  5.1 13.2 %collective-permute-start.2 = (bf16[13,256]{1,0:T(8,128)(2,1)S(1)}, bf16[13,256]{1,0:T(8,128)(2,1)S(1)}, u32[]{:S(2)}, u32[]{:S(2)}) collective-permute-start(bf16[13,256]{1,0:T(8,128)(2,1)S(1)} %concatenate.157), channel_id=1, source_target_pairs={{6,0},{0,2},{2,4},{4,6},{7,1},{1,3},{3,5},{5,7},{14,8},{8,10},{10,... | collective-permute-start | bytes 19976 | tf_op jit(solution)/shard_map/ppermute | solution.py:238
  8.2 13.0 %collective-permute-start.1 = (bf16[13,256]{1,0:T(8,128)(2,1)S(1)}, bf16[13,256]{1,0:T(8,128)(2,1)S(1)}, u32[]{:S(2)}, u32[]{:S(2)}) collective-permute-start(bf16[13,256]{1,0:T(8,128)(2,1)S(1)} %concatenate.157), channel_id=1, source_target_pairs={{4,0},{6,2},{0,4},{2,6},{5,1},{7,3},{1,5},{3,7},{12,8},{14,10},{8,... | collective-permute-start | bytes 19976 | tf_op jit(solution)/shard_map/ppermute | solution.py:238
  12.2 15.1 %collective-permute-start.5 = (bf16[256,384]{0,1:T(8,128)(2,1)S(1)}, bf16[256,384]{0,1:T(8,128)(2,1)S(1)}, u32[]{:S(2)}, u32[]{:S(2)}) collective-permute-start(bf16[256,384]{0,1:T(8,128)(2,1)S(1)} %bitcast.232), channel_id=1, source_target_pairs={{6,0},{0,2},{2,4},{4,6},{7,1},{1,3},{3,5},{5,7},{14,8},{8,10},{10,... | collective-permute-start | bytes 589832 | tf_op jit(solution)/shard_map/ppermute | solution.py:238
  12.8 15.5 %collective-permute-start.4 = (bf16[256,384]{0,1:T(8,128)(2,1)S(1)}, bf16[256,384]{0,1:T(8,128)(2,1)S(1)}, u32[]{:S(2)}, u32[]{:S(2)}) collective-permute-start(bf16[256,384]{0,1:T(8,128)(2,1)S(1)} %bitcast.233), channel_id=1, source_target_pairs={{4,0},{6,2},{0,4},{2,6},{5,1},{7,3},{1,5},{3,7},{12,8},{14,10},{8,... | collective-permute-start | bytes 589832 | tf_op jit(solution)/shard_map/ppermute | solution.py:238
  29.2 16.5 %collective-permute-start.16 = (bf16[256,640]{1,0:T(8,128)(2,1)S(1)}, bf16[256,640]{1,0:T(8,128)(2,1)S(1)}, u32[]{:S(2)}, u32[]{:S(2)}) collective-permute-start(bf16[256,640]{1,0:T(8,128)(2,1)S(1)} %pad_maximum_fusion.15), channel_id=1, source_target_pairs={{2,0},{4,2},{6,4},{0,6},{3,1},{5,3},{7,5},{1,7},{10,8},{12,10},{14... | collective-permute-start | bytes 983048 | tf_op jit(solution)/shard_map/ppermute | solution.py:238
  32.3 29.9 %collective-permute-start.18 = (bf16[256,640]{1,0:T(8,128)(2,1)S(1)}, bf16[256,640]{1,0:T(8,128)(2,1)S(1)}, u32[]{:S(2)}, u32[]{:S(2)}) collective-permute-start(bf16[256,640]{1,0:T(8,128)(2,1)S(1)} %pad_maximum_fusion.15), channel_id=1, source_target_pairs={{6,0},{0,2},{2,4},{4,6},{7,1},{1,3},{3,5},{5,7},{14,8},{8,10},{10,... | collective-permute-start | bytes 983048 | tf_op jit(solution)/shard_map/ppermute | solution.py:238
  32.6 29.6 %collective-permute-start.17 = (bf16[256,640]{1,0:T(8,128)(2,1)S(1)}, bf16[256,640]{1,0:T(8,128)(2,1)S(1)}, u32[]{:S(2)}, u32[]{:S(2)}) collective-permute-start(bf16[256,640]{1,0:T(8,128)(2,1)S(1)} %pad_maximum_fusion.15), channel_id=1, source_target_pairs={{4,0},{6,2},{0,4},{2,6},{5,1},{7,3},{1,5},{3,7},{12,8},{14,10},{8,... | collective-permute-start | bytes 983048 | tf_op jit(solution)/shard_map/ppermute | solution.py:238
  34.2 40.8 %collective-permute-start.7 = (bf16[1024,384]{0,1:T(8,128)(2,1)S(1)}, bf16[1024,384]{0,1:T(8,128)(2,1)S(1)}, u32[]{:S(2)}, u32[]{:S(2)}) collective-permute-start(bf16[1024,384]{0,1:T(8,128)(2,1)S(1)} %pad_maximum_fusion.7), channel_id=1, source_target_pairs={{0,8},{8,0},{16,24},{24,16},{1,9},{9,1},{17,25},{25,17},{2,10},{10... | collective-permute-start | bytes 2359304 | tf_op jit(solution)/shard_map/ppermute | solution.py:252
  34.3 39.9 %collective-permute-start.6 = (bf16[1024,384]{0,1:T(8,128)(2,1)S(1)}, bf16[1024,384]{0,1:T(8,128)(2,1)S(1)}, u32[]{:S(2)}, u32[]{:S(2)}) collective-permute-start(bf16[1024,384]{0,1:T(8,128)(2,1)S(1)} %pad_maximum_fusion.7), channel_id=1, source_target_pairs={{16,0},{24,8},{0,16},{8,24},{17,1},{25,9},{1,17},{9,25},{18,2},{26... | collective-permute-start | bytes 2359304 | tf_op jit(solution)/shard_map/ppermute | solution.py:244
  71.2 83.4 %collective-permute-start.21 = (bf16[1024,768]{1,0:T(8,128)(2,1)}, bf16[1024,768]{1,0:T(8,128)(2,1)}, u32[]{:S(2)}, u32[]{:S(2)}) collective-permute-start(bf16[1024,768]{1,0:T(8,128)(2,1)} %pad_maximum_fusion.3), channel_id=1, source_target_pairs={{0,8},{8,0},{16,24},{24,16},{1,9},{9,1},{17,25},{25,17},{2,10},{10... | collective-permute-start | bytes 4718600 | tf_op jit(solution)/shard_map/ppermute | solution.py:252
  71.2 85.8 %collective-permute-start.20 = (bf16[1024,768]{1,0:T(8,128)(2,1)}, bf16[1024,768]{1,0:T(8,128)(2,1)S(1)}, u32[]{:S(2)}, u32[]{:S(2)}) collective-permute-start(bf16[1024,768]{1,0:T(8,128)(2,1)} %pad_maximum_fusion.3), channel_id=1, source_target_pairs={{16,0},{24,8},{0,16},{8,24},{17,1},{25,9},{1,17},{9,25},{18,2},{26... | collective-permute-start | bytes 4718600 | tf_op jit(solution)/shard_map/ppermute | solution.py:244
  77.4 22.1 %collective-permute-start.10 = (bf16[352,384]{1,0:T(8,128)(2,1)S(1)}, bf16[352,384]{1,0:T(8,128)(2,1)S(1)}, u32[]{:S(2)}, u32[]{:S(2)}) collective-permute-start(bf16[352,384]{1,0:T(8,128)(2,1)S(1)} %get-tuple-element.125), channel_id=1, source_target_pairs={{4,0},{6,2},{0,4},{2,6},{5,1},{7,3},{1,5},{3,7},{12,8},{14,10},{8,... | collective-permute-start | bytes 811016 | tf_op jit(solution)/shard_map/ppermute | solution.py:238
  80.6 18.9 %collective-permute-start.9 = (bf16[352,384]{1,0:T(8,128)(2,1)S(1)}, bf16[352,384]{1,0:T(8,128)(2,1)S(1)}, u32[]{:S(2)}, u32[]{:S(2)}) collective-permute-start(bf16[352,384]{1,0:T(8,128)(2,1)S(1)} %get-tuple-element.126), channel_id=1, source_target_pairs={{2,0},{4,2},{6,4},{0,6},{3,1},{5,3},{7,5},{1,7},{10,8},{12,10},{14... | collective-permute-start | bytes 811016 | tf_op jit(solution)/shard_map/ppermute | solution.py:238
  121.8 18.7 %collective-permute-start.14 = (bf16[352,128]{1,0:T(8,128)(2,1)S(1)}, bf16[352,128]{1,0:T(8,128)(2,1)S(1)}, u32[]{:S(2)}, u32[]{:S(2)}) collective-permute-start(bf16[352,128]{1,0:T(8,128)(2,1)S(1)} %get-tuple-element.166), channel_id=1, source_target_pairs={{6,0},{0,2},{2,4},{4,6},{7,1},{1,3},{3,5},{5,7},{14,8},{8,10},{10,... | collective-permute-start | bytes 270344 | tf_op jit(solution)/shard_map/ppermute | solution.py:238
  123.2 18.7 %collective-permute-start.13 = (bf16[352,128]{1,0:T(8,128)(2,1)S(1)}, bf16[352,128]{1,0:T(8,128)(2,1)S(1)}, u32[]{:S(2)}, u32[]{:S(2)}) collective-permute-start(bf16[352,128]{1,0:T(8,128)(2,1)S(1)} %get-tuple-element.167), channel_id=1, source_target_pairs={{4,0},{6,2},{0,4},{2,6},{5,1},{7,3},{1,5},{3,7},{12,8},{14,10},{8,... | collective-permute-start | bytes 270344 | tf_op jit(solution)/shard_map/ppermute | solution.py:238
  125.9 27.6 %collective-permute-start.25 = (bf16[512,256]{1,0:T(8,128)(2,1)}, bf16[512,256]{1,0:T(8,128)(2,1)S(1)}, u32[]{:S(2)}, u32[]{:S(2)}) collective-permute-start(bf16[512,256]{1,0:T(8,128)(2,1)} %dynamic-slice_bitcast_fusion.8), channel_id=1, source_target_pairs={{6,0},{0,2},{2,4},{4,6},{7,1},{1,3},{3,5},{5,7},{14,8},{8,10},{10,... | collective-permute-start | bytes 786440 | tf_op jit(solution)/shard_map/ppermute | solution.py:238
  140.5 13.0 %collective-permute-start.24 = (bf16[512,256]{1,0:T(8,128)(2,1)}, bf16[512,256]{1,0:T(8,128)(2,1)S(1)}, u32[]{:S(2)}, u32[]{:S(2)}) collective-permute-start(bf16[512,256]{1,0:T(8,128)(2,1)} %dynamic-slice_bitcast_fusion.8), channel_id=1, source_target_pairs={{4,0},{6,2},{0,4},{2,6},{5,1},{7,3},{1,5},{3,7},{12,8},{14,10},{8,... | collective-permute-start | bytes 786440 | tf_op jit(solution)/shard_map/ppermute | solution.py:238
  153.5 35.9 %collective-permute-start.27 = (bf16[512,1024]{1,0:T(8,128)(2,1)S(1)}, bf16[512,1024]{1,0:T(8,128)(2,1)S(1)}, u32[]{:S(2)}, u32[]{:S(2)}) collective-permute-start(bf16[512,1024]{1,0:T(8,128)(2,1)S(1)} %constant_dynamic-update-slice_fusion.14), channel_id=1, source_target_pairs={{0,8},{8,0},{16,24},{24,16},{1,9},{9,1},{17,25},{25,17},{2,10},{10... | collective-permute-start | bytes 3145736 | tf_op jit(solution)/shard_map/ppermute | solution.py:252
  153.6 25.6 %collective-permute-start.26 = (bf16[512,1024]{1,0:T(8,128)(2,1)S(1)}, bf16[512,1024]{1,0:T(8,128)(2,1)S(1)}, u32[]{:S(2)}, u32[]{:S(2)}) collective-permute-start(bf16[512,1024]{1,0:T(8,128)(2,1)S(1)} %constant_dynamic-update-slice_fusion.14), channel_id=1, source_target_pairs={{16,0},{24,8},{0,16},{8,24},{17,1},{25,9},{1,17},{9,25},{18,2},{26... | collective-permute-start | bytes 3145736 | tf_op jit(solution)/shard_map/ppermute | solution.py:244
  157.1 22.0 %collective-permute-start.22 = (bf16[1024,768]{1,0:T(8,128)(2,1)S(1)}, bf16[1024,768]{1,0:T(8,128)(2,1)S(1)}, u32[]{:S(2)}, u32[]{:S(2)}) collective-permute-start(bf16[1024,768]{1,0:T(8,128)(2,1)S(1)} %collective-permute-done.20), channel_id=1, source_target_pairs={{0,8},{8,0},{16,24},{24,16},{1,9},{9,1},{17,25},{25,17},{2,10},{10... | collective-permute-start | bytes 4718600 | tf_op jit(solution)/shard_map/ppermute | solution.py:252
  194.3 34.5 %collective-permute-start.29 = (f32[352,1024]{1,0:T(8,128)S(1)}, f32[352,1024]{1,0:T(8,128)S(1)}, u32[]{:S(2)}, u32[]{:S(2)}) collective-permute-start(f32[352,1024]{1,0:T(8,128)S(1)} %fusion.16), channel_id=1, source_target_pairs={{0,1},{1,0},{2,3},{3,2},{4,5},{5,4},{6,7},{7,6},{8,9},{9,8},{10,11... | collective-permute-start | bytes 4325384 | tf_op jit(solution)/shard_map/ppermute | solution.py:283
  198.2 71.8 %collective-permute-start.30 = (f32[352,1024]{1,0:T(8,128)}, f32[352,1024]{1,0:T(8,128)}, u32[]{:S(2)}, u32[]{:S(2)}) collective-permute-start(f32[352,1024]{1,0:T(8,128)} %convolution_add_fusion.4), channel_id=1, source_target_pairs={{0,1},{1,0},{2,3},{3,2},{4,5},{5,4},{6,7},{7,6},{8,9},{9,8},{10,11... | collective-permute-start | bytes 4325384 | tf_op jit(solution)/shard_map/ppermute | solution.py:283
  242.3 116.6 %collective-permute-start.75 = (f32[1024,1024]{1,0:T(8,128)}, f32[1024,1024]{1,0:T(8,128)}, u32[]{:S(2)}, u32[]{:S(2)}) collective-permute-start(f32[1024,1024]{1,0:T(8,128)} %fusion.55), channel_id=1, source_target_pairs={{0,8},{8,0},{16,24},{24,16},{1,9},{9,1},{17,25},{25,17},{2,10},{10... | collective-permute-start | bytes 12582920 | tf_op jit(solution)/shard_map/ppermute | solution.py:252
  265.3 13.2 %collective-permute-start.36 = (bf16[352,384]{1,0:T(8,128)(2,1)S(1)}, bf16[352,384]{1,0:T(8,128)(2,1)S(1)}, u32[]{:S(2)}, u32[]{:S(2)}) collective-permute-start(bf16[352,384]{1,0:T(8,128)(2,1)S(1)} %get-tuple-element.121), channel_id=1, source_target_pairs={{6,0},{0,2},{2,4},{4,6},{7,1},{1,3},{3,5},{5,7},{14,8},{8,10},{10,... | collective-permute-start | bytes 811016 | tf_op jit(solution)/shard_map/ppermute | solution.py:238
  265.3 24.6 %collective-permute-start.35 = (bf16[352,384]{1,0:T(8,128)(2,1)S(1)}, bf16[352,384]{1,0:T(8,128)(2,1)S(1)}, u32[]{:S(2)}, u32[]{:S(2)}) collective-permute-start(bf16[352,384]{1,0:T(8,128)(2,1)S(1)} %get-tuple-element.122), channel_id=1, source_target_pairs={{4,0},{6,2},{0,4},{2,6},{5,1},{7,3},{1,5},{3,7},{12,8},{14,10},{8,... | collective-permute-start | bytes 811016 | tf_op jit(solution)/shard_map/ppermute | solution.py:238
  270.0 21.9 %collective-permute-start.59 = (f32[256,1024]{1,0:T(8,128)S(1)}, f32[256,1024]{1,0:T(8,128)S(1)}, u32[]{:S(2)}, u32[]{:S(2)}) collective-permute-start(f32[256,1024]{1,0:T(8,128)S(1)} %fusion.94), channel_id=1, source_target_pairs={{0,8},{8,0},{16,24},{24,16},{1,9},{9,1},{17,25},{25,17},{2,10},{10... | collective-permute-start | bytes 3145736 | tf_op jit(solution)/shard_map/ppermute | solution.py:252
  293.9 16.2 %collective-permute-start.51 = (f32[1024,256]{0,1:T(8,128)S(1)}, f32[1024,256]{0,1:T(8,128)S(1)}, u32[]{:S(2)}, u32[]{:S(2)}) collective-permute-start(f32[1024,256]{0,1:T(8,128)S(1)} %fusion.87), channel_id=1, source_target_pairs={{0,8},{8,0},{16,24},{24,16},{1,9},{9,1},{17,25},{25,17},{2,10},{10... | collective-permute-start | bytes 3145736 | tf_op jit(solution)/shard_map/ppermute | solution.py:252
  306.2 60.1 %collective-permute-start.67 = (f32[1024,1024]{0,1:T(8,128)}, f32[1024,1024]{0,1:T(8,128)}, u32[]{:S(2)}, u32[]{:S(2)}) collective-permute-start(f32[1024,1024]{0,1:T(8,128)} %fusion.61), channel_id=1, source_target_pairs={{0,8},{8,0},{16,24},{24,16},{1,9},{9,1},{17,25},{25,17},{2,10},{10... | collective-permute-start | bytes 12582920 | tf_op jit(solution)/shard_map/ppermute | solution.py:252
  313.3 30.9 %collective-permute-start.37 = (f32[352,1024]{1,0:T(8,128)S(1)}, f32[352,1024]{1,0:T(8,128)S(1)}, u32[]{:S(2)}, u32[]{:S(2)}) collective-permute-start(f32[352,1024]{1,0:T(8,128)S(1)} %fusion.149), channel_id=1, source_target_pairs={{0,1},{1,0},{2,3},{3,2},{4,5},{5,4},{6,7},{7,6},{8,9},{9,8},{10,11... | collective-permute-start | bytes 4325384 | tf_op jit(solution)/shard_map/ppermute | solution.py:283
  328.6 26.9 %collective-permute-start.38 = (f32[1024,512]{0,1:T(8,128)}, f32[1024,512]{0,1:T(8,128)}, u32[]{:S(2)}, u32[]{:S(2)}) collective-permute-start(f32[1024,512]{0,1:T(8,128)} %fusion.72), channel_id=1, source_target_pairs={{0,8},{8,0},{16,24},{24,16},{1,9},{9,1},{17,25},{25,17},{2,10},{10... | collective-permute-start | bytes 6291464 | tf_op jit(solution)/shard_map/ppermute | solution.py:252
  334.2 20.3 %collective-permute-start.57 = (f32[256,128]{0,1:T(8,128)S(1)}, f32[256,128]{0,1:T(8,128)S(1)}, u32[]{:S(2)}, u32[]{:S(2)}) collective-permute-start(f32[256,128]{0,1:T(8,128)S(1)} %fusion.101), channel_id=1, source_target_pairs={{0,8},{8,0},{16,24},{24,16},{1,9},{9,1},{17,25},{25,17},{2,10},{10... | collective-permute-start | bytes 393224 | tf_op jit(solution)/shard_map/ppermute | solution.py:252
  358.0 15.5 %collective-permute-start.39 = (bf16[1024,256]{0,1:T(8,128)(2,1)S(1)}, bf16[1024,256]{0,1:T(8,128)(2,1)S(1)}, u32[]{:S(2)}, u32[]{:S(2)}) collective-permute-start(bf16[1024,256]{0,1:T(8,128)(2,1)S(1)} %slice.817), channel_id=1, source_target_pairs={{16,0},{24,8},{0,16},{8,24},{17,1},{25,9},{1,17},{9,25},{18,2},{26... | collective-permute-start | bytes 1572872 | tf_op jit(solution)/shard_map/ppermute | solution.py:244
  365.2 52.6 %collective-permute-start.76 = (f32[512,1024]{1,0:T(8,128)}, f32[512,1024]{1,0:T(8,128)S(1)}, u32[]{:S(2)}, u32[]{:S(2)}) collective-permute-start(f32[512,1024]{1,0:T(8,128)} %slice.682), channel_id=1, source_target_pairs={{16,0},{24,8},{0,16},{8,24},{17,1},{25,9},{1,17},{9,25},{18,2},{26... | collective-permute-start | bytes 6291464 | tf_op jit(solution)/shard_map/ppermute | solution.py:244
  372.5 118.4 %collective-permute-start.68 = (f32[1024,512]{0,1:T(8,128)}, f32[1024,512]{0,1:T(8,128)}, u32[]{:S(2)}, u32[]{:S(2)}) collective-permute-start(f32[1024,512]{0,1:T(8,128)} %slice.673), channel_id=1, source_target_pairs={{16,0},{24,8},{0,16},{8,24},{17,1},{25,9},{1,17},{9,25},{18,2},{26... | collective-permute-start | bytes 6291464 | tf_op jit(solution)/shard_map/ppermute | solution.py:244
  385.2 78.0 %collective-permute-start.45 = (f32[256,256]{0,1:T(8,128)S(1)}, f32[256,256]{0,1:T(8,128)S(1)}, u32[]{:S(2)}, u32[]{:S(2)}) collective-permute-start(f32[256,256]{0,1:T(8,128)S(1)} %get-tuple-element.137), channel_id=1, source_target_pairs={{6,0},{0,2},{2,4},{4,6},{7,1},{1,3},{3,5},{5,7},{14,8},{8,10},{10,... | collective-permute-start | bytes 786440 | tf_op jit(solution)/shard_map/ppermute | solution.py:238
  387.0 80.0 %collective-permute-start.47 = (f32[256,256]{0,1:T(8,128)S(1)}, f32[256,256]{0,1:T(8,128)S(1)}, u32[]{:S(2)}, u32[]{:S(2)}) collective-permute-start(f32[256,256]{0,1:T(8,128)S(1)} %get-tuple-element.138), channel_id=1, source_target_pairs={{2,0},{4,2},{6,4},{0,6},{3,1},{5,3},{7,5},{1,7},{10,8},{12,10},{14... | collective-permute-start | bytes 786440 | tf_op jit(solution)/shard_map/ppermute | solution.py:238
  389.1 78.0 %collective-permute-start.46 = (f32[256,256]{0,1:T(8,128)S(1)}, f32[256,256]{0,1:T(8,128)S(1)}, u32[]{:S(2)}, u32[]{:S(2)}) collective-permute-start(f32[256,256]{0,1:T(8,128)S(1)} %get-tuple-element.139), channel_id=1, source_target_pairs={{4,0},{6,2},{0,4},{2,6},{5,1},{7,3},{1,5},{3,7},{12,8},{14,10},{8,... | collective-permute-start | bytes 786440 | tf_op jit(solution)/shard_map/ppermute | solution.py:238
  417.8 45.4 %collective-permute-start.43 = (f32[88,128]{1,0:T(8,128)S(1)}, f32[88,128]{1,0:T(8,128)S(1)}, u32[]{:S(2)}, u32[]{:S(2)}) collective-permute-start(f32[88,128]{1,0:T(8,128)S(1)} %dynamic-slice_reduce_fusion), channel_id=1, source_target_pairs={{16,0},{24,8},{0,16},{8,24},{17,1},{25,9},{1,17},{9,25},{18,2},{26... | collective-permute-start | bytes 135176 | tf_op jit(solution)/shard_map/ppermute | solution.py:244
  463.2 13.6 %collective-permute-start.79 = (bf16[512,256]{1,0:T(8,128)(2,1)S(1)}, bf16[512,256]{1,0:T(8,128)(2,1)S(1)}, u32[]{:S(2)}, u32[]{:S(2)}) collective-permute-start(bf16[512,256]{1,0:T(8,128)(2,1)S(1)} %get-tuple-element.128), channel_id=1, source_target_pairs={{2,0},{4,2},{6,4},{0,6},{3,1},{5,3},{7,5},{1,7},{10,8},{12,10},{14... | collective-permute-start | bytes 786440 | tf_op jit(solution)/shard_map/ppermute | solution.py:238
  467.0 22.2 %collective-permute-start.78 = (bf16[512,256]{1,0:T(8,128)(2,1)S(1)}, bf16[512,256]{1,0:T(8,128)(2,1)S(1)}, u32[]{:S(2)}, u32[]{:S(2)}) collective-permute-start(bf16[512,256]{1,0:T(8,128)(2,1)S(1)} %get-tuple-element.129), channel_id=1, source_target_pairs={{4,0},{6,2},{0,4},{2,6},{5,1},{7,3},{1,5},{3,7},{12,8},{14,10},{8,... | collective-permute-start | bytes 786440 | tf_op jit(solution)/shard_map/ppermute | solution.py:238
  467.1 31.0 %collective-permute-start.44 = (f32[88,128]{1,0:T(8,128)S(1)}, f32[88,128]{1,0:T(8,128)S(1)}, u32[]{:S(2)}, u32[]{:S(2)}) collective-permute-start(f32[88,128]{1,0:T(8,128)S(1)} %fusion.105), channel_id=1, source_target_pairs={{0,8},{8,0},{16,24},{24,16},{1,9},{9,1},{17,25},{25,17},{2,10},{10... | collective-permute-start | bytes 135176 | tf_op jit(solution)/shard_map/ppermute | solution.py:252
  474.2 29.3 %collective-permute-start.48 = (f32[256,256]{0,1:T(8,128)S(1)}, f32[256,256]{0,1:T(8,128)}, u32[]{:S(2)}, u32[]{:S(2)}) collective-permute-start(f32[256,256]{0,1:T(8,128)S(1)} %fusion.83), channel_id=1, source_target_pairs={{16,0},{24,8},{0,16},{8,24},{17,1},{25,9},{1,17},{9,25},{18,2},{26... | collective-permute-start | bytes 786440 | tf_op jit(solution)/shard_map/ppermute | solution.py:244
  490.1 31.0 %collective-permute-start.80 = (f32[512,256]{1,0:T(8,128)}, f32[512,256]{1,0:T(8,128)}, u32[]{:S(2)}, u32[]{:S(2)}) collective-permute-start(f32[512,256]{1,0:T(8,128)} %fusion.66), channel_id=1, source_target_pairs={{16,0},{24,8},{0,16},{8,24},{17,1},{25,9},{1,17},{9,25},{18,2},{26... | collective-permute-start | bytes 1572872 | tf_op jit(solution)/shard_map/ppermute | solution.py:244
  494.0 15.4 %collective-permute-start.71 = (bf16[256,512]{0,1:T(8,128)(2,1)}, bf16[256,512]{0,1:T(8,128)(2,1)S(1)}, u32[]{:S(2)}, u32[]{:S(2)}) collective-permute-start(bf16[256,512]{0,1:T(8,128)(2,1)} %get-tuple-element.131), channel_id=1, source_target_pairs={{2,0},{4,2},{6,4},{0,6},{3,1},{5,3},{7,5},{1,7},{10,8},{12,10},{14... | collective-permute-start | bytes 786440 | tf_op jit(solution)/shard_map/ppermute | solution.py:238
  498.0 20.0 %collective-permute-start.70 = (bf16[256,512]{0,1:T(8,128)(2,1)}, bf16[256,512]{0,1:T(8,128)(2,1)}, u32[]{:S(2)}, u32[]{:S(2)}) collective-permute-start(bf16[256,512]{0,1:T(8,128)(2,1)} %get-tuple-element.132), channel_id=1, source_target_pairs={{4,0},{6,2},{0,4},{2,6},{5,1},{7,3},{1,5},{3,7},{12,8},{14,10},{8,... | collective-permute-start | bytes 786440 | tf_op jit(solution)/shard_map/ppermute | solution.py:238
  503.4 18.3 %collective-permute-start.49 = (f32[256,256]{0,1:T(8,128)S(1)}, f32[256,256]{0,1:T(8,128)S(1)}, u32[]{:S(2)}, u32[]{:S(2)}) collective-permute-start(f32[256,256]{0,1:T(8,128)S(1)} %fusion.83), channel_id=1, source_target_pairs={{0,8},{8,0},{16,24},{24,16},{1,9},{9,1},{17,25},{25,17},{2,10},{10... | collective-permute-start | bytes 786440 | tf_op jit(solution)/shard_map/ppermute | solution.py:252
  505.2 16.6 %collective-permute-start.50 = (f32[256,256]{0,1:T(8,128)}, f32[256,256]{0,1:T(8,128)S(1)}, u32[]{:S(2)}, u32[]{:S(2)}) collective-permute-start(f32[256,256]{0,1:T(8,128)} %collective-permute-done.48), channel_id=1, source_target_pairs={{0,8},{8,0},{16,24},{24,16},{1,9},{9,1},{17,25},{25,17},{2,10},{10... | collective-permute-start | bytes 786440 | tf_op jit(solution)/shard_map/ppermute | solution.py:252
  509.4 22.5 %collective-permute-start.81 = (f32[512,256]{1,0:T(8,128)}, f32[512,256]{1,0:T(8,128)}, u32[]{:S(2)}, u32[]{:S(2)}) collective-permute-start(f32[512,256]{1,0:T(8,128)} %fusion.66), channel_id=1, source_target_pairs={{0,8},{8,0},{16,24},{24,16},{1,9},{9,1},{17,25},{25,17},{2,10},{10... | collective-permute-start | bytes 1572872 | tf_op jit(solution)/shard_map/ppermute | solution.py:252
  (102 other events, 933.3 us)

commit v5 on v4

--- a/solution.py
+++ b/solution.py
@@ -472,27 +472,22 @@
 
     grad_up = scatter_z(own_up, 0, BF)
     grad_out = scatter_z(own_out, 1, BF)
-    cut = 2 * head_cols
-    d_pair = jnp.concatenate(
-        [lax.select_n((k + n - z) % n, *[v[:, :cut] for v in dx_back]) for k in range(n)], axis=1
-    )
-    d_value = jnp.concatenate(
-        [lax.select_n((k + n - z) % n, *[v[:, cut:] for v in dx_back]) for k in range(n)], axis=1
-    )
-    half_v, half_p = d_value.shape[1] // 2, d_pair.shape[1] // 2
-    value_far = dot_tn(first_in, d_value[:, half_v:])
-    pair_far = dot_tn(first_in, d_pair[:, half_p:])
-    value_near = dot_tn(first_in, d_value[:, :half_v])
-    pair_near = dot_tn(first_in, d_pair[:, :half_p])
+    cut, slot_cols = 2 * head_cols, 3 * head_cols
+    d_project = lax.optimization_barrier(
+        jnp.concatenate([lax.select_n((k + n - z) % n, *dx_back) for k in range(n)], axis=1)
+    )
+    d_slots = [d_project[:, k * slot_cols : (k + 1) * slot_cols] for k in range(n)]
+    near, far = d_slots[: n // 2], d_slots[n // 2 :]
+    value_far = dot_tn(first_in, jnp.concatenate([v[:, cut:] for v in far], axis=1))
+    pair_far = dot_tn(first_in, jnp.concatenate([v[:, :cut] for v in far], axis=1))
+    value_near = dot_tn(first_in, jnp.concatenate([v[:, cut:] for v in near], axis=1))
+    pair_near = dot_tn(first_in, jnp.concatenate([v[:, :cut] for v in near], axis=1))
     own_value = sum_rep(value_near, value_far, 1)
     own_pair = sum_rep(pair_near, pair_far, 1)
     grad_value = scatter_z(own_value, 0)
     grad_pair = scatter_z(own_pair, 0)
-    w_pair = jnp.concatenate([w[:, :cut] for w in slots_qkv], axis=1)
-    w_value = jnp.concatenate([w[:, cut:] for w in slots_qkv], axis=1)
-    partial_first = dot_nt(
-        jnp.concatenate([d_pair, d_value], axis=1), jnp.concatenate([w_pair, w_value], axis=1)
-    )
+    w_qkv = jnp.concatenate(slots_qkv, axis=1)
+    partial_first = dot_nt(d_project, w_qkv)
     d_first = partial_first + tp_swap(partial_first)
     d_norm_one, gain_one, shift_one = norm_backward(d_first, part_one, inv_one, gains[0])
     tokens_grad = to_plain(upstream_one + d_norm_one, 1, part)

time: 547 us -> 540 us (0.987)
  waiting for transfers between devices: 278 us -> 267 us
  starting transfers between devices: 100 us -> 91 us
  other arithmetic: 49.8 us -> 56 us
    ppermute x5, waiting for transfers between devices: 43.7 us -> 32.9 us  [tp_swap(): return lax.ppermute(x, 'tp', [(0, 1), (1, 0)])]
    ppermute x42, starting transfers between devices: 77.1 us -> 66.4 us  [z_pull(): return lax.ppermute(x, 'fsdp', [((j + s) % n, j) for j in range(n)])]
    unnamed x180 -> x163, local copies, waits for them, and re-layouts: 12.8 us -> 13.8 us
  transfers between devices with their start and end apart: 83 -> 83, of which waited for: 36 -> 39; matrix products, arithmetic and copies ran while one was open for 20% -> 23% of each run, Pallas kernels for 6% -> 6%
where the time goes in v5:
time: 540 us; the launch traced here: 532 us
  waiting for transfers between devices  267 us (49%)
  starting transfers between devices  91 us (17%)
  other arithmetic  56 us (10%)
  matrix products  43.8 us (8%)
  local copies, waits for them, and re-layouts  38.8 us (7%)
  Pallas kernels  31.6 us (6%)
    ppermute x42, waiting for transfers between devices, z_pull(): return lax.ppermute(x, 'fsdp', [((j + s) % n, j) for j in range(n)])  130 us
    ppermute x14, waiting for transfers between devices, y_pull(): lax.ppermute(x, 'rep', [((a + d) % ys * 2 + c, a * 2 + c) for a in range(...  104 us
    ppermute x42, starting transfers between devices, z_pull(): return lax.ppermute(x, 'fsdp', [((j + s) % n, j) for j in range(n)])  66.4 us
    ppermute x5, waiting for transfers between devices, tp_swap(): return lax.ppermute(x, 'tp', [(0, 1), (1, 0)])  32.9 us
    dot_general x10, matrix products, dot_tn(): lax.dot_general(a, b, (((0,), (0,)), ((), ())), preferred_element_type=F32)  22.9 us
    ppermute x14, starting transfers between devices, y_pull(): lax.ppermute(x, 'rep', [((a + d) % ys * 2 + c, a * 2 + c) for a in range(...  16.7 us
    pallas_call x1, Pallas kernels, attend_backward(): pl.pallas_call(functools.partial(backward_kernel, heads), out_shape=(jax....  15.9 us
    pallas_call x1, Pallas kernels, attend_forward(): pl.pallas_call(functools.partial(forward_kernel, heads), out_shape=(jax.S...  15.7 us
  transfers between devices with their start and end apart: 83, of which 39 were waited for; matrix products, arithmetic and copies ran while one was open for 23% of the time, Pallas kernels for 6%

profile of v5, /device:TPU:0, one launch (start us, length us, event | category | flops | bytes accessed | tf_op | source)
XLA Modules:
  0.0 532.1 jit_solution(9424449436836536878)
XLA Ops:
  5.1 3.1 collective-permute-start.2
  8.2 2.6 collective-permute-start.1
  18.3 2.9 collective-permute-start.3
  25.5 2.8 collective-permute-done.4
  29.9 3.1 collective-permute-start.16
  38.0 3.1 collective-permute-done.16
  41.1 21.7 %collective-permute-done.17 = bf16[256,640]{1,0:T(8,128)(2,1)S(1)} collective-permute-done((bf16[256,640]{1,0:T(8,128)(2,1)S(1)}, bf16[256,640]{1,0:T(8,128)(2,1)S(1)}, u32[]{:S(2)}, u32[]{:S(2)}) %collective-permute-start.17) | collective-permute-done | bytes 327712 | tf_op jit(solution)/shard_map/ppermute | solution.py:238
  66.3 3.5 collective-permute-done.19
  74.9 2.8 collective-permute-start.9
  82.0 2.3 collective-permute-done.11
  84.2 8.5 %collective-permute-done.10 = bf16[352,384]{1,0:T(8,128)(2,1)S(1)} collective-permute-done((bf16[352,384]{1,0:T(8,128)(2,1)S(1)}, bf16[352,384]{1,0:T(8,128)(2,1)S(1)}, u32[]{:S(2)}, u32[]{:S(2)}) %collective-permute-start.10) | collective-permute-done | bytes 270368 | tf_op jit(solution)/shard_map/ppermute | solution.py:238
  93.9 15.7 %attend_forward.1 = (bf16[1408,128]{1,0:T(8,128)(2,1)}, f32[11,1,256]{2,1,0:T(1,128)}) custom-call(bf16[1408,384]{1,0:T(8,128)(2,1)} %pad_maximum_fusion.5.x_ref, s32[1408,128]{1,0:T(8,128)} %broadcast_in_dim.18.key_ref, s32[11,1,128]{2,1,0:T(1,128)} %and_select_fusion.seg_ref), custom_call_target="tpu_custom_call" | custom-call | flops 1015021568 | bytes 1441792 | tf_op jit(solution)/shard_map/attend_forward/pallas_call | solution.py:162
  110.6 7.9 %collective-permute-start.12 = (bf16[352,128]{1,0:T(8,128)(2,1)S(1)}, bf16[352,128]{1,0:T(8,128)(2,1)S(1)}, u32[]{:S(2)}, u32[]{:S(2)}) collective-permute-start(bf16[352,128]{1,0:T(8,128)(2,1)S(1)} %get-tuple-element.161), channel_id=1, source_target_pairs={{2,0},{4,2},{6,4},{0,6},{3,1},{5,3},{7,5},{1,7},{10,8},{12,10},{14... | collective-permute-start | bytes 270344 | tf_op jit(solution)/shard_map/ppermute | solution.py:238
  120.8 3.2 collective-permute-start.25
  126.4 11.8 %collective-permute-done.13 = bf16[352,128]{1,0:T(8,128)(2,1)S(1)} collective-permute-done((bf16[352,128]{1,0:T(8,128)(2,1)S(1)}, bf16[352,128]{1,0:T(8,128)(2,1)S(1)}, u32[]{:S(2)}, u32[]{:S(2)}) %collective-permute-start.13) | collective-permute-done | bytes 90144 | tf_op jit(solution)/shard_map/ppermute | solution.py:238
  139.7 9.4 %collective-permute-done.23 = bf16[512,256]{1,0:T(8,128)(2,1)S(1)} collective-permute-done((bf16[512,256]{1,0:T(8,128)(2,1)}, bf16[512,256]{1,0:T(8,128)(2,1)S(1)}, u32[]{:S(2)}, u32[]{:S(2)}) %collective-permute-start.23) | collective-permute-done | bytes 262176 | tf_op jit(solution)/shard_map/ppermute | solution.py:238
  159.8 16.5 %collective-permute-done.26 = bf16[512,1024]{1,0:T(8,128)(2,1)S(1)} collective-permute-done((bf16[512,1024]{1,0:T(8,128)(2,1)S(1)}, bf16[512,1024]{1,0:T(8,128)(2,1)S(1)}, u32[]{:S(2)}, u32[]{:S(2)}) %collective-permute-start.26) | collective-permute-done | bytes 1048608 | tf_op jit(solution)/shard_map/ppermute | solution.py:244
  177.1 3.7 fusion.149
  185.2 3.3 fusion.69
  202.5 3.6 fusion.75
  206.1 25.5 %collective-permute-done.29 = f32[352,1024]{1,0:T(8,128)S(1)} collective-permute-done((f32[352,1024]{1,0:T(8,128)S(1)}, f32[352,1024]{1,0:T(8,128)S(1)}, u32[]{:S(2)}, u32[]{:S(2)}) %collective-permute-start.29) | collective-permute-done | bytes 1441824 | tf_op jit(solution)/shard_map/ppermute | solution.py:283
  236.9 2.5 collective-permute-start.31
  242.2 2.2 collective-permute-done.32
  245.2 15.9 %attend_backward.1 = (bf16[1408,384]{1,0:T(8,128)(2,1)}, f32[2,128]{1,0:T(2,128)}) custom-call(bf16[1408,384]{1,0:T(8,128)(2,1)} %pad_maximum_fusion.5.x_ref, bf16[1408,128]{1,0:T(8,128)(2,1)} %get-tuple-element.39.o_ref, bf16[1408,128]{1,0:T(8,128)(2,1)} %pad_maximum_fusion.15.g_ref, f32[11,1,256]{2,1,0:T(1,128)} %get-tuple-element.43.lse_ref, ...), custom_call_target="tpu_custom_call" | custom-call | flops 2537553920 | bytes 3604480 | tf_op jit(solution)/shard_map/attend_backward/pallas_call | solution.py:181
  262.4 2.2 collective-permute-start.34
  265.5 4.7 multiply_reduce_fusion
  274.5 3.3 collective-permute-done.36
  277.9 10.4 %collective-permute-done.35 = bf16[352,384]{1,0:T(8,128)(2,1)S(1)} collective-permute-done((bf16[352,384]{1,0:T(8,128)(2,1)S(1)}, bf16[352,384]{1,0:T(8,128)(2,1)S(1)}, u32[]{:S(2)}, u32[]{:S(2)}) %collective-permute-start.35) | collective-permute-done | bytes 270368 | tf_op jit(solution)/shard_map/ppermute | solution.py:238
  295.6 5.2 collective-permute-done.60
  300.9 3.8 collective-permute-start.63
  311.6 5.2 collective-permute-done.64
  318.4 3.8 collective-permute-start.55
  329.8 6.2 %collective-permute-done.54 = f32[256,128]{0,1:T(8,128)S(1)} collective-permute-done((f32[256,128]{0,1:T(8,128)S(1)}, f32[256,128]{0,1:T(8,128)S(1)}, u32[]{:S(2)}, u32[]{:S(2)}) %collective-permute-start.54) | collective-permute-done | bytes 131104 | tf_op jit(solution)/shard_map/ppermute | solution.py:238
  336.2 2.3 collective-permute-done.37
  340.0 2.3 fusion.27
  349.1 2.5 convolution_add_fusion.3
  352.3 3.5 convolution_add_fusion.1
  360.0 3.5 convolution_add_fusion.2
  373.3 2.8 collective-permute-start.40
  382.8 28.7 %collective-permute-done.76 = f32[512,1024]{1,0:T(8,128)S(1)} collective-permute-done((f32[512,1024]{1,0:T(8,128)}, f32[512,1024]{1,0:T(8,128)S(1)}, u32[]{:S(2)}, u32[]{:S(2)}) %collective-permute-start.76) | collective-permute-done | bytes 2097184 | tf_op jit(solution)/shard_map/ppermute | solution.py:244
  414.2 42.6 %collective-permute-done.43 = f32[88,128]{1,0:T(8,128)S(1)} collective-permute-done((f32[88,128]{1,0:T(8,128)S(1)}, f32[88,128]{1,0:T(8,128)S(1)}, u32[]{:S(2)}, u32[]{:S(2)}) %collective-permute-start.43) | collective-permute-done | bytes 45088 | tf_op jit(solution)/shard_map/ppermute | solution.py:244
  456.8 3.8 collective-permute-start.79
  460.9 6.9 %collective-permute-done.77 = bf16[512,256]{1,0:T(8,128)(2,1)S(1)} collective-permute-done((bf16[512,256]{1,0:T(8,128)(2,1)S(1)}, bf16[512,256]{1,0:T(8,128)(2,1)S(1)}, u32[]{:S(2)}, u32[]{:S(2)}) %collective-permute-start.77) | collective-permute-done | bytes 262176 | tf_op jit(solution)/shard_map/ppermute | solution.py:238
  470.3 12.4 %collective-permute-done.78 = bf16[512,256]{1,0:T(8,128)(2,1)S(1)} collective-permute-done((bf16[512,256]{1,0:T(8,128)(2,1)S(1)}, bf16[512,256]{1,0:T(8,128)(2,1)S(1)}, u32[]{:S(2)}, u32[]{:S(2)}) %collective-permute-start.78) | collective-permute-done | bytes 262176 | tf_op jit(solution)/shard_map/ppermute | solution.py:238
  487.1 4.1 collective-permute-start.71
  498.3 4.2 collective-permute-done.71
  502.5 8.6 %collective-permute-done.70 = bf16[256,512]{0,1:T(8,128)(2,1)} collective-permute-done((bf16[256,512]{0,1:T(8,128)(2,1)}, bf16[256,512]{0,1:T(8,128)(2,1)}, u32[]{:S(2)}, u32[]{:S(2)}) %collective-permute-start.70) | collective-permute-done | bytes 262176 | tf_op jit(solution)/shard_map/ppermute | solution.py:238
  519.1 5.7 %collective-permute-done.72 = f32[256,512]{0,1:T(8,128)S(1)} collective-permute-done((f32[256,512]{0,1:T(8,128)}, f32[256,512]{0,1:T(8,128)S(1)}, u32[]{:S(2)}, u32[]{:S(2)}) %collective-permute-start.72) | collective-permute-done | bytes 524320 | tf_op jit(solution)/shard_map/ppermute | solution.py:244
  (485 shorter events, 172.1 us)
Async XLA Ops:
  5.1 13.2 %collective-permute-start.2 = (bf16[13,256]{1,0:T(8,128)(2,1)S(1)}, bf16[13,256]{1,0:T(8,128)(2,1)S(1)}, u32[]{:S(2)}, u32[]{:S(2)}) collective-permute-start(bf16[13,256]{1,0:T(8,128)(2,1)S(1)} %concatenate.154), channel_id=1, source_target_pairs={{6,0},{0,2},{2,4},{4,6},{7,1},{1,3},{3,5},{5,7},{14,8},{8,10},{10,... | collective-permute-start | bytes 19976 | tf_op jit(solution)/shard_map/ppermute | solution.py:238
  8.2 12.9 %collective-permute-start.1 = (bf16[13,256]{1,0:T(8,128)(2,1)S(1)}, bf16[13,256]{1,0:T(8,128)(2,1)S(1)}, u32[]{:S(2)}, u32[]{:S(2)}) collective-permute-start(bf16[13,256]{1,0:T(8,128)(2,1)S(1)} %concatenate.154), channel_id=1, source_target_pairs={{4,0},{6,2},{0,4},{2,6},{5,1},{7,3},{1,5},{3,7},{12,8},{14,10},{8,... | collective-permute-start | bytes 19976 | tf_op jit(solution)/shard_map/ppermute | solution.py:238
  12.2 13.3 %collective-permute-start.5 = (bf16[256,384]{0,1:T(8,128)(2,1)S(1)}, bf16[256,384]{0,1:T(8,128)(2,1)S(1)}, u32[]{:S(2)}, u32[]{:S(2)}) collective-permute-start(bf16[256,384]{0,1:T(8,128)(2,1)S(1)} %bitcast.231), channel_id=1, source_target_pairs={{6,0},{0,2},{2,4},{4,6},{7,1},{1,3},{3,5},{5,7},{14,8},{8,10},{10,... | collective-permute-start | bytes 589832 | tf_op jit(solution)/shard_map/ppermute | solution.py:238
  12.8 15.5 %collective-permute-start.4 = (bf16[256,384]{0,1:T(8,128)(2,1)S(1)}, bf16[256,384]{0,1:T(8,128)(2,1)S(1)}, u32[]{:S(2)}, u32[]{:S(2)}) collective-permute-start(bf16[256,384]{0,1:T(8,128)(2,1)S(1)} %bitcast.232), channel_id=1, source_target_pairs={{4,0},{6,2},{0,4},{2,6},{5,1},{7,3},{1,5},{3,7},{12,8},{14,10},{8,... | collective-permute-start | bytes 589832 | tf_op jit(solution)/shard_map/ppermute | solution.py:238
  34.0 31.6 %collective-permute-start.6 = (bf16[1024,384]{0,1:T(8,128)(2,1)S(1)}, bf16[1024,384]{0,1:T(8,128)(2,1)S(1)}, u32[]{:S(2)}, u32[]{:S(2)}) collective-permute-start(bf16[1024,384]{0,1:T(8,128)(2,1)S(1)} %pad_maximum_fusion.8), channel_id=1, source_target_pairs={{16,0},{24,8},{0,16},{8,24},{17,1},{25,9},{1,17},{9,25},{18,2},{26... | collective-permute-start | bytes 2359304 | tf_op jit(solution)/shard_map/ppermute | solution.py:244
  35.7 27.2 %collective-permute-start.17 = (bf16[256,640]{1,0:T(8,128)(2,1)S(1)}, bf16[256,640]{1,0:T(8,128)(2,1)S(1)}, u32[]{:S(2)}, u32[]{:S(2)}) collective-permute-start(bf16[256,640]{1,0:T(8,128)(2,1)S(1)} %pad_maximum_fusion.16), channel_id=1, source_target_pairs={{4,0},{6,2},{0,4},{2,6},{5,1},{7,3},{1,5},{3,7},{12,8},{14,10},{8,... | collective-permute-start | bytes 983048 | tf_op jit(solution)/shard_map/ppermute | solution.py:238
  38.0 24.9 %collective-permute-start.18 = (bf16[256,640]{1,0:T(8,128)(2,1)S(1)}, bf16[256,640]{1,0:T(8,128)(2,1)S(1)}, u32[]{:S(2)}, u32[]{:S(2)}) collective-permute-start(bf16[256,640]{1,0:T(8,128)(2,1)S(1)} %pad_maximum_fusion.16), channel_id=1, source_target_pairs={{6,0},{0,2},{2,4},{4,6},{7,1},{1,3},{3,5},{5,7},{14,8},{8,10},{10,... | collective-permute-start | bytes 983048 | tf_op jit(solution)/shard_map/ppermute | solution.py:238
  38.0 33.2 %collective-permute-start.7 = (bf16[1024,384]{0,1:T(8,128)(2,1)S(1)}, bf16[1024,384]{0,1:T(8,128)(2,1)S(1)}, u32[]{:S(2)}, u32[]{:S(2)}) collective-permute-start(bf16[1024,384]{0,1:T(8,128)(2,1)S(1)} %pad_maximum_fusion.8), channel_id=1, source_target_pairs={{0,8},{8,0},{16,24},{24,16},{1,9},{9,1},{17,25},{25,17},{2,10},{10... | collective-permute-start | bytes 2359304 | tf_op jit(solution)/shard_map/ppermute | solution.py:252
  73.1 19.7 %collective-permute-start.10 = (bf16[352,384]{1,0:T(8,128)(2,1)S(1)}, bf16[352,384]{1,0:T(8,128)(2,1)S(1)}, u32[]{:S(2)}, u32[]{:S(2)}) collective-permute-start(bf16[352,384]{1,0:T(8,128)(2,1)S(1)} %get-tuple-element.121), channel_id=1, source_target_pairs={{4,0},{6,2},{0,4},{2,6},{5,1},{7,3},{1,5},{3,7},{12,8},{14,10},{8,... | collective-permute-start | bytes 811016 | tf_op jit(solution)/shard_map/ppermute | solution.py:238
  74.9 17.9 %collective-permute-start.9 = (bf16[352,384]{1,0:T(8,128)(2,1)S(1)}, bf16[352,384]{1,0:T(8,128)(2,1)S(1)}, u32[]{:S(2)}, u32[]{:S(2)}) collective-permute-start(bf16[352,384]{1,0:T(8,128)(2,1)S(1)} %get-tuple-element.122), channel_id=1, source_target_pairs={{2,0},{4,2},{6,4},{0,6},{3,1},{5,3},{7,5},{1,7},{10,8},{12,10},{14... | collective-permute-start | bytes 811016 | tf_op jit(solution)/shard_map/ppermute | solution.py:238
  79.0 73.3 %collective-permute-start.21 = (bf16[1024,768]{1,0:T(8,128)(2,1)}, bf16[1024,768]{1,0:T(8,128)(2,1)}, u32[]{:S(2)}, u32[]{:S(2)}) collective-permute-start(bf16[1024,768]{1,0:T(8,128)(2,1)} %pad_maximum_fusion.3), channel_id=1, source_target_pairs={{0,8},{8,0},{16,24},{24,16},{1,9},{9,1},{17,25},{25,17},{2,10},{10... | collective-permute-start | bytes 4718600 | tf_op jit(solution)/shard_map/ppermute | solution.py:252
  79.0 75.7 %collective-permute-start.20 = (bf16[1024,768]{1,0:T(8,128)(2,1)}, bf16[1024,768]{1,0:T(8,128)(2,1)S(1)}, u32[]{:S(2)}, u32[]{:S(2)}) collective-permute-start(bf16[1024,768]{1,0:T(8,128)(2,1)} %pad_maximum_fusion.3), channel_id=1, source_target_pairs={{16,0},{24,8},{0,16},{8,24},{17,1},{25,9},{1,17},{9,25},{18,2},{26... | collective-permute-start | bytes 4718600 | tf_op jit(solution)/shard_map/ppermute | solution.py:244
  118.5 19.7 %collective-permute-start.13 = (bf16[352,128]{1,0:T(8,128)(2,1)S(1)}, bf16[352,128]{1,0:T(8,128)(2,1)S(1)}, u32[]{:S(2)}, u32[]{:S(2)}) collective-permute-start(bf16[352,128]{1,0:T(8,128)(2,1)S(1)} %get-tuple-element.163), channel_id=1, source_target_pairs={{4,0},{6,2},{0,4},{2,6},{5,1},{7,3},{1,5},{3,7},{12,8},{14,10},{8,... | collective-permute-start | bytes 270344 | tf_op jit(solution)/shard_map/ppermute | solution.py:238
  120.8 29.8 %collective-permute-start.25 = (bf16[512,256]{1,0:T(8,128)(2,1)}, bf16[512,256]{1,0:T(8,128)(2,1)S(1)}, u32[]{:S(2)}, u32[]{:S(2)}) collective-permute-start(bf16[512,256]{1,0:T(8,128)(2,1)} %dynamic-slice_bitcast_fusion.8), channel_id=1, source_target_pairs={{6,0},{0,2},{2,4},{4,6},{7,1},{1,3},{3,5},{5,7},{14,8},{8,10},{10,... | collective-permute-start | bytes 786440 | tf_op jit(solution)/shard_map/ppermute | solution.py:238
  125.9 24.7 %collective-permute-start.24 = (bf16[512,256]{1,0:T(8,128)(2,1)}, bf16[512,256]{1,0:T(8,128)(2,1)S(1)}, u32[]{:S(2)}, u32[]{:S(2)}) collective-permute-start(bf16[512,256]{1,0:T(8,128)(2,1)} %dynamic-slice_bitcast_fusion.8), channel_id=1, source_target_pairs={{4,0},{6,2},{0,4},{2,6},{5,1},{7,3},{1,5},{3,7},{12,8},{14,10},{8,... | collective-permute-start | bytes 786440 | tf_op jit(solution)/shard_map/ppermute | solution.py:238
  150.7 41.6 %collective-permute-start.27 = (bf16[512,1024]{1,0:T(8,128)(2,1)S(1)}, bf16[512,1024]{1,0:T(8,128)(2,1)S(1)}, u32[]{:S(2)}, u32[]{:S(2)}) collective-permute-start(bf16[512,1024]{1,0:T(8,128)(2,1)S(1)} %constant_dynamic-update-slice_fusion.6), channel_id=1, source_target_pairs={{0,8},{8,0},{16,24},{24,16},{1,9},{9,1},{17,25},{25,17},{2,10},{10... | collective-permute-start | bytes 3145736 | tf_op jit(solution)/shard_map/ppermute | solution.py:252
  150.7 25.6 %collective-permute-start.26 = (bf16[512,1024]{1,0:T(8,128)(2,1)S(1)}, bf16[512,1024]{1,0:T(8,128)(2,1)S(1)}, u32[]{:S(2)}, u32[]{:S(2)}) collective-permute-start(bf16[512,1024]{1,0:T(8,128)(2,1)S(1)} %constant_dynamic-update-slice_fusion.6), channel_id=1, source_target_pairs={{16,0},{24,8},{0,16},{8,24},{17,1},{25,9},{1,17},{9,25},{18,2},{26... | collective-permute-start | bytes 3145736 | tf_op jit(solution)/shard_map/ppermute | solution.py:244
  154.9 21.5 %collective-permute-start.22 = (bf16[1024,768]{1,0:T(8,128)(2,1)S(1)}, bf16[1024,768]{1,0:T(8,128)(2,1)S(1)}, u32[]{:S(2)}, u32[]{:S(2)}) collective-permute-start(bf16[1024,768]{1,0:T(8,128)(2,1)S(1)} %collective-permute-done.20), channel_id=1, source_target_pairs={{0,8},{8,0},{16,24},{24,16},{1,9},{9,1},{17,25},{25,17},{2,10},{10... | collective-permute-start | bytes 4718600 | tf_op jit(solution)/shard_map/ppermute | solution.py:252
  176.3 17.5 %collective-permute-start.28 = (bf16[512,1024]{1,0:T(8,128)(2,1)S(1)}, bf16[512,1024]{1,0:T(8,128)(2,1)S(1)}, u32[]{:S(2)}, u32[]{:S(2)}) collective-permute-start(bf16[512,1024]{1,0:T(8,128)(2,1)S(1)} %collective-permute-done.26), channel_id=1, source_target_pairs={{0,8},{8,0},{16,24},{24,16},{1,9},{9,1},{17,25},{25,17},{2,10},{10... | collective-permute-start | bytes 3145736 | tf_op jit(solution)/shard_map/ppermute | solution.py:252
  188.5 163.8 %collective-permute-start.75 = (f32[1024,1024]{1,0:T(8,128)}, f32[1024,1024]{1,0:T(8,128)}, u32[]{:S(2)}, u32[]{:S(2)}) collective-permute-start(f32[1024,1024]{1,0:T(8,128)} %fusion.69), channel_id=1, source_target_pairs={{0,8},{8,0},{16,24},{24,16},{1,9},{9,1},{17,25},{25,17},{2,10},{10... | collective-permute-start | bytes 12582920 | tf_op jit(solution)/shard_map/ppermute | solution.py:252
  197.1 34.5 %collective-permute-start.29 = (f32[352,1024]{1,0:T(8,128)S(1)}, f32[352,1024]{1,0:T(8,128)S(1)}, u32[]{:S(2)}, u32[]{:S(2)}) collective-permute-start(f32[352,1024]{1,0:T(8,128)S(1)} %fusion.30), channel_id=1, source_target_pairs={{0,1},{1,0},{2,3},{3,2},{4,5},{5,4},{6,7},{7,6},{8,9},{9,8},{10,11... | collective-permute-start | bytes 4325384 | tf_op jit(solution)/shard_map/ppermute | solution.py:283
  201.0 61.4 %collective-permute-start.30 = (f32[352,1024]{1,0:T(8,128)}, f32[352,1024]{1,0:T(8,128)}, u32[]{:S(2)}, u32[]{:S(2)}) collective-permute-start(f32[352,1024]{1,0:T(8,128)} %convolution_add_fusion.4), channel_id=1, source_target_pairs={{0,1},{1,0},{2,3},{3,2},{4,5},{5,4},{6,7},{7,6},{8,9},{9,8},{10,11... | collective-permute-start | bytes 4325384 | tf_op jit(solution)/shard_map/ppermute | solution.py:283
  242.2 48.0 %collective-permute-start.59 = (f32[256,1024]{1,0:T(8,128)}, f32[256,1024]{1,0:T(8,128)}, u32[]{:S(2)}, u32[]{:S(2)}) collective-permute-start(f32[256,1024]{1,0:T(8,128)} %fusion.108), channel_id=1, source_target_pairs={{0,8},{8,0},{16,24},{24,16},{1,9},{9,1},{17,25},{25,17},{2,10},{10... | collective-permute-start | bytes 3145736 | tf_op jit(solution)/shard_map/ppermute | solution.py:252
  262.4 12.1 %collective-permute-start.34 = (bf16[352,384]{1,0:T(8,128)(2,1)S(1)}, bf16[352,384]{1,0:T(8,128)(2,1)S(1)}, u32[]{:S(2)}, u32[]{:S(2)}) collective-permute-start(bf16[352,384]{1,0:T(8,128)(2,1)S(1)} %get-tuple-element.116), channel_id=1, source_target_pairs={{2,0},{4,2},{6,4},{0,6},{3,1},{5,3},{7,5},{1,7},{10,8},{12,10},{14... | collective-permute-start | bytes 811016 | tf_op jit(solution)/shard_map/ppermute | solution.py:238
  264.6 13.2 %collective-permute-start.36 = (bf16[352,384]{1,0:T(8,128)(2,1)S(1)}, bf16[352,384]{1,0:T(8,128)(2,1)S(1)}, u32[]{:S(2)}, u32[]{:S(2)}) collective-permute-start(bf16[352,384]{1,0:T(8,128)(2,1)S(1)} %get-tuple-element.117), channel_id=1, source_target_pairs={{6,0},{0,2},{2,4},{4,6},{7,1},{1,3},{3,5},{5,7},{14,8},{8,10},{10,... | collective-permute-start | bytes 811016 | tf_op jit(solution)/shard_map/ppermute | solution.py:238
  264.6 23.6 %collective-permute-start.35 = (bf16[352,384]{1,0:T(8,128)(2,1)S(1)}, bf16[352,384]{1,0:T(8,128)(2,1)S(1)}, u32[]{:S(2)}, u32[]{:S(2)}) collective-permute-start(bf16[352,384]{1,0:T(8,128)(2,1)S(1)} %get-tuple-element.118), channel_id=1, source_target_pairs={{4,0},{6,2},{0,4},{2,6},{5,1},{7,3},{1,5},{3,7},{12,8},{14,10},{8,... | collective-permute-start | bytes 811016 | tf_op jit(solution)/shard_map/ppermute | solution.py:238
  274.5 85.5 %collective-permute-start.67 = (f32[1024,1024]{0,1:T(8,128)}, f32[1024,1024]{0,1:T(8,128)}, u32[]{:S(2)}, u32[]{:S(2)}) collective-permute-start(f32[1024,1024]{0,1:T(8,128)} %fusion.75), channel_id=1, source_target_pairs={{0,8},{8,0},{16,24},{24,16},{1,9},{9,1},{17,25},{25,17},{2,10},{10... | collective-permute-start | bytes 12582920 | tf_op jit(solution)/shard_map/ppermute | solution.py:252
  290.2 14.6 %collective-permute-start.51 = (f32[1024,256]{0,1:T(8,128)S(1)}, f32[1024,256]{0,1:T(8,128)S(1)}, u32[]{:S(2)}, u32[]{:S(2)}) collective-permute-start(f32[1024,256]{0,1:T(8,128)S(1)} %fusion.101), channel_id=1, source_target_pairs={{0,8},{8,0},{16,24},{24,16},{1,9},{9,1},{17,25},{25,17},{2,10},{10... | collective-permute-start | bytes 3145736 | tf_op jit(solution)/shard_map/ppermute | solution.py:252
  307.2 31.3 %collective-permute-start.37 = (f32[352,1024]{1,0:T(8,128)S(1)}, f32[352,1024]{1,0:T(8,128)S(1)}, u32[]{:S(2)}, u32[]{:S(2)}) collective-permute-start(f32[352,1024]{1,0:T(8,128)S(1)} %fusion), channel_id=1, source_target_pairs={{0,1},{1,0},{2,3},{3,2},{4,5},{5,4},{6,7},{7,6},{8,9},{9,8},{10,11... | collective-permute-start | bytes 4325384 | tf_op jit(solution)/shard_map/ppermute | solution.py:283
  326.4 22.7 %collective-permute-start.38 = (f32[1024,512]{0,1:T(8,128)}, f32[1024,512]{0,1:T(8,128)}, u32[]{:S(2)}, u32[]{:S(2)}) collective-permute-start(f32[1024,512]{0,1:T(8,128)} %fusion.86), channel_id=1, source_target_pairs={{0,8},{8,0},{16,24},{24,16},{1,9},{9,1},{17,25},{25,17},{2,10},{10... | collective-permute-start | bytes 6291464 | tf_op jit(solution)/shard_map/ppermute | solution.py:252
  351.7 15.0 %collective-permute-start.39 = (bf16[1024,256]{0,1:T(8,128)(2,1)S(1)}, bf16[1024,256]{0,1:T(8,128)(2,1)S(1)}, u32[]{:S(2)}, u32[]{:S(2)}) collective-permute-start(bf16[1024,256]{0,1:T(8,128)(2,1)S(1)} %slice.724), channel_id=1, source_target_pairs={{16,0},{24,8},{0,16},{8,24},{17,1},{25,9},{1,17},{9,25},{18,2},{26... | collective-permute-start | bytes 1572872 | tf_op jit(solution)/shard_map/ppermute | solution.py:244
  358.5 53.0 %collective-permute-start.76 = (f32[512,1024]{1,0:T(8,128)}, f32[512,1024]{1,0:T(8,128)S(1)}, u32[]{:S(2)}, u32[]{:S(2)}) collective-permute-start(f32[512,1024]{1,0:T(8,128)} %slice.625), channel_id=1, source_target_pairs={{16,0},{24,8},{0,16},{8,24},{17,1},{25,9},{1,17},{9,25},{18,2},{26... | collective-permute-start | bytes 6291464 | tf_op jit(solution)/shard_map/ppermute | solution.py:244
  366.2 117.9 %collective-permute-start.68 = (f32[1024,512]{0,1:T(8,128)}, f32[1024,512]{0,1:T(8,128)}, u32[]{:S(2)}, u32[]{:S(2)}) collective-permute-start(f32[1024,512]{0,1:T(8,128)} %slice.616), channel_id=1, source_target_pairs={{16,0},{24,8},{0,16},{8,24},{17,1},{25,9},{1,17},{9,25},{18,2},{26... | collective-permute-start | bytes 6291464 | tf_op jit(solution)/shard_map/ppermute | solution.py:244
  378.2 78.6 %collective-permute-start.45 = (f32[256,256]{0,1:T(8,128)S(1)}, f32[256,256]{0,1:T(8,128)S(1)}, u32[]{:S(2)}, u32[]{:S(2)}) collective-permute-start(f32[256,256]{0,1:T(8,128)S(1)} %get-tuple-element.133), channel_id=1, source_target_pairs={{6,0},{0,2},{2,4},{4,6},{7,1},{1,3},{3,5},{5,7},{14,8},{8,10},{10,... | collective-permute-start | bytes 786440 | tf_op jit(solution)/shard_map/ppermute | solution.py:238
  380.2 80.4 %collective-permute-start.47 = (f32[256,256]{0,1:T(8,128)S(1)}, f32[256,256]{0,1:T(8,128)S(1)}, u32[]{:S(2)}, u32[]{:S(2)}) collective-permute-start(f32[256,256]{0,1:T(8,128)S(1)} %get-tuple-element.134), channel_id=1, source_target_pairs={{2,0},{4,2},{6,4},{0,6},{3,1},{5,3},{7,5},{1,7},{10,8},{12,10},{14... | collective-permute-start | bytes 786440 | tf_op jit(solution)/shard_map/ppermute | solution.py:238
  382.1 78.6 %collective-permute-start.46 = (f32[256,256]{0,1:T(8,128)S(1)}, f32[256,256]{0,1:T(8,128)S(1)}, u32[]{:S(2)}, u32[]{:S(2)}) collective-permute-start(f32[256,256]{0,1:T(8,128)S(1)} %get-tuple-element.135), channel_id=1, source_target_pairs={{4,0},{6,2},{0,4},{2,6},{5,1},{7,3},{1,5},{3,7},{12,8},{14,10},{8,... | collective-permute-start | bytes 786440 | tf_op jit(solution)/shard_map/ppermute | solution.py:238
  411.5 45.3 %collective-permute-start.43 = (f32[88,128]{1,0:T(8,128)S(1)}, f32[88,128]{1,0:T(8,128)S(1)}, u32[]{:S(2)}, u32[]{:S(2)}) collective-permute-start(f32[88,128]{1,0:T(8,128)S(1)} %dynamic-slice_reduce_fusion), channel_id=1, source_target_pairs={{16,0},{24,8},{0,16},{8,24},{17,1},{25,9},{1,17},{9,25},{18,2},{26... | collective-permute-start | bytes 135176 | tf_op jit(solution)/shard_map/ppermute | solution.py:244
  456.8 13.5 %collective-permute-start.79 = (bf16[512,256]{1,0:T(8,128)(2,1)S(1)}, bf16[512,256]{1,0:T(8,128)(2,1)S(1)}, u32[]{:S(2)}, u32[]{:S(2)}) collective-permute-start(bf16[512,256]{1,0:T(8,128)(2,1)S(1)} %get-tuple-element.124), channel_id=1, source_target_pairs={{2,0},{4,2},{6,4},{0,6},{3,1},{5,3},{7,5},{1,7},{10,8},{12,10},{14... | collective-permute-start | bytes 786440 | tf_op jit(solution)/shard_map/ppermute | solution.py:238
  460.6 22.1 %collective-permute-start.78 = (bf16[512,256]{1,0:T(8,128)(2,1)S(1)}, bf16[512,256]{1,0:T(8,128)(2,1)S(1)}, u32[]{:S(2)}, u32[]{:S(2)}) collective-permute-start(bf16[512,256]{1,0:T(8,128)(2,1)S(1)} %get-tuple-element.125), channel_id=1, source_target_pairs={{4,0},{6,2},{0,4},{2,6},{5,1},{7,3},{1,5},{3,7},{12,8},{14,10},{8,... | collective-permute-start | bytes 786440 | tf_op jit(solution)/shard_map/ppermute | solution.py:238
  460.7 30.5 %collective-permute-start.44 = (f32[88,128]{1,0:T(8,128)S(1)}, f32[88,128]{1,0:T(8,128)S(1)}, u32[]{:S(2)}, u32[]{:S(2)}) collective-permute-start(f32[88,128]{1,0:T(8,128)S(1)} %fusion.119), channel_id=1, source_target_pairs={{0,8},{8,0},{16,24},{24,16},{1,9},{9,1},{17,25},{25,17},{2,10},{10... | collective-permute-start | bytes 135176 | tf_op jit(solution)/shard_map/ppermute | solution.py:252
  467.8 28.8 %collective-permute-start.48 = (f32[256,256]{0,1:T(8,128)S(1)}, f32[256,256]{0,1:T(8,128)}, u32[]{:S(2)}, u32[]{:S(2)}) collective-permute-start(f32[256,256]{0,1:T(8,128)S(1)} %fusion.97), channel_id=1, source_target_pairs={{16,0},{24,8},{0,16},{8,24},{17,1},{25,9},{1,17},{9,25},{18,2},{26... | collective-permute-start | bytes 786440 | tf_op jit(solution)/shard_map/ppermute | solution.py:244
  483.6 31.0 %collective-permute-start.80 = (f32[512,256]{1,0:T(8,128)}, f32[512,256]{1,0:T(8,128)}, u32[]{:S(2)}, u32[]{:S(2)}) collective-permute-start(f32[512,256]{1,0:T(8,128)} %fusion.80), channel_id=1, source_target_pairs={{16,0},{24,8},{0,16},{8,24},{17,1},{25,9},{1,17},{9,25},{18,2},{26... | collective-permute-start | bytes 1572872 | tf_op jit(solution)/shard_map/ppermute | solution.py:244
  487.1 15.3 %collective-permute-start.71 = (bf16[256,512]{0,1:T(8,128)(2,1)}, bf16[256,512]{0,1:T(8,128)(2,1)S(1)}, u32[]{:S(2)}, u32[]{:S(2)}) collective-permute-start(bf16[256,512]{0,1:T(8,128)(2,1)} %get-tuple-element.127), channel_id=1, source_target_pairs={{2,0},{4,2},{6,4},{0,6},{3,1},{5,3},{7,5},{1,7},{10,8},{12,10},{14... | collective-permute-start | bytes 786440 | tf_op jit(solution)/shard_map/ppermute | solution.py:238
  491.2 19.9 %collective-permute-start.70 = (bf16[256,512]{0,1:T(8,128)(2,1)}, bf16[256,512]{0,1:T(8,128)(2,1)}, u32[]{:S(2)}, u32[]{:S(2)}) collective-permute-start(bf16[256,512]{0,1:T(8,128)(2,1)} %get-tuple-element.128), channel_id=1, source_target_pairs={{4,0},{6,2},{0,4},{2,6},{5,1},{7,3},{1,5},{3,7},{12,8},{14,10},{8,... | collective-permute-start | bytes 786440 | tf_op jit(solution)/shard_map/ppermute | solution.py:238
  496.6 18.6 %collective-permute-start.49 = (f32[256,256]{0,1:T(8,128)S(1)}, f32[256,256]{0,1:T(8,128)S(1)}, u32[]{:S(2)}, u32[]{:S(2)}) collective-permute-start(f32[256,256]{0,1:T(8,128)S(1)} %fusion.97), channel_id=1, source_target_pairs={{0,8},{8,0},{16,24},{24,16},{1,9},{9,1},{17,25},{25,17},{2,10},{10... | collective-permute-start | bytes 786440 | tf_op jit(solution)/shard_map/ppermute | solution.py:252
  498.3 16.9 %collective-permute-start.50 = (f32[256,256]{0,1:T(8,128)}, f32[256,256]{0,1:T(8,128)S(1)}, u32[]{:S(2)}, u32[]{:S(2)}) collective-permute-start(f32[256,256]{0,1:T(8,128)} %collective-permute-done.48), channel_id=1, source_target_pairs={{0,8},{8,0},{16,24},{24,16},{1,9},{9,1},{17,25},{25,17},{2,10},{10... | collective-permute-start | bytes 786440 | tf_op jit(solution)/shard_map/ppermute | solution.py:252
  502.5 22.4 %collective-permute-start.81 = (f32[512,256]{1,0:T(8,128)}, f32[512,256]{1,0:T(8,128)}, u32[]{:S(2)}, u32[]{:S(2)}) collective-permute-start(f32[512,256]{1,0:T(8,128)} %fusion.80), channel_id=1, source_target_pairs={{0,8},{8,0},{16,24},{24,16},{1,9},{9,1},{17,25},{25,17},{2,10},{10... | collective-permute-start | bytes 1572872 | tf_op jit(solution)/shard_map/ppermute | solution.py:252
  513.0 11.9 %collective-permute-start.72 = (f32[256,512]{0,1:T(8,128)}, f32[256,512]{0,1:T(8,128)S(1)}, u32[]{:S(2)}, u32[]{:S(2)}) collective-permute-start(f32[256,512]{0,1:T(8,128)} %fusion.82), channel_id=1, source_target_pairs={{16,0},{24,8},{0,16},{8,24},{17,1},{25,9},{1,17},{9,25},{18,2},{26... | collective-permute-start | bytes 1572872 | tf_op jit(solution)/shard_map/ppermute | solution.py:244
  (97 other events, 765.0 us)

commit v6 on v5

--- a/solution.py
+++ b/solution.py
@@ -469,23 +469,17 @@
     bias_one = jnp.sum(late_up_one, axis=0) * scales[0]
     gain_two = jnp.sum(late_second * late_part, axis=0)
     shift_two = jnp.sum(late_second, axis=0)
+    d_up_bias = [jnp.sum(v, axis=0) for v in late_hidden]
 
     grad_up = scatter_z(own_up, 0, BF)
     grad_out = scatter_z(own_out, 1, BF)
-    cut, slot_cols = 2 * head_cols, 3 * head_cols
-    d_project = lax.optimization_barrier(
-        jnp.concatenate([lax.select_n((k + n - z) % n, *dx_back) for k in range(n)], axis=1)
-    )
-    d_slots = [d_project[:, k * slot_cols : (k + 1) * slot_cols] for k in range(n)]
-    near, far = d_slots[: n // 2], d_slots[n // 2 :]
-    value_far = dot_tn(first_in, jnp.concatenate([v[:, cut:] for v in far], axis=1))
-    pair_far = dot_tn(first_in, jnp.concatenate([v[:, :cut] for v in far], axis=1))
-    value_near = dot_tn(first_in, jnp.concatenate([v[:, cut:] for v in near], axis=1))
-    pair_near = dot_tn(first_in, jnp.concatenate([v[:, :cut] for v in near], axis=1))
-    own_value = sum_rep(value_near, value_far, 1)
-    own_pair = sum_rep(pair_near, pair_far, 1)
-    grad_value = scatter_z(own_value, 0)
-    grad_pair = scatter_z(own_pair, 0)
+    d_project = jnp.concatenate(
+        [lax.select_n((k + n - z) % n, *dx_back) for k in range(n)], axis=1
+    )
+    half = d_project.shape[1] // 2
+    qkv_far = dot_tn(first_in, d_project[:, half:])
+    qkv_near = dot_tn(first_in, d_project[:, :half])
+    grad_qkv = scatter_z(sum_rep(qkv_near, qkv_far, 1), 0)
     w_qkv = jnp.concatenate(slots_qkv, axis=1)
     partial_first = dot_nt(d_project, w_qkv)
     d_first = partial_first + tp_swap(partial_first)
@@ -499,7 +493,6 @@
         1,
         part,
     )
-    d_up_bias = [jnp.sum(after(v, own_pair), axis=0) for v in late_hidden]
     own_rep = lax.dynamic_index_in_dim(jnp.stack(slot_rep), z, 0, keepdims=False)
     qv_grads = lax.dynamic_update_slice_in_dim(
         jnp.zeros((2, local_heads * HD), F32), head_sums, own_rep * head_cols, 1
@@ -533,13 +526,7 @@
 
     d_out, d_up = in_rep_order(grad_out, 0), in_rep_order(grad_up, 1)
     d_down = in_rep_order(grad_down, 0)
-    d_qkv = jnp.concatenate(
-        [
-            in_rep_order([g.reshape(part, 2, q_cols) for g in grad_pair], 2),
-            in_rep_order([g.reshape(part, 1, q_cols) for g in grad_value], 2),
-        ],
-        axis=1,
-    )
+    d_qkv = in_rep_order([g.reshape(part, 3, q_cols) for g in grad_qkv], 2)
     return (
         block_out,
         tokens_grad,

time: 540 us -> 571 us (1.057)
  waiting for transfers between devices: 267 us -> 307 us
  other arithmetic: 56 us -> 42.7 us
  starting transfers between devices: 91 us -> 99.8 us
    ppermute x14 -> x12, waiting for transfers between devices: 104 us -> 124 us  [y_pull(): lax.ppermute(x, 'rep', [((a + d) % ys * 2 + c, a * 2 + c) for a in range(...]
    ppermute x42 -> x39, waiting for transfers between devices: 130 us -> 143 us  [z_pull(): return lax.ppermute(x, 'fsdp', [((j + s) % n, j) for j in range(n)])]
    ppermute x42 -> x39, starting transfers between devices: 66.4 us -> 76.7 us  [z_pull(): return lax.ppermute(x, 'fsdp', [((j + s) % n, j) for j in range(n)])]
    ppermute x5, waiting for transfers between devices: 32.9 us -> 39.4 us  [tp_swap(): return lax.ppermute(x, 'tp', [(0, 1), (1, 0)])]
    unnamed x163 -> x127, local copies, waits for them, and re-layouts: 13.8 us -> 8.59 us
    ppermute x14 -> x12, starting transfers between devices: 16.7 us -> 14.7 us  [y_pull(): lax.ppermute(x, 'rep', [((a + d) % ys * 2 + c, a * 2 + c) for a in range(...]
    dot_general x10 -> x8, matrix products: 22.9 us -> 23.1 us  [dot_tn(): lax.dot_general(a, b, (((0,), (0,)), ((), ())), preferred_element_type=F32)]
  transfers between devices with their start and end apart: 83 -> 75, of which waited for: 39 -> 32; matrix products, arithmetic and copies ran while one was open for 23% -> 19% of each run, Pallas kernels for 6% -> 6%
where the time goes in v6:
time: 571 us; the launch traced here: 562 us
  waiting for transfers between devices  307 us (54%)
  starting transfers between devices  99.8 us (17%)
  matrix products  44 us (8%)
  other arithmetic  42.7 us (7%)
  local copies, waits for them, and re-layouts  33.4 us (6%)
  Pallas kernels  31.6 us (6%)
    ppermute x39, waiting for transfers between devices, z_pull(): return lax.ppermute(x, 'fsdp', [((j + s) % n, j) for j in range(n)])  143 us
    ppermute x12, waiting for transfers between devices, y_pull(): lax.ppermute(x, 'rep', [((a + d) % ys * 2 + c, a * 2 + c) for a in range(...  124 us
    ppermute x39, starting transfers between devices, z_pull(): return lax.ppermute(x, 'fsdp', [((j + s) % n, j) for j in range(n)])  76.7 us
    ppermute x5, waiting for transfers between devices, tp_swap(): return lax.ppermute(x, 'tp', [(0, 1), (1, 0)])  39.4 us
    dot_general x8, matrix products, dot_tn(): lax.dot_general(a, b, (((0,), (0,)), ((), ())), preferred_element_type=F32)  23.1 us
    pallas_call x1, Pallas kernels, attend_backward(): pl.pallas_call(functools.partial(backward_kernel, heads), out_shape=(jax....  15.9 us
    pallas_call x1, Pallas kernels, attend_forward(): pl.pallas_call(functools.partial(forward_kernel, heads), out_shape=(jax.S...  15.7 us
    ppermute x12, starting transfers between devices, y_pull(): lax.ppermute(x, 'rep', [((a + d) % ys * 2 + c, a * 2 + c) for a in range(...  14.7 us
  transfers between devices with their start and end apart: 75, of which 32 were waited for; matrix products, arithmetic and copies ran while one was open for 19% of the time, Pallas kernels for 6%

profile of v6, /device:TPU:0, one launch (start us, length us, event | category | flops | bytes accessed | tf_op | source)
XLA Modules:
  0.0 561.6 jit_solution(13061019342164384063)
XLA Ops:
  5.2 3.1 collective-permute-start.2
  8.3 2.6 collective-permute-start.1
  17.7 2.9 collective-permute-start.3
  24.3 4.1 collective-permute-done.4
  29.0 3.4 collective-permute-start.16
  35.9 4.6 collective-permute-done.16
  40.6 21.6 %collective-permute-done.17 = bf16[256,640]{1,0:T(8,128)(2,1)S(1)} collective-permute-done((bf16[256,640]{1,0:T(8,128)(2,1)S(1)}, bf16[256,640]{1,0:T(8,128)(2,1)S(1)}, u32[]{:S(2)}, u32[]{:S(2)}) %collective-permute-start.17) | collective-permute-done | bytes 327712 | tf_op jit(solution)/shard_map/ppermute | solution.py:238
  65.7 3.5 collective-permute-done.19
  73.6 2.8 collective-permute-start.9
  80.7 2.2 collective-permute-done.11
  83.0 8.5 %collective-permute-done.10 = bf16[352,384]{1,0:T(8,128)(2,1)S(1)} collective-permute-done((bf16[352,384]{1,0:T(8,128)(2,1)S(1)}, bf16[352,384]{1,0:T(8,128)(2,1)S(1)}, u32[]{:S(2)}, u32[]{:S(2)}) %collective-permute-start.10) | collective-permute-done | bytes 270368 | tf_op jit(solution)/shard_map/ppermute | solution.py:238
  92.6 15.7 %attend_forward.1 = (bf16[1408,128]{1,0:T(8,128)(2,1)}, f32[11,1,256]{2,1,0:T(1,128)}) custom-call(bf16[1408,384]{1,0:T(8,128)(2,1)} %pad_maximum_fusion.6.x_ref, s32[1408,128]{1,0:T(8,128)} %broadcast_in_dim.18.key_ref, s32[11,1,128]{2,1,0:T(1,128)} %and_select_fusion.seg_ref), custom_call_target="tpu_custom_call" | custom-call | flops 1015021568 | bytes 1441792 | tf_op jit(solution)/shard_map/attend_forward/pallas_call | solution.py:162
  109.3 8.0 %collective-permute-start.12 = (bf16[352,128]{1,0:T(8,128)(2,1)S(1)}, bf16[352,128]{1,0:T(8,128)(2,1)S(1)}, u32[]{:S(2)}, u32[]{:S(2)}) collective-permute-start(bf16[352,128]{1,0:T(8,128)(2,1)S(1)} %get-tuple-element.138), channel_id=1, source_target_pairs={{2,0},{4,2},{6,4},{0,6},{3,1},{5,3},{7,5},{1,7},{10,8},{12,10},{14... | collective-permute-start | bytes 270344 | tf_op jit(solution)/shard_map/ppermute | solution.py:238
  119.7 3.0 collective-permute-start.25
  124.6 12.7 %collective-permute-done.13 = bf16[352,128]{1,0:T(8,128)(2,1)S(1)} collective-permute-done((bf16[352,128]{1,0:T(8,128)(2,1)S(1)}, bf16[352,128]{1,0:T(8,128)(2,1)S(1)}, u32[]{:S(2)}, u32[]{:S(2)}) %collective-permute-start.13) | collective-permute-done | bytes 90144 | tf_op jit(solution)/shard_map/ppermute | solution.py:238
  138.7 9.1 %collective-permute-done.23 = bf16[512,256]{1,0:T(8,128)(2,1)S(1)} collective-permute-done((bf16[512,256]{1,0:T(8,128)(2,1)S(1)}, bf16[512,256]{1,0:T(8,128)(2,1)S(1)}, u32[]{:S(2)}, u32[]{:S(2)}) %collective-permute-start.23) | collective-permute-done | bytes 262176 | tf_op jit(solution)/shard_map/ppermute | solution.py:238
  158.7 16.4 %collective-permute-done.26 = bf16[512,1024]{1,0:T(8,128)(2,1)S(1)} collective-permute-done((bf16[512,1024]{1,0:T(8,128)(2,1)S(1)}, bf16[512,1024]{1,0:T(8,128)(2,1)S(1)}, u32[]{:S(2)}, u32[]{:S(2)}) %collective-permute-start.26) | collective-permute-done | bytes 1048608 | tf_op jit(solution)/shard_map/ppermute | solution.py:244
  175.9 3.7 fusion.145
  183.8 3.2 fusion.76
  201.1 3.4 fusion.82
  204.6 25.7 %collective-permute-done.29 = f32[352,1024]{1,0:T(8,128)S(1)} collective-permute-done((f32[352,1024]{1,0:T(8,128)S(1)}, f32[352,1024]{1,0:T(8,128)S(1)}, u32[]{:S(2)}, u32[]{:S(2)}) %collective-permute-start.29) | collective-permute-done | bytes 1441824 | tf_op jit(solution)/shard_map/ppermute | solution.py:283
  235.5 2.5 collective-permute-start.31
  243.7 15.9 %attend_backward.1 = (bf16[1408,384]{1,0:T(8,128)(2,1)}, f32[2,128]{1,0:T(2,128)}) custom-call(bf16[1408,384]{1,0:T(8,128)(2,1)} %pad_maximum_fusion.6.x_ref, bf16[1408,128]{1,0:T(8,128)(2,1)} %get-tuple-element.35.o_ref, bf16[1408,128]{1,0:T(8,128)(2,1)} %pad_maximum_fusion.13.g_ref, f32[11,1,256]{2,1,0:T(1,128)} %get-tuple-element.39.lse_ref, ...), custom_call_target="tpu_custom_call" | custom-call | flops 2537553920 | bytes 3604480 | tf_op jit(solution)/shard_map/attend_backward/pallas_call | solution.py:181
  271.5 3.3 multiply_reduce_fusion
  274.9 3.3 collective-permute-done.34
  278.2 3.8 collective-permute-done.36
  282.0 10.4 %collective-permute-done.35 = bf16[352,384]{1,0:T(8,128)(2,1)S(1)} collective-permute-done((bf16[352,384]{1,0:T(8,128)(2,1)S(1)}, bf16[352,384]{1,0:T(8,128)(2,1)S(1)}, u32[]{:S(2)}, u32[]{:S(2)}) %collective-permute-start.35) | collective-permute-done | bytes 270368 | tf_op jit(solution)/shard_map/ppermute | solution.py:238
  299.2 2.9 collective-permute-done.52
  303.4 2.9 collective-permute-start.55
  306.8 2.5 collective-permute-done.53
  309.3 3.0 collective-permute-done.54
  314.2 3.1 collective-permute-done.56
  317.3 2.8 fusion.89
  321.6 8.5 %collective-permute-done.37 = f32[352,1024]{1,0:T(8,128)S(1)} collective-permute-done((f32[352,1024]{1,0:T(8,128)S(1)}, f32[352,1024]{1,0:T(8,128)S(1)}, u32[]{:S(2)}, u32[]{:S(2)}) %collective-permute-start.37) | collective-permute-done | bytes 1441824 | tf_op jit(solution)/shard_map/ppermute | solution.py:283
  332.1 3.9 collective-permute-start.38
  339.8 3.3 collective-permute-done.39
  343.1 3.8 convolution_add_fusion.1
  347.8 2.9 convolution_add_fusion.3
  352.4 3.5 convolution_add_fusion.2
  359.0 94.2 %collective-permute-done.41 = f32[88,128]{1,0:T(8,128)S(1)} collective-permute-done((f32[88,128]{1,0:T(8,128)S(1)}, f32[88,128]{1,0:T(8,128)S(1)}, u32[]{:S(2)}, u32[]{:S(2)}) %collective-permute-start.41) | collective-permute-done | bytes 45088 | tf_op jit(solution)/shard_map/ppermute | solution.py:244
  455.5 2.3 collective-permute-start.47
  459.2 8.6 %collective-permute-done.45 = f32[256,384]{0,1:T(8,128)S(1)} collective-permute-done((f32[256,384]{0,1:T(8,128)S(1)}, f32[256,384]{0,1:T(8,128)S(1)}, u32[]{:S(2)}, u32[]{:S(2)}) %collective-permute-start.45) | collective-permute-done | bytes 393248 | tf_op jit(solution)/shard_map/ppermute | solution.py:238
  467.7 15.0 %collective-permute-start.69 = (bf16[512,256]{1,0:T(8,128)(2,1)S(1)}, bf16[512,256]{1,0:T(8,128)(2,1)S(1)}, u32[]{:S(2)}, u32[]{:S(2)}) collective-permute-start(bf16[512,256]{1,0:T(8,128)(2,1)S(1)} %get-tuple-element.114), channel_id=1, source_target_pairs={{6,0},{0,2},{2,4},{4,6},{7,1},{1,3},{3,5},{5,7},{14,8},{8,10},{10,... | collective-permute-start | bytes 786440 | tf_op jit(solution)/shard_map/ppermute | solution.py:238
  482.7 15.8 %collective-permute-done.46 = f32[256,384]{0,1:T(8,128)S(1)} collective-permute-done((f32[256,384]{0,1:T(8,128)S(1)}, f32[256,384]{0,1:T(8,128)S(1)}, u32[]{:S(2)}, u32[]{:S(2)}) %collective-permute-start.46) | collective-permute-done | bytes 393248 | tf_op jit(solution)/shard_map/ppermute | solution.py:238
  501.6 6.9 %collective-permute-start.61 = (bf16[256,512]{0,1:T(8,128)(2,1)}, bf16[256,512]{0,1:T(8,128)(2,1)S(1)}, u32[]{:S(2)}, u32[]{:S(2)}) collective-permute-start(bf16[256,512]{0,1:T(8,128)(2,1)} %get-tuple-element.117), channel_id=1, source_target_pairs={{6,0},{0,2},{2,4},{4,6},{7,1},{1,3},{3,5},{5,7},{14,8},{8,10},{10,... | collective-permute-start | bytes 786440 | tf_op jit(solution)/shard_map/ppermute | solution.py:238
  508.6 12.3 %collective-permute-done.70 = bf16[512,256]{1,0:T(8,128)(2,1)S(1)} collective-permute-done((bf16[512,256]{1,0:T(8,128)(2,1)S(1)}, bf16[512,256]{1,0:T(8,128)(2,1)S(1)}, u32[]{:S(2)}, u32[]{:S(2)}) %collective-permute-start.70) | collective-permute-done | bytes 262176 | tf_op jit(solution)/shard_map/ppermute | solution.py:238
  532.2 7.8 %collective-permute-done.62 = bf16[256,512]{0,1:T(8,128)(2,1)} collective-permute-done((bf16[256,512]{0,1:T(8,128)(2,1)}, bf16[256,512]{0,1:T(8,128)(2,1)}, u32[]{:S(2)}, u32[]{:S(2)}) %collective-permute-start.62) | collective-permute-done | bytes 262176 | tf_op jit(solution)/shard_map/ppermute | solution.py:238
  547.0 7.3 %collective-permute-done.64 = f32[256,512]{0,1:T(8,128)} collective-permute-done((f32[256,512]{0,1:T(8,128)S(1)}, f32[256,512]{0,1:T(8,128)}, u32[]{:S(2)}, u32[]{:S(2)}) %collective-permute-start.64) | collective-permute-done | bytes 524320 | tf_op jit(solution)/shard_map/ppermute | solution.py:244
  (418 shorter events, 145.3 us)
Async XLA Ops:
  5.2 12.5 %collective-permute-start.2 = (bf16[13,256]{1,0:T(8,128)(2,1)S(1)}, bf16[13,256]{1,0:T(8,128)(2,1)S(1)}, u32[]{:S(2)}, u32[]{:S(2)}) collective-permute-start(bf16[13,256]{1,0:T(8,128)(2,1)S(1)} %concatenate.142), channel_id=1, source_target_pairs={{6,0},{0,2},{2,4},{4,6},{7,1},{1,3},{3,5},{5,7},{14,8},{8,10},{10,... | collective-permute-start | bytes 19976 | tf_op jit(solution)/shard_map/ppermute | solution.py:238
  8.3 12.2 %collective-permute-start.1 = (bf16[13,256]{1,0:T(8,128)(2,1)S(1)}, bf16[13,256]{1,0:T(8,128)(2,1)S(1)}, u32[]{:S(2)}, u32[]{:S(2)}) collective-permute-start(bf16[13,256]{1,0:T(8,128)(2,1)S(1)} %concatenate.142), channel_id=1, source_target_pairs={{4,0},{6,2},{0,4},{2,6},{5,1},{7,3},{1,5},{3,7},{12,8},{14,10},{8,... | collective-permute-start | bytes 19976 | tf_op jit(solution)/shard_map/ppermute | solution.py:238
  12.9 15.5 %collective-permute-start.4 = (bf16[256,384]{0,1:T(8,128)(2,1)S(1)}, bf16[256,384]{0,1:T(8,128)(2,1)S(1)}, u32[]{:S(2)}, u32[]{:S(2)}) collective-permute-start(bf16[256,384]{0,1:T(8,128)(2,1)S(1)} %bitcast.223), channel_id=1, source_target_pairs={{4,0},{6,2},{0,4},{2,6},{5,1},{7,3},{1,5},{3,7},{12,8},{14,10},{8,... | collective-permute-start | bytes 589832 | tf_op jit(solution)/shard_map/ppermute | solution.py:238
  32.5 32.6 %collective-permute-start.6 = (bf16[1024,384]{0,1:T(8,128)(2,1)S(1)}, bf16[1024,384]{0,1:T(8,128)(2,1)S(1)}, u32[]{:S(2)}, u32[]{:S(2)}) collective-permute-start(bf16[1024,384]{0,1:T(8,128)(2,1)S(1)} %pad_maximum_fusion.7), channel_id=1, source_target_pairs={{16,0},{24,8},{0,16},{8,24},{17,1},{25,9},{1,17},{9,25},{18,2},{26... | collective-permute-start | bytes 2359304 | tf_op jit(solution)/shard_map/ppermute | solution.py:244
  34.1 28.1 %collective-permute-start.17 = (bf16[256,640]{1,0:T(8,128)(2,1)S(1)}, bf16[256,640]{1,0:T(8,128)(2,1)S(1)}, u32[]{:S(2)}, u32[]{:S(2)}) collective-permute-start(bf16[256,640]{1,0:T(8,128)(2,1)S(1)} %pad_maximum_fusion.14), channel_id=1, source_target_pairs={{4,0},{6,2},{0,4},{2,6},{5,1},{7,3},{1,5},{3,7},{12,8},{14,10},{8,... | collective-permute-start | bytes 983048 | tf_op jit(solution)/shard_map/ppermute | solution.py:238
  35.8 26.4 %collective-permute-start.18 = (bf16[256,640]{1,0:T(8,128)(2,1)S(1)}, bf16[256,640]{1,0:T(8,128)(2,1)S(1)}, u32[]{:S(2)}, u32[]{:S(2)}) collective-permute-start(bf16[256,640]{1,0:T(8,128)(2,1)S(1)} %pad_maximum_fusion.14), channel_id=1, source_target_pairs={{6,0},{0,2},{2,4},{4,6},{7,1},{1,3},{3,5},{5,7},{14,8},{8,10},{10,... | collective-permute-start | bytes 983048 | tf_op jit(solution)/shard_map/ppermute | solution.py:238
  35.8 34.1 %collective-permute-start.7 = (bf16[1024,384]{0,1:T(8,128)(2,1)S(1)}, bf16[1024,384]{0,1:T(8,128)(2,1)S(1)}, u32[]{:S(2)}, u32[]{:S(2)}) collective-permute-start(bf16[1024,384]{0,1:T(8,128)(2,1)S(1)} %pad_maximum_fusion.7), channel_id=1, source_target_pairs={{0,8},{8,0},{16,24},{24,16},{1,9},{9,1},{17,25},{25,17},{2,10},{10... | collective-permute-start | bytes 2359304 | tf_op jit(solution)/shard_map/ppermute | solution.py:252
  71.8 19.7 %collective-permute-start.10 = (bf16[352,384]{1,0:T(8,128)(2,1)S(1)}, bf16[352,384]{1,0:T(8,128)(2,1)S(1)}, u32[]{:S(2)}, u32[]{:S(2)}) collective-permute-start(bf16[352,384]{1,0:T(8,128)(2,1)S(1)} %get-tuple-element.112), channel_id=1, source_target_pairs={{4,0},{6,2},{0,4},{2,6},{5,1},{7,3},{1,5},{3,7},{12,8},{14,10},{8,... | collective-permute-start | bytes 811016 | tf_op jit(solution)/shard_map/ppermute | solution.py:238
  73.6 17.8 %collective-permute-start.9 = (bf16[352,384]{1,0:T(8,128)(2,1)S(1)}, bf16[352,384]{1,0:T(8,128)(2,1)S(1)}, u32[]{:S(2)}, u32[]{:S(2)}) collective-permute-start(bf16[352,384]{1,0:T(8,128)(2,1)S(1)} %get-tuple-element.113), channel_id=1, source_target_pairs={{2,0},{4,2},{6,4},{0,6},{3,1},{5,3},{7,5},{1,7},{10,8},{12,10},{14... | collective-permute-start | bytes 811016 | tf_op jit(solution)/shard_map/ppermute | solution.py:238
  77.8 73.3 %collective-permute-start.21 = (bf16[1024,768]{1,0:T(8,128)(2,1)}, bf16[1024,768]{1,0:T(8,128)(2,1)}, u32[]{:S(2)}, u32[]{:S(2)}) collective-permute-start(bf16[1024,768]{1,0:T(8,128)(2,1)} %pad_maximum_fusion.3), channel_id=1, source_target_pairs={{0,8},{8,0},{16,24},{24,16},{1,9},{9,1},{17,25},{25,17},{2,10},{10... | collective-permute-start | bytes 4718600 | tf_op jit(solution)/shard_map/ppermute | solution.py:252
  77.8 75.7 %collective-permute-start.20 = (bf16[1024,768]{1,0:T(8,128)(2,1)}, bf16[1024,768]{1,0:T(8,128)(2,1)S(1)}, u32[]{:S(2)}, u32[]{:S(2)}) collective-permute-start(bf16[1024,768]{1,0:T(8,128)(2,1)} %pad_maximum_fusion.3), channel_id=1, source_target_pairs={{16,0},{24,8},{0,16},{8,24},{17,1},{25,9},{1,17},{9,25},{18,2},{26... | collective-permute-start | bytes 4718600 | tf_op jit(solution)/shard_map/ppermute | solution.py:244
  117.2 20.0 %collective-permute-start.13 = (bf16[352,128]{1,0:T(8,128)(2,1)S(1)}, bf16[352,128]{1,0:T(8,128)(2,1)S(1)}, u32[]{:S(2)}, u32[]{:S(2)}) collective-permute-start(bf16[352,128]{1,0:T(8,128)(2,1)S(1)} %get-tuple-element.140), channel_id=1, source_target_pairs={{4,0},{6,2},{0,4},{2,6},{5,1},{7,3},{1,5},{3,7},{12,8},{14,10},{8,... | collective-permute-start | bytes 270344 | tf_op jit(solution)/shard_map/ppermute | solution.py:238
  119.7 29.7 %collective-permute-start.25 = (bf16[512,256]{1,0:T(8,128)(2,1)S(1)}, bf16[512,256]{1,0:T(8,128)(2,1)S(1)}, u32[]{:S(2)}, u32[]{:S(2)}) collective-permute-start(bf16[512,256]{1,0:T(8,128)(2,1)S(1)} %dynamic-slice_bitcast_fusion.8), channel_id=1, source_target_pairs={{6,0},{0,2},{2,4},{4,6},{7,1},{1,3},{3,5},{5,7},{14,8},{8,10},{10,... | collective-permute-start | bytes 786440 | tf_op jit(solution)/shard_map/ppermute | solution.py:238
  124.5 24.8 %collective-permute-start.24 = (bf16[512,256]{1,0:T(8,128)(2,1)S(1)}, bf16[512,256]{1,0:T(8,128)(2,1)S(1)}, u32[]{:S(2)}, u32[]{:S(2)}) collective-permute-start(bf16[512,256]{1,0:T(8,128)(2,1)S(1)} %dynamic-slice_bitcast_fusion.8), channel_id=1, source_target_pairs={{4,0},{6,2},{0,4},{2,6},{5,1},{7,3},{1,5},{3,7},{12,8},{14,10},{8,... | collective-permute-start | bytes 786440 | tf_op jit(solution)/shard_map/ppermute | solution.py:238
  149.4 41.4 %collective-permute-start.27 = (bf16[512,1024]{1,0:T(8,128)(2,1)S(1)}, bf16[512,1024]{1,0:T(8,128)(2,1)S(1)}, u32[]{:S(2)}, u32[]{:S(2)}) collective-permute-start(bf16[512,1024]{1,0:T(8,128)(2,1)S(1)} %constant_dynamic-update-slice_fusion.6), channel_id=1, source_target_pairs={{0,8},{8,0},{16,24},{24,16},{1,9},{9,1},{17,25},{25,17},{2,10},{10... | collective-permute-start | bytes 3145736 | tf_op jit(solution)/shard_map/ppermute | solution.py:252
  149.5 25.6 %collective-permute-start.26 = (bf16[512,1024]{1,0:T(8,128)(2,1)S(1)}, bf16[512,1024]{1,0:T(8,128)(2,1)S(1)}, u32[]{:S(2)}, u32[]{:S(2)}) collective-permute-start(bf16[512,1024]{1,0:T(8,128)(2,1)S(1)} %constant_dynamic-update-slice_fusion.6), channel_id=1, source_target_pairs={{16,0},{24,8},{0,16},{8,24},{17,1},{25,9},{1,17},{9,25},{18,2},{26... | collective-permute-start | bytes 3145736 | tf_op jit(solution)/shard_map/ppermute | solution.py:244
  153.6 21.5 %collective-permute-start.22 = (bf16[1024,768]{1,0:T(8,128)(2,1)S(1)}, bf16[1024,768]{1,0:T(8,128)(2,1)S(1)}, u32[]{:S(2)}, u32[]{:S(2)}) collective-permute-start(bf16[1024,768]{1,0:T(8,128)(2,1)S(1)} %collective-permute-done.20), channel_id=1, source_target_pairs={{0,8},{8,0},{16,24},{24,16},{1,9},{9,1},{17,25},{25,17},{2,10},{10... | collective-permute-start | bytes 4718600 | tf_op jit(solution)/shard_map/ppermute | solution.py:252
  175.1 17.4 %collective-permute-start.28 = (bf16[512,1024]{1,0:T(8,128)(2,1)S(1)}, bf16[512,1024]{1,0:T(8,128)(2,1)S(1)}, u32[]{:S(2)}, u32[]{:S(2)}) collective-permute-start(bf16[512,1024]{1,0:T(8,128)(2,1)S(1)} %collective-permute-done.26), channel_id=1, source_target_pairs={{0,8},{8,0},{16,24},{24,16},{1,9},{9,1},{17,25},{25,17},{2,10},{10... | collective-permute-start | bytes 3145736 | tf_op jit(solution)/shard_map/ppermute | solution.py:252
  187.1 156.0 %collective-permute-start.67 = (f32[1024,1024]{1,0:T(8,128)}, f32[1024,1024]{1,0:T(8,128)}, u32[]{:S(2)}, u32[]{:S(2)}) collective-permute-start(f32[1024,1024]{1,0:T(8,128)} %fusion.76), channel_id=1, source_target_pairs={{0,8},{8,0},{16,24},{24,16},{1,9},{9,1},{17,25},{25,17},{2,10},{10... | collective-permute-start | bytes 12582920 | tf_op jit(solution)/shard_map/ppermute | solution.py:252
  195.7 34.5 %collective-permute-start.29 = (f32[352,1024]{1,0:T(8,128)S(1)}, f32[352,1024]{1,0:T(8,128)S(1)}, u32[]{:S(2)}, u32[]{:S(2)}) collective-permute-start(f32[352,1024]{1,0:T(8,128)S(1)} %fusion.30), channel_id=1, source_target_pairs={{0,1},{1,0},{2,3},{3,2},{4,5},{5,4},{6,7},{7,6},{8,9},{9,8},{10,11... | collective-permute-start | bytes 4325384 | tf_op jit(solution)/shard_map/ppermute | solution.py:283
  199.7 62.0 %collective-permute-start.30 = (f32[352,1024]{1,0:T(8,128)}, f32[352,1024]{1,0:T(8,128)}, u32[]{:S(2)}, u32[]{:S(2)}) collective-permute-start(f32[352,1024]{1,0:T(8,128)} %convolution_add_fusion.4), channel_id=1, source_target_pairs={{0,1},{1,0},{2,3},{3,2},{4,5},{5,4},{6,7},{7,6},{8,9},{9,8},{10,11... | collective-permute-start | bytes 4325384 | tf_op jit(solution)/shard_map/ppermute | solution.py:283
  240.8 52.9 %collective-permute-start.51 = (f32[256,1024]{1,0:T(8,128)}, f32[256,1024]{1,0:T(8,128)}, u32[]{:S(2)}, u32[]{:S(2)}) collective-permute-start(f32[256,1024]{1,0:T(8,128)} %fusion.108), channel_id=1, source_target_pairs={{0,8},{8,0},{16,24},{24,16},{1,9},{9,1},{17,25},{25,17},{2,10},{10... | collective-permute-start | bytes 3145736 | tf_op jit(solution)/shard_map/ppermute | solution.py:252
  268.6 13.4 %collective-permute-start.36 = (bf16[352,384]{1,0:T(8,128)(2,1)}, bf16[352,384]{1,0:T(8,128)(2,1)S(1)}, u32[]{:S(2)}, u32[]{:S(2)}) collective-permute-start(bf16[352,384]{1,0:T(8,128)(2,1)} %get-tuple-element.108), channel_id=1, source_target_pairs={{6,0},{0,2},{2,4},{4,6},{7,1},{1,3},{3,5},{5,7},{14,8},{8,10},{10,... | collective-permute-start | bytes 811016 | tf_op jit(solution)/shard_map/ppermute | solution.py:238
  268.6 23.9 %collective-permute-start.35 = (bf16[352,384]{1,0:T(8,128)(2,1)S(1)}, bf16[352,384]{1,0:T(8,128)(2,1)S(1)}, u32[]{:S(2)}, u32[]{:S(2)}) collective-permute-start(bf16[352,384]{1,0:T(8,128)(2,1)S(1)} %get-tuple-element.109), channel_id=1, source_target_pairs={{4,0},{6,2},{0,4},{2,6},{5,1},{7,3},{1,5},{3,7},{12,8},{14,10},{8,... | collective-permute-start | bytes 811016 | tf_op jit(solution)/shard_map/ppermute | solution.py:238
  298.6 31.5 %collective-permute-start.37 = (f32[352,1024]{1,0:T(8,128)S(1)}, f32[352,1024]{1,0:T(8,128)S(1)}, u32[]{:S(2)}, u32[]{:S(2)}) collective-permute-start(f32[352,1024]{1,0:T(8,128)S(1)} %fusion), channel_id=1, source_target_pairs={{0,1},{1,0},{2,3},{3,2},{4,5},{5,4},{6,7},{7,6},{8,9},{9,8},{10,11... | collective-permute-start | bytes 4325384 | tf_op jit(solution)/shard_map/ppermute | solution.py:283
  309.3 43.1 %collective-permute-start.59 = (f32[1024,1024]{0,1:T(8,128)}, f32[1024,1024]{0,1:T(8,128)}, u32[]{:S(2)}, u32[]{:S(2)}) collective-permute-start(f32[1024,1024]{0,1:T(8,128)} %fusion.82), channel_id=1, source_target_pairs={{0,8},{8,0},{16,24},{24,16},{1,9},{9,1},{17,25},{25,17},{2,10},{10... | collective-permute-start | bytes 12582920 | tf_op jit(solution)/shard_map/ppermute | solution.py:252
  320.1 27.5 %collective-permute-start.43 = (f32[1024,768]{0,1:T(8,128)}, f32[1024,768]{0,1:T(8,128)}, u32[]{:S(2)}, u32[]{:S(2)}) collective-permute-start(f32[1024,768]{0,1:T(8,128)} %fusion.89), channel_id=1, source_target_pairs={{0,8},{8,0},{16,24},{24,16},{1,9},{9,1},{17,25},{25,17},{2,10},{10... | collective-permute-start | bytes 9437192 | tf_op jit(solution)/shard_map/ppermute | solution.py:252
  347.1 110.6 %collective-permute-start.68 = (f32[512,1024]{1,0:T(8,128)S(1)}, f32[512,1024]{1,0:T(8,128)S(1)}, u32[]{:S(2)}, u32[]{:S(2)}) collective-permute-start(f32[512,1024]{1,0:T(8,128)S(1)} %slice.546), channel_id=1, source_target_pairs={{16,0},{24,8},{0,16},{8,24},{17,1},{25,9},{1,17},{9,25},{18,2},{26... | collective-permute-start | bytes 6291464 | tf_op jit(solution)/shard_map/ppermute | solution.py:244
  350.9 102.3 %collective-permute-start.44 = (bf16[1024,384]{0,1:T(8,128)(2,1)S(1)}, bf16[1024,384]{0,1:T(8,128)(2,1)S(1)}, u32[]{:S(2)}, u32[]{:S(2)}) collective-permute-start(bf16[1024,384]{0,1:T(8,128)(2,1)S(1)} %slice.638), channel_id=1, source_target_pairs={{16,0},{24,8},{0,16},{8,24},{17,1},{25,9},{1,17},{9,25},{18,2},{26... | collective-permute-start | bytes 2359304 | tf_op jit(solution)/shard_map/ppermute | solution.py:244
  356.2 142.4 %collective-permute-start.60 = (f32[1024,512]{0,1:T(8,128)S(1)}, f32[1024,512]{0,1:T(8,128)S(1)}, u32[]{:S(2)}, u32[]{:S(2)}) collective-permute-start(f32[1024,512]{0,1:T(8,128)S(1)} %slice.537), channel_id=1, source_target_pairs={{16,0},{24,8},{0,16},{8,24},{17,1},{25,9},{1,17},{9,25},{18,2},{26... | collective-permute-start | bytes 6291464 | tf_op jit(solution)/shard_map/ppermute | solution.py:244
  357.2 95.9 %collective-permute-start.41 = (f32[88,128]{1,0:T(8,128)S(1)}, f32[88,128]{1,0:T(8,128)S(1)}, u32[]{:S(2)}, u32[]{:S(2)}) collective-permute-start(f32[88,128]{1,0:T(8,128)S(1)} %dynamic-slice_reduce_fusion), channel_id=1, source_target_pairs={{16,0},{24,8},{0,16},{8,24},{17,1},{25,9},{1,17},{9,25},{18,2},{26... | collective-permute-start | bytes 135176 | tf_op jit(solution)/shard_map/ppermute | solution.py:244
  453.2 69.4 %collective-permute-start.42 = (f32[88,128]{1,0:T(8,128)S(1)}, f32[88,128]{1,0:T(8,128)S(1)}, u32[]{:S(2)}, u32[]{:S(2)}) collective-permute-start(f32[88,128]{1,0:T(8,128)S(1)} %fusion.117), channel_id=1, source_target_pairs={{0,8},{8,0},{16,24},{24,16},{1,9},{9,1},{17,25},{25,17},{2,10},{10... | collective-permute-start | bytes 135176 | tf_op jit(solution)/shard_map/ppermute | solution.py:252
  453.6 14.1 %collective-permute-start.45 = (f32[256,384]{0,1:T(8,128)S(1)}, f32[256,384]{0,1:T(8,128)S(1)}, u32[]{:S(2)}, u32[]{:S(2)}) collective-permute-start(f32[256,384]{0,1:T(8,128)S(1)} %get-tuple-element.104), channel_id=1, source_target_pairs={{6,0},{0,2},{2,4},{4,6},{7,1},{1,3},{3,5},{5,7},{14,8},{8,10},{10,... | collective-permute-start | bytes 1179656 | tf_op jit(solution)/shard_map/ppermute | solution.py:238
  455.5 27.3 %collective-permute-start.47 = (f32[256,384]{0,1:T(8,128)S(1)}, f32[256,384]{0,1:T(8,128)S(1)}, u32[]{:S(2)}, u32[]{:S(2)}) collective-permute-start(f32[256,384]{0,1:T(8,128)S(1)} %get-tuple-element.105), channel_id=1, source_target_pairs={{2,0},{4,2},{6,4},{0,6},{3,1},{5,3},{7,5},{1,7},{10,8},{12,10},{14... | collective-permute-start | bytes 1179656 | tf_op jit(solution)/shard_map/ppermute | solution.py:238
  457.8 40.7 %collective-permute-start.46 = (f32[256,384]{0,1:T(8,128)S(1)}, f32[256,384]{0,1:T(8,128)S(1)}, u32[]{:S(2)}, u32[]{:S(2)}) collective-permute-start(f32[256,384]{0,1:T(8,128)S(1)} %get-tuple-element.106), channel_id=1, source_target_pairs={{4,0},{6,2},{0,4},{2,6},{5,1},{7,3},{1,5},{3,7},{12,8},{14,10},{8,... | collective-permute-start | bytes 1179656 | tf_op jit(solution)/shard_map/ppermute | solution.py:238
  467.7 33.9 %collective-permute-start.69 = (bf16[512,256]{1,0:T(8,128)(2,1)S(1)}, bf16[512,256]{1,0:T(8,128)(2,1)S(1)}, u32[]{:S(2)}, u32[]{:S(2)}) collective-permute-start(bf16[512,256]{1,0:T(8,128)(2,1)S(1)} %get-tuple-element.114), channel_id=1, source_target_pairs={{6,0},{0,2},{2,4},{4,6},{7,1},{1,3},{3,5},{5,7},{14,8},{8,10},{10,... | collective-permute-start | bytes 786440 | tf_op jit(solution)/shard_map/ppermute | solution.py:238
  482.7 25.9 %collective-permute-start.71 = (bf16[512,256]{1,0:T(8,128)(2,1)S(1)}, bf16[512,256]{1,0:T(8,128)(2,1)S(1)}, u32[]{:S(2)}, u32[]{:S(2)}) collective-permute-start(bf16[512,256]{1,0:T(8,128)(2,1)S(1)} %get-tuple-element.115), channel_id=1, source_target_pairs={{2,0},{4,2},{6,4},{0,6},{3,1},{5,3},{7,5},{1,7},{10,8},{12,10},{14... | collective-permute-start | bytes 786440 | tf_op jit(solution)/shard_map/ppermute | solution.py:238
  498.5 22.4 %collective-permute-start.70 = (bf16[512,256]{1,0:T(8,128)(2,1)S(1)}, bf16[512,256]{1,0:T(8,128)(2,1)S(1)}, u32[]{:S(2)}, u32[]{:S(2)}) collective-permute-start(bf16[512,256]{1,0:T(8,128)(2,1)S(1)} %get-tuple-element.116), channel_id=1, source_target_pairs={{4,0},{6,2},{0,4},{2,6},{5,1},{7,3},{1,5},{3,7},{12,8},{14,10},{8,... | collective-permute-start | bytes 786440 | tf_op jit(solution)/shard_map/ppermute | solution.py:238
  498.6 28.2 %collective-permute-start.48 = (f32[256,384]{0,1:T(8,128)S(1)}, f32[256,384]{0,1:T(8,128)}, u32[]{:S(2)}, u32[]{:S(2)}) collective-permute-start(f32[256,384]{0,1:T(8,128)S(1)} %fusion.98), channel_id=1, source_target_pairs={{16,0},{24,8},{0,16},{8,24},{17,1},{25,9},{1,17},{9,25},{18,2},{26... | collective-permute-start | bytes 1179656 | tf_op jit(solution)/shard_map/ppermute | solution.py:244
  501.6 25.2 %collective-permute-start.61 = (bf16[256,512]{0,1:T(8,128)(2,1)}, bf16[256,512]{0,1:T(8,128)(2,1)S(1)}, u32[]{:S(2)}, u32[]{:S(2)}) collective-permute-start(bf16[256,512]{0,1:T(8,128)(2,1)} %get-tuple-element.117), channel_id=1, source_target_pairs={{6,0},{0,2},{2,4},{4,6},{7,1},{1,3},{3,5},{5,7},{14,8},{8,10},{10,... | collective-permute-start | bytes 786440 | tf_op jit(solution)/shard_map/ppermute | solution.py:238
  521.0 20.7 %collective-permute-start.72 = (f32[512,256]{1,0:T(8,128)S(1)}, f32[512,256]{1,0:T(8,128)}, u32[]{:S(2)}, u32[]{:S(2)}) collective-permute-start(f32[512,256]{1,0:T(8,128)S(1)} %fusion.94), channel_id=1, source_target_pairs={{16,0},{24,8},{0,16},{8,24},{17,1},{25,9},{1,17},{9,25},{18,2},{26... | collective-permute-start | bytes 1572872 | tf_op jit(solution)/shard_map/ppermute | solution.py:244
  522.6 17.3 %collective-permute-start.62 = (bf16[256,512]{0,1:T(8,128)(2,1)}, bf16[256,512]{0,1:T(8,128)(2,1)}, u32[]{:S(2)}, u32[]{:S(2)}) collective-permute-start(bf16[256,512]{0,1:T(8,128)(2,1)} %get-tuple-element.119), channel_id=1, source_target_pairs={{4,0},{6,2},{0,4},{2,6},{5,1},{7,3},{1,5},{3,7},{12,8},{14,10},{8,... | collective-permute-start | bytes 786440 | tf_op jit(solution)/shard_map/ppermute | solution.py:238
  526.8 16.3 %collective-permute-start.49 = (f32[256,384]{0,1:T(8,128)S(1)}, f32[256,384]{0,1:T(8,128)}, u32[]{:S(2)}, u32[]{:S(2)}) collective-permute-start(f32[256,384]{0,1:T(8,128)S(1)} %fusion.98), channel_id=1, source_target_pairs={{0,8},{8,0},{16,24},{24,16},{1,9},{9,1},{17,25},{25,17},{2,10},{10... | collective-permute-start | bytes 1179656 | tf_op jit(solution)/shard_map/ppermute | solution.py:252
  526.8 16.8 %collective-permute-start.50 = (f32[256,384]{0,1:T(8,128)}, f32[256,384]{0,1:T(8,128)}, u32[]{:S(2)}, u32[]{:S(2)}) collective-permute-start(f32[256,384]{0,1:T(8,128)} %collective-permute-done.48), channel_id=1, source_target_pairs={{0,8},{8,0},{16,24},{24,16},{1,9},{9,1},{17,25},{25,17},{2,10},{10... | collective-permute-start | bytes 1179656 | tf_op jit(solution)/shard_map/ppermute | solution.py:252
  532.1 22.3 %collective-permute-start.73 = (f32[512,256]{1,0:T(8,128)S(1)}, f32[512,256]{1,0:T(8,128)}, u32[]{:S(2)}, u32[]{:S(2)}) collective-permute-start(f32[512,256]{1,0:T(8,128)S(1)} %fusion.94), channel_id=1, source_target_pairs={{0,8},{8,0},{16,24},{24,16},{1,9},{9,1},{17,25},{25,17},{2,10},{10... | collective-permute-start | bytes 1572872 | tf_op jit(solution)/shard_map/ppermute | solution.py:252
  541.2 13.2 %collective-permute-start.64 = (f32[256,512]{0,1:T(8,128)S(1)}, f32[256,512]{0,1:T(8,128)}, u32[]{:S(2)}, u32[]{:S(2)}) collective-permute-start(f32[256,512]{0,1:T(8,128)S(1)} %fusion.96), channel_id=1, source_target_pairs={{16,0},{24,8},{0,16},{8,24},{17,1},{25,9},{1,17},{9,25},{18,2},{26... | collective-permute-start | bytes 1572872 | tf_op jit(solution)/shard_map/ppermute | solution.py:244
  541.8 12.6 %collective-permute-start.74 = (f32[512,256]{1,0:T(8,128)}, f32[512,256]{1,0:T(8,128)}, u32[]{:S(2)}, u32[]{:S(2)}) collective-permute-start(f32[512,256]{1,0:T(8,128)} %collective-permute-done.72), channel_id=1, source_target_pairs={{0,8},{8,0},{16,24},{24,16},{1,9},{9,1},{17,25},{25,17},{2,10},{10... | collective-permute-start | bytes 1572872 | tf_op jit(solution)/shard_map/ppermute | solution.py:252
  543.0 14.4 %collective-permute-start.65 = (f32[256,512]{0,1:T(8,128)S(1)}, f32[256,512]{0,1:T(8,128)}, u32[]{:S(2)}, u32[]{:S(2)}) collective-permute-start(f32[256,512]{0,1:T(8,128)S(1)} %fusion.96), channel_id=1, source_target_pairs={{0,8},{8,0},{16,24},{24,16},{1,9},{9,1},{17,25},{25,17},{2,10},{10... | collective-permute-start | bytes 1572872 | tf_op jit(solution)/shard_map/ppermute | solution.py:252
  (71 other events, 716.9 us)
